TPU v7x, 128 devices: a whole 4x4x4 slice. The times are simulated.
128 devices in a mesh: wide: 16 (over y, z), narrow: 8 (over x, core).
Axes of the slice: x: 4, y: 4, z: 4, core: 2. Of those that a mesh axis runs over, the one named last changes fastest.
Arguments:
- hidden_in: bfloat16 [1024, 7168], P(None, ('wide', 'narrow'))
- attn_gain: bfloat16 [7168], P(('wide', 'narrow')), may hold values from 0.099609375 to 1.8984375
- w_qkv: bfloat16 [7168, 8, 1152], P('wide', 'narrow'), may hold values from -0.0625 to 0.0625
- cache_kv: bfloat16 [2, 4096, 8, 2, 128], P(None, 'wide', 'narrow'), as said below
- lengths: int32 [2], replicated, may hold values from 1 to 4096, as said below
- offsets: int32 [2], replicated, may hold values from 0 to 4095
- w_out: bfloat16 [7168, 7168], P('narrow', 'wide'), may hold values from -0.0625 to 0.0625
- mlp_gain: bfloat16 [7168], P(('wide', 'narrow')), may hold values from 0.099609375 to 1.8984375
- w_gate_up: bfloat16 [7168, 2, 20480], P('wide', None, 'narrow'), may hold values from -0.0625 to 0.0625
- w_down: bfloat16 [20480, 7168], P('narrow', 'wide'), may hold values from -0.0390625 to 0.0390625
Outputs:
- hidden_out: bfloat16 [1024, 7168], P(None, ('wide', 'narrow'))
- softmax_sums: float32 [1024, 56], P('wide', 'narrow')
- new_cache: bfloat16 [1024, 8, 2, 128], P('wide', 'narrow')
Inputs may be any that keep to these rules, and one draw needn't show every extreme that they name: `lengths`: at least one request has all 4096 cached positions in use. `cache_kv`: positions at or beyond a request's length are never read.
All inputs are finite; a program needn't handle non-finite values.
Results may differ from a plain program's by a relative error of at most 0.01.
Values may be sent and summed in bfloat16 or wider, within the bound.
A program may use at most 192 MiB of HBM per device.

v0:
```python
import jax
import jax.numpy as jnp
from jax import lax
from jax.sharding import PartitionSpec as P

D = 7168
HDIM = 128
R = 2
GROUP = 7


epsilon = 1e-05
rope_base = 5000000.0
floor_score = -1e30


def norm_block(values, gain_vec):
    gathered, gain_row = (
        lax.all_gather(values, "narrow", axis=1, tiled=True),
        lax.all_gather(gain_vec.reshape(1, -1), "narrow", axis=1, tiled=True),
    )
    widened = gathered.astype(jnp.float32)
    squares = lax.psum(jnp.sum(widened * widened, axis=1), "wide")
    inv_scale = lax.rsqrt(squares / D + epsilon)
    return (widened * inv_scale[:, None] * gain_row.astype(jnp.float32)).astype(jnp.bfloat16)


def narrow_sums(partial_value):
    return lax.psum_scatter(partial_value, "narrow", scatter_dimension=1, tiled=True)


def token_angles(lengths, offsets, first_token, row_count, dim_size):
    token_ids = first_token + jnp.arange(row_count, dtype=jnp.int32)
    request_ids = token_ids % R
    start_pos = offsets + lengths
    matches = request_ids[:, None] == jnp.arange(start_pos.shape[0], dtype=jnp.int32)[None, :]
    chosen = jnp.sum(jnp.where(matches, start_pos[None, :], 0), axis=1)
    position = (chosen + token_ids // R).astype(jnp.float32)
    inverse = rope_base ** (-(jnp.arange(dim_size // 2, dtype=jnp.float32) * 2.0) / dim_size)
    return position[:, None] * inverse[None, :]


def rotate(values, angles):
    half_dim = values.shape[-1] // 2
    first_half = values[..., :half_dim]
    second_half = values[..., half_dim:]
    cosine = jnp.cos(angles)[:, None, :]
    sine_part = jnp.sin(angles)[:, None, :]
    return jnp.concatenate(
        [
            first_half * cosine - second_half * sine_part,
            second_half * cosine + first_half * sine_part,
        ],
        axis=-1,
    )


def absorb(running, scores, allowed, value_block, einsum_form):
    peak, weight_sum, accumulated = running
    scores = jnp.where(allowed, scores, floor_score)
    reduce_axes = tuple(range(3, scores.ndim))
    new_peak = jnp.maximum(peak, jnp.max(scores, axis=reduce_axes))
    expanded = new_peak.reshape(new_peak.shape + (1,) * len(reduce_axes))
    weights = jnp.where(allowed, jnp.exp(scores - expanded), 0.0)
    factor = jnp.exp(peak - new_peak)
    weight_sum = weight_sum * factor + jnp.sum(weights, axis=reduce_axes)
    accumulated = accumulated * factor[..., None] + jnp.einsum(
        einsum_form, weights.astype(jnp.bfloat16), value_block, preferred_element_type=jnp.float32
    )
    return (new_peak, weight_sum, accumulated)


def cache_step(running, remote, queries, request_ids, lengths):
    score_scale = HDIM ** (-0.5)
    scores = (
        jnp.einsum(
            "thgd,rphd->thgrp", queries, remote[:, :, :, 0], preferred_element_type=jnp.float32
        )
        * score_scale
    )
    position = jnp.arange(remote.shape[1], dtype=jnp.int32)
    usable = position[None, :] < lengths[:, None]
    owned = request_ids[:, None] == jnp.arange(lengths.shape[0], dtype=jnp.int32)[None, :]
    allowed = owned[:, None, None, :, None] & usable[None, None, None, :, :]
    return absorb(running, scores, allowed, remote[:, :, :, 1], "thgrp,rphd->thgd")


def start_state(row_count, heads_here):
    peak = jnp.full((row_count, heads_here, GROUP), floor_score, jnp.float32)
    weight_sum = jnp.zeros((row_count, heads_here, GROUP), jnp.float32)
    accumulated = jnp.zeros((row_count, heads_here, GROUP, HDIM), jnp.float32)
    return (peak, weight_sum, accumulated)


def local(
    hidden_in, attn_gain, w_qkv, cache_kv, lengths, offsets, w_out, mlp_gain, w_gate_up, w_down
):
    all_tokens = hidden_in.shape[0]
    per_device = all_tokens // lax.axis_size("wide")
    first_token = lax.axis_index("wide") * per_device
    heads_here = w_qkv.shape[1]
    score_scale = HDIM ** (-0.5)
    normed = norm_block(hidden_in, attn_gain)
    flat_qkv = w_qkv.reshape(w_qkv.shape[0], -1)
    row_block = normed
    projected = lax.psum_scatter(
        jnp.dot(row_block, flat_qkv, preferred_element_type=jnp.float32),
        "wide",
        scatter_dimension=0,
        tiled=True,
    )
    projected = projected.reshape(per_device, heads_here, GROUP + 2, HDIM)
    angles = token_angles(lengths, offsets, first_token, per_device, HDIM)
    queries = rotate(projected[:, :, :GROUP].reshape(per_device, heads_here * GROUP, HDIM), angles)
    queries = queries.astype(jnp.bfloat16).reshape(per_device, heads_here, GROUP, HDIM)
    new_keys = rotate(projected[:, :, GROUP], angles).astype(jnp.bfloat16)
    new_values = projected[:, :, GROUP + 1].astype(jnp.bfloat16)
    new_cache = jnp.stack([new_keys, new_values], axis=2)
    span_all = lax.all_gather(new_cache, "wide", axis=0, tiled=True)
    my_tokens = first_token + jnp.arange(per_device, dtype=jnp.int32)
    my_requests = my_tokens % R
    owned_any = jnp.any(
        my_requests[:, None] == jnp.arange(lengths.shape[0], dtype=jnp.int32)[None, :], axis=0
    )
    furthest = jnp.max(jnp.where(owned_any, lengths, 0))
    remote = lax.all_gather(cache_kv, "wide", axis=1, tiled=True)
    running = lax.cond(
        jnp.int32(0) < furthest,
        lambda state: cache_step(state, remote, queries, my_requests, lengths),
        lambda state: state,
        start_state(per_device, heads_here),
    )
    token_all = jnp.arange(all_tokens, dtype=jnp.int32)
    span_allowed = ((token_all % R)[None, :] == my_requests[:, None]) & (
        token_all[None, :] <= my_tokens[:, None]
    )
    span_scores = (
        jnp.einsum("thgd,shd->thgs", queries, span_all[:, :, 0], preferred_element_type=jnp.float32)
        * score_scale
    )
    peak, weight_sum, accumulated = absorb(
        running, span_scores, span_allowed[:, None, None, :], span_all[:, :, 1], "thgs,shd->thgd"
    )
    attended = (accumulated / weight_sum[..., None]).astype(jnp.bfloat16).reshape(per_device, -1)
    softmax_sums = (peak + jnp.log(weight_sum)).reshape(per_device, -1)
    attn_partial = jnp.dot(
        lax.all_gather(attended, "wide", axis=0, tiled=True),
        w_out,
        preferred_element_type=jnp.float32,
    )
    residual = (hidden_in.astype(jnp.float32) + narrow_sums(attn_partial)).astype(jnp.bfloat16)
    normed_mlp = norm_block(residual, mlp_gain)
    flat_gate_up = w_gate_up.reshape(w_gate_up.shape[0], -1)
    unit_count = w_gate_up.shape[2]
    row_block = normed_mlp
    summed = lax.psum_scatter(
        jnp.dot(row_block, flat_gate_up, preferred_element_type=jnp.float32),
        "wide",
        scatter_dimension=0,
        tiled=True,
    ).reshape(per_device, 2, unit_count)
    hidden = (jax.nn.silu(summed[:, 0]) * summed[:, 1]).astype(jnp.bfloat16)
    mlp_partial = jnp.dot(
        lax.all_gather(hidden, "wide", axis=0, tiled=True),
        w_down,
        preferred_element_type=jnp.float32,
    )
    hidden_out = (residual.astype(jnp.float32) + narrow_sums(mlp_partial)).astype(jnp.bfloat16)
    return (hidden_out, softmax_sums, new_cache)


def solution(mesh):
    return jax.shard_map(
        local,
        mesh=mesh,
        in_specs=(
            P(None, ("wide", "narrow")),
            P(("wide", "narrow")),
            P("wide", "narrow", None),
            P(None, "wide", "narrow", None, None),
            P(),
            P(),
            P("narrow", "wide"),
            P(("wide", "narrow")),
            P("wide", None, "narrow"),
            P("narrow", "wide"),
        ),
        out_specs=(
            P(None, ("wide", "narrow")),
            P("wide", "narrow"),
            P("wide", "narrow", None, None),
        ),
        check_vma=False,
    )
```

profile of v0, /device:TPU:1, one launch (start us, length us, event | category | flops | bytes accessed | tf_op | source)
XLA Modules:
  0.0 627.5 jit_solution(1078234093537580694)
XLA Ops:
  7.2 0.0 reduce-scatter.5.cloned.1.call-start
  7.2 1.4 dynamic-slice
  9.3 0.9 dynamic-update-slice
  10.2 0.8 dynamic-update-slice.1
  11.0 13.2 %all-reduce.2 = (bf16[448]{0:T(512)(128)(2,1)S(1)}, bf16[448]{0:T(512)(128)(2,1)S(1)}) all-reduce(bf16[448]{0:T(512)(128)(2,1)S(1)} %dynamic-update-slice, bf16[448]{0:T(512)(128)(2,1)S(1)} %dynamic-update-slice.1), channel_id=2, replica_groups=mesh['wide'=16,'narrow'=8] {'narrow'}, use_global_device_ids=true, to_apply=%add | all-reduce | flops 896 | bytes 3584
  24.2 16.6 %all_gather.25 = bf16[1024,448]{0,1:T(8,128)(2,1)S(1)} all-gather(bf16[1024,56]{0,1:T(8,128)(2,1)} %param.12), channel_id=1, replica_groups=mesh['wide'=16,'narrow'=8] {'narrow'}, dimensions={1}, use_global_device_ids=true | all-gather | bytes 1032192 | tf_op jit(solution)/shard_map/all_gather | solution.py:19
  40.8 0.2 fusion.32
  41.0 34.7 %psum.14 = f32[1024]{0:T(1024)S(1)} all-reduce(f32[1024]{0:T(1024)S(1)} %fusion.32), channel_id=1, replica_groups=mesh['wide'=16,'narrow'=8] {'wide'}, use_global_device_ids=true, to_apply=%region_3.4 | all-reduce | flops 1024 | bytes 8192 | tf_op jit(solution)/shard_map/psum | solution.py:23
  75.7 5.0 fusion.44
  80.7 0.0 reduce-scatter.5.cloned.1.call-update
  80.7 0.0 all-gather.6.cloned.1.call-start
  80.8 0.9 copy-done.3
  81.7 0.7 copy.28
  82.4 0.0 all-gather.6.cloned.1.call-update
  82.4 0.0 all-gather.8.cloned.1.call-start
  82.5 0.1 fusion.81
  82.6 0.6 select_reduce_fusion.1
  84.0 0.1 select_reduce_fusion
  84.1 0.2 multiply_cosine_fusion.1
  84.3 0.1 fusion.62
  84.4 74.8 %reduce-scatter.5.cloned.1.call-done = f32[64,1152]{1,0:T(8,128)} async-done(((f32[1024,1152]{1,0:T(8,128)}), f32[64,1152]{1,0:T(8,128)}) %reduce-scatter.5.cloned.1.call-update) | async-done | bytes 294928 | tf_op jit(solution)/shard_map/reduce_scatter | solution.py:106
  159.2 1.0 reshape.470
  160.4 0.2 fusion.75
  160.6 0.1 pad_maximum_fusion.1
  160.7 0.1 subtract_convert_fusion
  160.8 0.1 pad_maximum_fusion
  160.9 19.0 %all_gather.27 = bf16[1024,1,2,128]{3,0,2,1:T(8,128)(2,1)S(1)} all-gather(bf16[64,1,2,128]{3,0,2,1:T(8,128)(2,1)S(1)} %pad_maximum_fusion.1), channel_id=1, replica_groups=mesh['wide'=16,'narrow'=8] {'wide'}, dimensions={0}, use_global_device_ids=true | all-gather | bytes 557056 | tf_op jit(solution)/shard_map/all_gather | solution.py:119
  179.9 1.7 fusion.38
  181.6 33.1 %all-gather.6.cloned.1.call-done = bf16[2,4096,1,2,128]{4,1,0,3,2:T(8,128)(2,1)} async-done(((bf16[2,256,1,2,128]{4,1,0,3,2:T(8,128)(2,1)}), bf16[2,4096,1,2,128]{4,1,0,3,2:T(8,128)(2,1)}) %all-gather.6.cloned.1.call-update) | async-done | bytes 4194320 | tf_op jit(solution)/shard_map/all_gather | solution.py:126
  214.8 23.4 %conditional.1 = (f32[64,1,7]{0,2,1:T(8,128)S(1)}, f32[64,1,7]{0,2,1:T(8,128)S(1)}, f32[64,1,7,128]{3,0,2,1:T(8,128)S(1)}) conditional(s32[]{:T(128)} %convert_element_type.73, () %tuple.19, (s32[64]{0:T(128)S(1)}, s32[64]{0:T(128)S(1)}, s32[2]{0:T(128)S(1)}, bf16[2,4096,1,2,128]{4,1,0,3,2:T(8,128)(2,1)}, bf16[64,1,7,128]{3,0,2,1:T(8,128)(2,1)S(1)}) %tuple.52), branch_computations={%region_6.7_spmd, %region_7.10_spmd} | conditional | flops 1927350912 | bytes 126217040 | solution.py:127
  214.8 0.1 iota_compare_fusion
  214.9 0.3 broadcast_and_fusion
  215.2 4.3 fusion
  219.6 5.2 copy-done.1
  224.8 3.9 fusion.22
  228.6 9.5 %fusion.2 = f32[64,7]{0,1:T(8,128)S(1)} fusion(f32[2,4096,64,7]{1,2,3,0:T(8,128)} %copy-done.1, f32[64,7]{0,1:T(8,128)S(1)} %get-tuple-element.67, pred[64,2,4096]{2,0,1:T(8,128)(4,1)S(1)} %broadcast_and_fusion), kind=kLoop, calls=%fused_computation.4 | loop fusion | flops 18349632 | bytes 15207936 | tf_op jit(solution)/shard_map/cond/branch_1_fun/reduce_sum | solution.py:66
  238.1 2.1 fusion.39
  240.2 0.6 add_bitcast_fusion
  240.9 2.1 fusion.43
  243.0 0.1 copy.32
  243.1 0.7 copy.54
  243.7 0.0 all-gather.8.cloned.1.call-update
  243.8 0.3 reduce-scatter.7.cloned.1.call-start
  244.0 42.8 %all-gather.8.cloned.1.call-done = bf16[1024,896]{1,0:T(8,128)(2,1)} async-done(((bf16[64,896]{1,0:T(8,128)(2,1)}), bf16[1024,896]{1,0:T(8,128)(2,1)}) %all-gather.8.cloned.1.call-update) | async-done | bytes 1835024 | tf_op jit(solution)/shard_map/all_gather | solution.py:147
  286.9 4.1 fusion.89
  291.0 0.0 reduce-scatter.9.cloned.1.call-start
  291.0 5.5 copy.43
  296.5 25.5 %reduce-scatter.7.cloned.1.call-done = f32[1024,56]{0,1:T(8,128)} async-done(((f32[1024,448]{0,1:T(8,128)}), f32[1024,56]{0,1:T(8,128)}) %reduce-scatter.7.cloned.1.call-update) | async-done | bytes 229392 | tf_op jit(solution)/shard_map/reduce_scatter | solution.py:29
  322.0 1.0 add_convert_fusion.1
  323.0 17.0 %all_gather.29 = bf16[1024,448]{0,1:T(8,128)(2,1)S(1)} all-gather(bf16[1024,56]{0,1:T(8,128)(2,1)S(1)} %add_convert_fusion.1), channel_id=1, replica_groups=mesh['wide'=16,'narrow'=8] {'narrow'}, dimensions={1}, use_global_device_ids=true | all-gather | bytes 1032192 | tf_op jit(solution)/shard_map/all_gather | solution.py:19
  340.0 0.2 fusion.35
  340.2 33.3 %psum.15 = f32[1024]{0:T(1024)S(1)} all-reduce(f32[1024]{0:T(1024)S(1)} %fusion.35), channel_id=1, replica_groups=mesh['wide'=16,'narrow'=8] {'wide'}, use_global_device_ids=true, to_apply=%region_14.15 | all-reduce | flops 1024 | bytes 8192 | tf_op jit(solution)/shard_map/psum | solution.py:23
  373.5 12.3 %fusion.48 = f32[1024,5120]{1,0:T(8,128)} fusion(bf16[448,5120]{1,0:T(8,128)(2,1)} %bitcast.180, bf16[1024,448]{0,1:T(8,128)(2,1)S(1)} %all_gather.29, f32[448]{0:T(512)S(1)} %mul.228, f32[1024]{0:T(1024)S(1)} %add_rsqrt_fusion), kind=kOutput, calls=%fused_computation.50 | convolution fusion | flops 4699455488 | bytes 26482432 | tf_op jit(solution)/shard_map/dot_general | solution.py:157
  385.8 0.0 all-gather.10.cloned.1.call-start
  385.9 133.5 %reduce-scatter.9.cloned.1.call-done = f32[64,5120]{1,0:T(8,128)} async-done(((f32[1024,5120]{1,0:T(8,128)}), f32[64,5120]{1,0:T(8,128)}) %reduce-scatter.9.cloned.1.call-update) | async-done | bytes 1310736 | tf_op jit(solution)/shard_map/reduce_scatter | solution.py:156
  519.4 3.3 reshape.478
  522.7 2.9 fusion.88
  525.6 0.9 fusion.60
  526.5 0.0 reduce-scatter.11.cloned.1.call-start
  526.6 56.2 %all-gather.10.cloned.1.call-done = bf16[1024,2560]{1,0:T(8,128)(2,1)} async-done(((bf16[64,2560]{1,0:T(8,128)(2,1)}), bf16[1024,2560]{1,0:T(8,128)(2,1)}) %all-gather.10.cloned.1.call-update) | async-done | bytes 5242896 | tf_op jit(solution)/shard_map/all_gather | solution.py:164
  582.8 6.3 %fusion.90 = f32[1024,448]{0,1:T(8,128)} fusion(bf16[1024,2560]{1,0:T(8,128)(2,1)} %all-gather.10.cloned.1.call-done, bf16[2560,448]{0,1:T(8,128)(2,1)S(1)} %copy-done), kind=kOutput, calls=%fused_computation.127 | convolution fusion | flops 2348810240 | bytes 9371648 | tf_op jit(solution)/shard_map/dot_general | solution.py:163
  589.1 0.6 copy.34
  589.8 29.3 %reduce-scatter.11.cloned.1.call-done = f32[1024,56]{0,1:T(8,128)} async-done(((f32[1024,448]{0,1:T(8,128)}), f32[1024,56]{0,1:T(8,128)}) %reduce-scatter.11.cloned.1.call-update) | async-done | bytes 229392 | tf_op jit(solution)/shard_map/reduce_scatter | solution.py:29
  619.1 1.6 add_convert_fusion
  (40 shorter events, 0.3 us)
Async XLA Ops:
  7.2 575.6 %copy-start = (bf16[2560,448]{0,1:T(8,128)(2,1)S(1)}, bf16[2560,448]{0,1:T(8,128)(2,1)}, u32[]{:S(2)}) copy-start(bf16[2560,448]{0,1:T(8,128)(2,1)} %param.21) | copy-start | bytes 6881284
  7.2 152.0 %reduce-scatter.5.cloned.1.call-start = ((), (), s32[]{:S(2)}) async-start(), calls=%async_computation.5 | async-start | bytes 5013504 | tf_op jit(solution)/shard_map/reduce_scatter | solution.py:106
  80.7 0.9 copy-start.3
  80.7 1.9 copy-start.4
  80.7 1.9 copy-start.5
  80.7 134.0 %all-gather.6.cloned.1.call-start = ((), (), s32[]{:S(2)}) async-start(), calls=%async_computation.4 | async-start | bytes 4456448 | tf_op jit(solution)/shard_map/all_gather | solution.py:126
  82.4 204.4 %all-gather.8.cloned.1.call-start = ((), (), s32[]{:S(2)}) async-start(), calls=%async_computation.6 | async-start | bytes 1949696 | tf_op jit(solution)/shard_map/all_gather | solution.py:147
  215.2 9.5 %copy-start.6 = (bf16[2,4096,1,2,128]{4,1,0,3,2:T(8,128)(2,1)S(1)}, bf16[2,4096,1,2,128]{4,1,0,3,2:T(8,128)(2,1)}, u32[]{:S(2)}) copy-start(bf16[2,4096,1,2,128]{4,1,0,3,2:T(8,128)(2,1)} %get-tuple-element.42) | copy-start | bytes 12582916 | tf_op jit(solution)/shard_map/cond
  219.5 5.2 copy-start.1
  243.8 78.2 %reduce-scatter.7.cloned.1.call-start = ((), (), s32[]{:S(2)}) async-start(), calls=%async_computation.7 | async-start | bytes 2064384 | tf_op jit(solution)/shard_map/reduce_scatter | solution.py:29
  291.0 228.5 %reduce-scatter.9.cloned.1.call-start = ((), (), s32[]{:S(2)}) async-start(), calls=%async_computation.8 | async-start | bytes 22282240 | tf_op jit(solution)/shard_map/reduce_scatter | solution.py:156
  291.0 31.0 %copy-start.2 = (bf16[1024,56]{0,1:T(8,128)(2,1)S(1)}, bf16[1024,56]{0,1:T(8,128)(2,1)}, u32[]{:S(2)}) copy-start(bf16[1024,56]{0,1:T(8,128)(2,1)} %param.12) | copy-start | bytes 344068
  385.8 196.9 %all-gather.10.cloned.1.call-start = ((), (), s32[]{:S(2)}) async-start(), calls=%async_computation.9 | async-start | bytes 5570560 | tf_op jit(solution)/shard_map/all_gather | solution.py:164
  526.5 92.5 %reduce-scatter.11.cloned.1.call-start = ((), (), s32[]{:S(2)}) async-start(), calls=%async_computation.10 | async-start | bytes 2064384 | tf_op jit(solution)/shard_map/reduce_scatter | solution.py:29
Sparse Core Ops, SparseCore 0:
  80.9 78.2 reduce-scatter.4
  161.4 53.3 all-gather.5
  243.9 42.9 all-gather.7
  291.1 30.8 reduce-scatter.6
  386.0 133.4 reduce-scatter.8
  526.7 56.0 all-gather.9
  589.3 29.7 reduce-scatter.10
where the time goes:
time: 630 us; the launch traced here: 628 us
  waiting for transfers between devices  395 us (63%)
  blocking collectives  134 us (21%)
  matrix products  39.8 us (6%)
  local copies, waits for them, and re-layouts  24.1 us (4%)
  other arithmetic  18.3 us (3%)
  between operations  15.6 us (2%)
    reduce_scatter x1, waiting for transfers between devices, local(): lax.psum_scatter(jnp.dot(row_block, flat_gate_up, preferred_element_type=...  134 us
    reduce_scatter x1, waiting for transfers between devices, local(): lax.psum_scatter(jnp.dot(row_block, flat_qkv, preferred_element_type=jnp....  74.8 us
    psum x2, blocking collectives, norm_block(): squares = lax.psum(jnp.sum(widened * widened, axis=1), 'wide')  68 us
    all_gather x1, waiting for transfers between devices, local(): lax.all_gather(hidden, 'wide', axis=0, tiled=True)  56.2 us
    reduce_scatter x2, waiting for transfers between devices, narrow_sums(): lax.psum_scatter(partial_value, 'narrow', scatter_dimension=1, tiled=True)  54.8 us
    all_gather x1, waiting for transfers between devices, local(): lax.all_gather(attended, 'wide', axis=0, tiled=True)  42.8 us
    all_gather x2, blocking collectives, norm_block(): lax.all_gather(values, 'narrow', axis=1, tiled=True)  33.6 us
    all_gather x1, waiting for transfers between devices, local(): remote = lax.all_gather(cache_kv, 'wide', axis=1, tiled=True)  33.1 us
  transfers between devices with their start and end apart: 7, of which 7 were waited for; matrix products, arithmetic and copies ran while one was open for 2% of the time, Pallas kernels for 0%

commit v1 on v0

v1 whole, which is shorter than its diff:
```python
import functools

import jax
import jax.numpy as jnp
from jax import lax
from jax.experimental import pallas as pl
from jax.experimental.pallas import tpu as pltpu
from jax.sharding import PartitionSpec as P

D = 7168
HDIM = 128
R = 2
GROUP = 7
SIDE = 4

epsilon = 1e-05
rope_base = 5000000.0
floor_score = -1e30

MESH = pl.DeviceIdType.MESH
BF = jnp.bfloat16
F32 = jnp.float32
ANY = pl.BlockSpec(memory_space=pl.ANY)
VM = pl.BlockSpec(memory_space=pltpu.VMEM)
SM = pl.BlockSpec(memory_space=pltpu.SMEM)
VMEM_LIMIT = 60 * 1024 * 1024


def wide_place():
    w = lax.axis_index("wide")
    return lax.div(w, SIDE), lax.rem(w, SIDE)


def turn(pos, by):
    return lax.rem(pos + by, SIDE)


def ring_devices(axis, by):
    if axis == "x":
        n = lax.axis_index("narrow")
        return {"narrow": turn(lax.div(n, 2), by) * 2 + lax.rem(n, 2)}
    y, z = wide_place()
    if axis == "y":
        return {"wide": turn(y, by) * SIDE + z}
    return {"wide": y * SIDE + turn(z, by)}


def partner_device():
    n = lax.axis_index("narrow")
    return {"narrow": lax.div(n, 2) * 2 + 1 - lax.rem(n, 2)}


def greet(devices):
    barrier = pltpu.get_barrier_semaphore()
    for device in devices:
        pl.semaphore_signal(barrier, inc=1, device_id=device, device_id_type=MESH)
    pl.semaphore_wait(barrier, len(devices))


class Copies:
    def __init__(self, send_sem, recv_sem):
        self.send_sem, self.recv_sem, self.used, self.made = send_sem, recv_sem, 0, []

    def slot(self):
        self.used += 1
        return self.used - 1

    def start(self, slot, src, dst, device):
        copy = pltpu.make_async_remote_copy(
            src_ref=src,
            dst_ref=dst,
            send_sem=self.send_sem.at[slot],
            recv_sem=self.recv_sem.at[slot],
            device_id=device,
            device_id_type=MESH,
        )
        copy.start()
        self.made.append(copy)

    def arrived(self, slot, dst):
        pltpu.make_async_copy(dst, dst, self.recv_sem.at[slot]).wait()

    def sent(self):
        for copy in self.made:
            copy.wait_send()


def interleave(*parts):
    live = list(parts)
    while live:
        for part in list(live):
            try:
                next(part)
            except StopIteration:
                live.remove(part)


def gather_wide_steps(x_ref, out_ref, local_sem, copies):
    y, z = wide_place()
    depth = x_ref.shape[1] // 2
    lower, upper = pl.ds(0, depth), pl.ds(depth, depth)

    def place(half, first, second):
        if half == 0:
            return out_ref.at[first, second, 0]
        return out_ref.at[second, first, 1]

    names = (("y", "z"), ("z", "y"))
    spots = ((y, z), (z, y))
    own = pltpu.make_async_copy(x_ref, out_ref.at[y, z], local_sem)
    own.start()
    hop1 = [[copies.slot() for _ in range(4)] for _ in range(2)]
    hop2 = [[[copies.slot() for _ in range(4)] for _ in range(4)] for _ in range(2)]

    def send2(half, block, src):
        first = turn(spots[half][0], block)
        target = place(half, first, spots[half][1])
        for way, by in ((0, 1), (1, 3)):
            copies.start(hop2[half][block][way], src, target, ring_devices(names[half][1], by))

    def relay2(half, block):
        first = turn(spots[half][0], block)
        for way, by, part in ((0, 1, lower), (1, 3, upper)):
            came = place(half, first, turn(spots[half][1], 4 - by))
            copies.arrived(hop2[half][block][way], came)
            copies.start(
                hop2[half][block][2 + way], came.at[part], came.at[part], ring_devices(names[half][1], by)
            )

    for half in range(2):
        target = place(half, *spots[half])
        for way, by in ((0, 1), (1, 3)):
            copies.start(hop1[half][way], x_ref.at[half], target, ring_devices(names[half][0], by))
        send2(half, 0, x_ref.at[half])
    yield
    for half in range(2):
        for way, by, part in ((0, 1, lower), (1, 3, upper)):
            came = place(half, turn(spots[half][0], 4 - by), spots[half][1])
            copies.arrived(hop1[half][way], came)
            copies.start(hop1[half][2 + way], came.at[part], came.at[part], ring_devices(names[half][0], by))
            send2(half, 4 - by, came)
        yield
    for half in range(2):
        relay2(half, 0)
        yield
    for half in range(2):
        far = place(half, turn(spots[half][0], 2), spots[half][1])
        copies.arrived(hop1[half][2], far.at[lower])
        copies.arrived(hop1[half][3], far.at[upper])
        send2(half, 2, far)
        yield
    for block in (3, 1, 2):
        for half in range(2):
            relay2(half, block)
            yield
    for half in range(2):
        for block in (0, 3, 1, 2):
            far = place(half, turn(spots[half][0], block), turn(spots[half][1], 2))
            copies.arrived(hop2[half][block][2], far.at[lower])
            copies.arrived(hop2[half][block][3], far.at[upper])
    own.wait()


WIDE_COPIES = 40


def wide_neighbours():
    return [ring_devices(axis, by) for axis in ("y", "z") for by in (1, 3)]


def gather_wide_kernel(x_ref, out_ref, local_sem, send_sem, recv_sem):
    copies = Copies(send_sem, recv_sem)
    greet(wide_neighbours())
    interleave(gather_wide_steps(x_ref, out_ref, local_sem, copies))
    copies.sent()


def gather_wide(x, collective_id):
    return pl.pallas_call(
        gather_wide_kernel,
        out_shape=jax.ShapeDtypeStruct((SIDE, SIDE) + x.shape, x.dtype),
        in_specs=[VM],
        out_specs=ANY,
        scratch_shapes=[
            pltpu.SemaphoreType.DMA,
            pltpu.SemaphoreType.DMA((WIDE_COPIES,)),
            pltpu.SemaphoreType.DMA((WIDE_COPIES,)),
        ],
        compiler_params=pltpu.CompilerParams(collective_id=collective_id, has_side_effects=True),
        name=f"gather_wide_{collective_id}",
    )(x)


def gather_narrow_steps(x_ref, out_ref, local_sem, copies):
    n = lax.axis_index("narrow")
    x, core = lax.div(n, 2), lax.rem(n, 2)
    depth = x_ref.shape[0] // 2
    lower, upper = pl.ds(0, depth), pl.ds(depth, depth)
    own = pltpu.make_async_copy(x_ref, out_ref.at[n], local_sem)
    own.start()
    slots = [copies.slot() for _ in range(8)]
    for way, by in ((0, 1), (1, 3)):
        copies.start(slots[way], x_ref, out_ref.at[n], ring_devices("x", by))
    copies.start(slots[4], x_ref, out_ref.at[n], partner_device())
    yield
    for way, by, part in ((0, 1, lower), (1, 3, upper)):
        came = out_ref.at[turn(x, 4 - by) * 2 + core]
        copies.arrived(slots[way], came)
        copies.start(slots[2 + way], came.at[part], came.at[part], ring_devices("x", by))
        copies.start(slots[5 + way], came, came, partner_device())
    yield
    far = out_ref.at[turn(x, 2) * 2 + core]
    copies.arrived(slots[2], far.at[lower])
    copies.arrived(slots[3], far.at[upper])
    copies.start(slots[7], far, far, partner_device())
    yield
    for slot, by in ((4, 0), (5, 3), (6, 1), (7, 2)):
        copies.arrived(slots[slot], out_ref.at[turn(x, by) * 2 + 1 - core])
    own.wait()


NARROW_COPIES = 8


def narrow_neighbours():
    return [ring_devices("x", 1), ring_devices("x", 3), partner_device()]


def gather_narrow_kernel(x_ref, out_ref, local_sem, send_sem, recv_sem):
    copies = Copies(send_sem, recv_sem)
    greet(narrow_neighbours())
    interleave(gather_narrow_steps(x_ref, out_ref, local_sem, copies))
    copies.sent()


def gather_narrow(x, collective_id):
    return pl.pallas_call(
        gather_narrow_kernel,
        out_shape=jax.ShapeDtypeStruct((8,) + x.shape, x.dtype),
        in_specs=[VM],
        out_specs=VM,
        scratch_shapes=[
            pltpu.SemaphoreType.DMA,
            pltpu.SemaphoreType.DMA((NARROW_COPIES,)),
            pltpu.SemaphoreType.DMA((NARROW_COPIES,)),
        ],
        compiler_params=pltpu.CompilerParams(collective_id=collective_id, has_side_effects=True),
        name=f"gather_narrow_{collective_id}",
    )(x)


def gather_both_kernel(x_ref, cache_ref, xo_ref, cacheo_ref, local_sem, send_n, recv_n, send_w, recv_w):
    near, far = Copies(send_n, recv_n), Copies(send_w, recv_w)
    greet(narrow_neighbours() + wide_neighbours())
    interleave(
        gather_narrow_steps(x_ref, xo_ref, local_sem.at[0], near),
        gather_wide_steps(cache_ref, cacheo_ref, local_sem.at[1], far),
    )
    near.sent()
    far.sent()


def gather_both(x, cache, collective_id):
    return pl.pallas_call(
        gather_both_kernel,
        out_shape=(
            jax.ShapeDtypeStruct((8,) + x.shape, x.dtype),
            jax.ShapeDtypeStruct((SIDE, SIDE) + cache.shape, cache.dtype),
        ),
        in_specs=[VM, VM],
        out_specs=(VM, ANY),
        scratch_shapes=[
            pltpu.SemaphoreType.DMA((2,)),
            pltpu.SemaphoreType.DMA((NARROW_COPIES,)),
            pltpu.SemaphoreType.DMA((NARROW_COPIES,)),
            pltpu.SemaphoreType.DMA((WIDE_COPIES,)),
            pltpu.SemaphoreType.DMA((WIDE_COPIES,)),
        ],
        compiler_params=pltpu.CompilerParams(collective_id=collective_id, has_side_effects=True),
        name="gather_both",
    )(x, cache)


def sum_narrow_kernel(p_ref, out_ref, mate, total, relay, direct, joined, send_sem, recv_sem):
    copies = Copies(send_sem, recv_sem)
    n = lax.axis_index("narrow")
    x, core = lax.div(n, 2), lax.rem(n, 2)
    width = p_ref.shape[3] // 2
    lower, upper = pl.ds(0, width), pl.ds(width, width)
    right, left = ring_devices("x", 1), ring_devices("x", 3)
    greet(narrow_neighbours())
    order = (2, 1, 3, 0)
    mates = {by: copies.slot() for by in order}
    slots = [copies.slot() for _ in range(6)]
    for by in order:
        copies.start(mates[by], p_ref.at[turn(x, by), 1 - core], mate.at[by], partner_device())

    def pair(by):
        copies.arrived(mates[by], mate.at[by])
        return p_ref[turn(x, by), core].astype(F32) + mate[by].astype(F32)

    total[2] = pair(2).astype(BF)
    copies.start(slots[0], total.at[2, :, lower], relay.at[0], right)
    copies.start(slots[1], total.at[2, :, upper], relay.at[1], left)
    total[1] = pair(1).astype(BF)
    copies.start(slots[2], total.at[1, :, upper], direct.at[0], right)
    total[3] = pair(3).astype(BF)
    copies.start(slots[3], total.at[3, :, lower], direct.at[1], left)
    copies.arrived(slots[0], relay.at[0])
    total[1, :, lower] = (total[1, :, lower].astype(F32) + relay[0].astype(F32)).astype(BF)
    copies.start(slots[4], total.at[1, :, lower], joined.at[0], right)
    copies.arrived(slots[1], relay.at[1])
    total[3, :, upper] = (total[3, :, upper].astype(F32) + relay[1].astype(F32)).astype(BF)
    copies.start(slots[5], total.at[3, :, upper], joined.at[1], left)
    out_ref[...] = pair(0)
    copies.arrived(slots[2], direct.at[0])
    out_ref[:, upper] += direct[0].astype(F32)
    copies.arrived(slots[3], direct.at[1])
    out_ref[:, lower] += direct[1].astype(F32)
    copies.arrived(slots[4], joined.at[0])
    out_ref[:, lower] += joined[0].astype(F32)
    copies.arrived(slots[5], joined.at[1])
    out_ref[:, upper] += joined[1].astype(F32)
    copies.sent()


def sum_narrow(p, collective_id):
    rows, cols = p.shape[2:]
    piece = pltpu.VMEM((2, rows, cols // 2), BF)
    return pl.pallas_call(
        sum_narrow_kernel,
        out_shape=jax.ShapeDtypeStruct((rows, cols), F32),
        in_specs=[VM],
        out_specs=VM,
        scratch_shapes=[
            pltpu.VMEM((4, rows, cols), BF),
            pltpu.VMEM((4, rows, cols), BF),
            piece,
            piece,
            piece,
            pltpu.SemaphoreType.DMA((10,)),
            pltpu.SemaphoreType.DMA((10,)),
        ],
        compiler_params=pltpu.CompilerParams(
            collective_id=collective_id, has_side_effects=True, vmem_limit_bytes=VMEM_LIMIT
        ),
        name=f"sum_narrow_{collective_id}",
    )(p)


def matmul_sum_kernel(
    x_ref, w_ref, sq_ref, out_ref, sqo_ref, part, mid, got1, got2, sq1, sqm, sq2,
    send1, recv1, send2, recv2, sq_send, sq_recv,
):
    pieces, width = part.shape[0], part.shape[-1]
    rows = x_ref.shape[3]
    y, z = wide_place()
    names = (("y", "z"), ("z", "y"))
    spots = ((y, z), (z, y))
    greet([ring_devices(axis, by) for axis in ("y", "z") for by in (1, 2, 3)])
    squares = Copies(sq_send, sq_recv)
    for by in (1, 2, 3):
        squares.start(by - 1, sq_ref.at[turn(y, by)], sq1.at[by - 1], ring_devices("y", by))

    def product(half, chunk, piece):
        block = x_ref[chunk, :, 0] if half == 0 else x_ref[:, chunk, 1]
        block = block.reshape(SIDE * rows, block.shape[-1])
        columns = pl.ds(pl.multiple_of(piece * width, 128), width)
        got = jnp.dot(block, w_ref[:, columns], preferred_element_type=F32)
        return got.reshape(SIDE, rows, width)

    def copy1(piece, half, kind, way, src):
        return pltpu.make_async_remote_copy(
            src_ref=src,
            dst_ref=got1.at[piece, half, kind, way],
            send_sem=send1.at[piece, half, kind, way],
            recv_sem=recv1.at[piece, half, kind, way],
            device_id=ring_devices(names[half][0], 1 if way == 0 else 3),
            device_id_type=MESH,
        )

    def copy2(piece, half, kind, way, src):
        return pltpu.make_async_remote_copy(
            src_ref=src,
            dst_ref=got2.at[piece, half, kind, way],
            send_sem=send2.at[piece, half, kind, way],
            recv_sem=recv2.at[piece, half, kind, way],
            device_id=ring_devices(names[half][1], 1 if way == 0 else 3),
            device_id_type=MESH,
        )

    def await1(piece, half, kind, way):
        ref = got1.at[piece, half, kind, way]
        pltpu.make_async_copy(ref, ref, recv1.at[piece, half, kind, way]).wait()
        return got1[piece, half, kind, way].astype(F32)

    def await2(piece, half, kind, way):
        ref = got2.at[piece, half, kind, way]
        pltpu.make_async_copy(ref, ref, recv2.at[piece, half, kind, way]).wait()
        return got2[piece, half, kind, way].astype(F32)

    lower, upper = pl.ds(0, 2), pl.ds(2, 2)
    low, high = pl.ds(0, rows // 2), pl.ds(rows // 2, rows // 2)

    def first(piece):
        for half in range(2):
            far = turn(spots[half][0], 2)
            part[piece, half, far] = product(half, far, piece).astype(BF)
            copy1(piece, half, 0, 0, part.at[piece, half, far, lower]).start()
            copy1(piece, half, 0, 1, part.at[piece, half, far, upper]).start()
        for half in range(2):
            right, left = turn(spots[half][0], 1), turn(spots[half][0], 3)
            part[piece, half, right] = product(half, right, piece).astype(BF)
            copy1(piece, half, 1, 0, part.at[piece, half, right, upper]).start()
            part[piece, half, left] = product(half, left, piece).astype(BF)
            copy1(piece, half, 1, 1, part.at[piece, half, left, lower]).start()

    def second(piece):
        for half in range(2):
            right, left = turn(spots[half][0], 1), turn(spots[half][0], 3)
            got = await1(piece, half, 0, 0)
            part[piece, half, right, lower] = (part[piece, half, right, lower].astype(F32) + got).astype(BF)
            copy1(piece, half, 2, 0, part.at[piece, half, right, lower]).start()
            got = await1(piece, half, 0, 1)
            part[piece, half, left, upper] = (part[piece, half, left, upper].astype(F32) + got).astype(BF)
            copy1(piece, half, 2, 1, part.at[piece, half, left, upper]).start()

    def third(piece):
        for half in range(2):
            own = product(half, spots[half][0], piece)
            mid[piece, half, lower] = (
                own[:2] + await1(piece, half, 1, 1) + await1(piece, half, 2, 0)
            ).astype(BF)
            mid[piece, half, upper] = (
                own[2:] + await1(piece, half, 1, 0) + await1(piece, half, 2, 1)
            ).astype(BF)
            far, right, left = (turn(spots[half][1], by) for by in (2, 1, 3))
            copy2(piece, half, 0, 0, mid.at[piece, half, far, low]).start()
            copy2(piece, half, 0, 1, mid.at[piece, half, far, high]).start()
            copy2(piece, half, 1, 0, mid.at[piece, half, right, high]).start()
            copy2(piece, half, 1, 1, mid.at[piece, half, left, low]).start()

    def fourth(piece):
        for half in range(2):
            right, left = turn(spots[half][1], 1), turn(spots[half][1], 3)
            got = await2(piece, half, 0, 0)
            mid[piece, half, right, low] = (mid[piece, half, right, low].astype(F32) + got).astype(BF)
            copy2(piece, half, 2, 0, mid.at[piece, half, right, low]).start()
            got = await2(piece, half, 0, 1)
            mid[piece, half, left, high] = (mid[piece, half, left, high].astype(F32) + got).astype(BF)
            copy2(piece, half, 2, 1, mid.at[piece, half, left, high]).start()

    def fifth(piece):
        columns = pl.ds(pl.multiple_of(piece * width, 128), width)
        for half in range(2):
            own = spots[half][1]
            out_ref[half, low, columns] = (
                mid[piece, half, own, low].astype(F32) + await2(piece, half, 1, 1) + await2(piece, half, 2, 0)
            )
            out_ref[half, high, columns] = (
                mid[piece, half, own, high].astype(F32) + await2(piece, half, 1, 0) + await2(piece, half, 2, 1)
            )

    stages = (first, second, third, fourth, fifth)

    def step(t, carry):
        for lag, stage in enumerate(stages):
            piece = t - lag

            @pl.when((piece >= 0) & (piece < pieces))
            def _():
                stage(jnp.clip(piece, 0, pieces - 1))

        return carry

    lax.fori_loop(0, pieces + len(stages) - 1, step, 0)

    for by in (1, 2, 3):
        squares.arrived(by - 1, sq1.at[by - 1])
    sqm[...] = sq_ref[y] + sq1[0] + sq1[1] + sq1[2]
    for by in (1, 2, 3):
        squares.start(2 + by, sqm.at[turn(z, by)], sq2.at[by - 1], ring_devices("z", by))
    for by in (1, 2, 3):
        squares.arrived(2 + by, sq2.at[by - 1])
    sqo_ref[...] = sqm[z] + sq2[0] + sq2[1] + sq2[2]
    squares.sent()

    def drain(piece, carry):
        for half in range(2):
            for kind in range(3):
                for way in range(2):
                    copy1(piece, half, kind, way, part.at[piece, half, 0, lower]).wait_send()
                    copy2(piece, half, kind, way, mid.at[piece, half, 0, low]).wait_send()
        return carry

    lax.fori_loop(0, pieces, drain, 0)


def matmul_sum(x, w, sq, pieces, collective_id):
    tokens, depth = x.shape
    cols = w.shape[1]
    width = cols // pieces
    rows = tokens // (2 * SIDE * SIDE)
    blocks = jnp.pad(sq.reshape(SIDE, SIDE, 1, 2 * rows), ((0, 0), (0, 0), (0, 0), (0, 128 - 2 * rows)))
    blocks = jnp.broadcast_to(blocks, (SIDE, SIDE, 8, 128))
    out, sq_out = pl.pallas_call(
        matmul_sum_kernel,
        out_shape=(
            jax.ShapeDtypeStruct((2, rows, cols), F32),
            jax.ShapeDtypeStruct((8, 128), F32),
        ),
        in_specs=[VM, VM, VM],
        out_specs=(VM, VM),
        scratch_shapes=[
            pltpu.VMEM((pieces, 2, SIDE, SIDE, rows, width), BF),
            pltpu.VMEM((pieces, 2, SIDE, rows, width), BF),
            pltpu.VMEM((pieces, 2, 3, 2, 2, rows, width), BF),
            pltpu.VMEM((pieces, 2, 3, 2, rows // 2, width), BF),
            pltpu.VMEM((3, SIDE, 8, 128), F32),
            pltpu.VMEM((SIDE, 8, 128), F32),
            pltpu.VMEM((3, 8, 128), F32),
            pltpu.SemaphoreType.DMA((pieces, 2, 3, 2)),
            pltpu.SemaphoreType.DMA((pieces, 2, 3, 2)),
            pltpu.SemaphoreType.DMA((pieces, 2, 3, 2)),
            pltpu.SemaphoreType.DMA((pieces, 2, 3, 2)),
            pltpu.SemaphoreType.DMA((6,)),
            pltpu.SemaphoreType.DMA((6,)),
        ],
        compiler_params=pltpu.CompilerParams(
            collective_id=collective_id, has_side_effects=True, vmem_limit_bytes=VMEM_LIMIT
        ),
        name=f"matmul_sum_{collective_id}",
    )(x.reshape(SIDE, SIDE, 2, rows, depth), w, blocks)
    return out.reshape(2 * rows, cols), sq_out[0, : 2 * rows]


def attend_kernel(lengths_ref, spot_ref, q_ref, cache_ref, span_ref, out_ref, sums_ref):
    scale = HDIM ** (-0.5)
    rows = q_ref.shape[1]
    per = span_ref.shape[2]
    block = cache_ref.shape[2] * 2

    for request in range(R):
        q = q_ref[request]

        def absorb(running, keys, values, allowed):
            peak, weight_sum, gathered = running
            scores = lax.dot_general(q, keys, (((1,), (1,)), ((), ())), preferred_element_type=F32) * scale
            scores = jnp.where(allowed(scores.shape), scores, floor_score)
            new_peak = jnp.maximum(peak, jnp.max(scores, axis=1, keepdims=True))
            weights = jnp.exp(scores - new_peak)
            factor = jnp.exp(peak - new_peak)
            weight_sum = weight_sum * factor + jnp.sum(weights, axis=1, keepdims=True)
            gathered = gathered * factor + jnp.dot(weights.astype(BF), values, preferred_element_type=F32)
            return new_peak, weight_sum, gathered

        span = span_ref[:, request].reshape(SIDE * SIDE * per, 2 * HDIM)

        def own_keys(shape):
            key = lax.broadcasted_iota(jnp.int32, shape, 1)
            row = lax.broadcasted_iota(jnp.int32, shape, 0)
            return key <= spot_ref[0] * per + lax.rem(row, per)

        running = absorb(
            (
                jnp.full((rows, 1), floor_score, F32),
                jnp.zeros((rows, 1), F32),
                jnp.zeros((rows, HDIM), F32),
            ),
            span[:, :HDIM],
            span[:, HDIM:],
            own_keys,
        )
        length = lengths_ref[request]

        def cached(index, running):
            pair = cache_ref[pl.ds(index * 2, 2), request].reshape(block, 2 * HDIM)

            def in_use(shape):
                return index * block + lax.broadcasted_iota(jnp.int32, shape, 1) < length

            keep = index * block + lax.broadcasted_iota(jnp.int32, (block, HDIM), 0) < length
            values = jnp.where(keep, pair[:, HDIM:], jnp.zeros((), BF))
            return absorb(running, pair[:, :HDIM], values, in_use)

        peak, weight_sum, gathered = lax.fori_loop(0, lax.div(length + block - 1, block), cached, running)
        out_ref[request] = (gathered / weight_sum).astype(BF)
        sums_ref[request] = jnp.broadcast_to(peak + jnp.log(weight_sum), (rows, HDIM))


def attend(lengths, spot, queries, cache, span):
    return pl.pallas_call(
        attend_kernel,
        out_shape=(
            jax.ShapeDtypeStruct(queries.shape, BF),
            jax.ShapeDtypeStruct(queries.shape, F32),
        ),
        in_specs=[SM, SM, VM, VM, VM],
        out_specs=(VM, VM),
        compiler_params=pltpu.CompilerParams(vmem_limit_bytes=VMEM_LIMIT),
        name="attend",
    )(lengths, spot, queries, cache, span)


def token_angles(lengths, offsets, first_token, row_count, dim_size):
    token_ids = first_token + jnp.arange(row_count, dtype=jnp.int32)
    request_ids = token_ids % R
    start_pos = offsets + lengths
    matches = request_ids[:, None] == jnp.arange(start_pos.shape[0], dtype=jnp.int32)[None, :]
    chosen = jnp.sum(jnp.where(matches, start_pos[None, :], 0), axis=1)
    position = (chosen + token_ids // R).astype(jnp.float32)
    inverse = rope_base ** (-(jnp.arange(dim_size // 2, dtype=jnp.float32) * 2.0) / dim_size)
    return position[:, None] * inverse[None, :]


def rotate(values, angles):
    half_dim = values.shape[-1] // 2
    first_half = values[..., :half_dim]
    second_half = values[..., half_dim:]
    cosine = jnp.cos(angles)[:, None, :]
    sine_part = jnp.sin(angles)[:, None, :]
    return jnp.concatenate(
        [
            first_half * cosine - second_half * sine_part,
            second_half * cosine + first_half * sine_part,
        ],
        axis=-1,
    )


def to_send(flipped, gain):
    widened = flipped.astype(F32)
    squares = jnp.sum(widened * widened, axis=0, keepdims=True)
    high = lax.reduce_precision(squares, 8, 7)
    rest = squares - high
    middle = lax.reduce_precision(rest, 8, 7)
    low = rest - middle
    scaled = widened * gain.astype(F32)[:, None]
    pad = jnp.zeros((5, flipped.shape[1]), F32)
    return jnp.concatenate([scaled, high, middle, low, pad], axis=0).astype(BF)


def unpack(gathered, rows):
    scaled = gathered[:, :rows].reshape(8 * rows, -1).T
    squares = jnp.sum(gathered[:, rows : rows + 3].astype(F32), axis=(0, 1))
    return scaled, squares


def rescale(sums, squares):
    inv_scale = lax.rsqrt(squares / D + epsilon)[:, None]
    return jnp.where(inv_scale > 0, sums * inv_scale, 0.0)


def local(
    hidden_in, attn_gain, w_qkv, cache_kv, lengths, offsets, w_out, mlp_gain, w_gate_up, w_down
):
    wide_index = lax.axis_index("wide")
    all_tokens, features = hidden_in.shape
    per_device = all_tokens // lax.axis_size("wide")
    first_token = wide_index * per_device
    flipped = hidden_in.T
    positions = cache_kv.shape[1]
    cache = cache_kv.reshape(R, positions, 2 * HDIM)
    gathered, cache_all = gather_both(to_send(flipped, attn_gain), cache, 1)
    scaled, squares = unpack(gathered, features)
    projected, squares = matmul_sum(scaled, w_qkv.reshape(w_qkv.shape[0], -1), squares, 3, 2)
    projected = rescale(projected, squares).reshape(per_device, GROUP + 2, HDIM)
    angles = token_angles(lengths, offsets, first_token, per_device, HDIM)
    rotated = rotate(projected[:, : GROUP + 1], angles).astype(BF)
    new_keys, new_values = rotated[:, GROUP], projected[:, GROUP + 1].astype(BF)
    new_cache = jnp.stack([new_keys, new_values], axis=1)[:, None]
    per_request = per_device // R
    span = jnp.concatenate([new_keys, new_values], axis=1).reshape(per_request, R, 2 * HDIM)
    span_all = gather_wide(span.transpose(1, 0, 2), 3)
    queries = rotated[:, :GROUP].reshape(per_request, R, GROUP, HDIM).transpose(1, 2, 0, 3)
    attended, sums = attend(
        lengths,
        wide_index.reshape(1),
        queries.reshape(R, GROUP * per_request, HDIM),
        cache_all.reshape(SIDE * SIDE, R, positions, 2 * HDIM),
        span_all.reshape(SIDE * SIDE, R, per_request, 2 * HDIM),
    )
    attended = attended.reshape(R, GROUP, per_request, HDIM).transpose(2, 0, 1, 3).reshape(2, -1, GROUP * HDIM)
    softmax_sums = sums[:, :, 0].reshape(R, GROUP, per_request).transpose(2, 0, 1).reshape(per_device, GROUP)
    attended_all = gather_wide(attended, 4).reshape(all_tokens, -1)
    out_terms = lax.dot_general(
        w_out, attended_all, (((0,), (1,)), ((), ())), preferred_element_type=F32
    ).astype(BF)
    summed = sum_narrow(out_terms.reshape(4, 2, features, all_tokens), 5)
    residual = (flipped.astype(F32) + summed).astype(BF)
    scaled, squares = unpack(gather_narrow(to_send(residual, mlp_gain), 6), features)
    units = w_gate_up.shape[2]
    both, squares = matmul_sum(scaled, w_gate_up.reshape(w_gate_up.shape[0], -1), squares, 4, 7)
    both = rescale(both, squares)
    hidden = (jax.nn.silu(both[:, :units]) * both[:, units:]).astype(BF)
    hidden_all = gather_wide(hidden.reshape(2, -1, units), 8).reshape(all_tokens, units)
    down_terms = lax.dot_general(
        w_down, hidden_all, (((0,), (1,)), ((), ())), preferred_element_type=F32
    ).astype(BF)
    summed = sum_narrow(down_terms.reshape(4, 2, features, all_tokens), 9)
    hidden_out = (residual.astype(F32) + summed).astype(BF).T
    return (hidden_out, softmax_sums, new_cache)


def solution(mesh):
    return jax.shard_map(
        local,
        mesh=mesh,
        in_specs=(
            P(None, ("wide", "narrow")),
            P(("wide", "narrow")),
            P("wide", "narrow", None),
            P(None, "wide", "narrow", None, None),
            P(),
            P(),
            P("narrow", "wide"),
            P(("wide", "narrow")),
            P("wide", None, "narrow"),
            P("narrow", "wide"),
        ),
        out_specs=(
            P(None, ("wide", "narrow")),
            P("wide", "narrow"),
            P("wide", "narrow", None, None),
        ),
        check_vma=False,
    )
```

time: 630 us -> 291 us (0.46)
  waiting for transfers between devices: 395 us -> 0 us
  Pallas kernels: 0 us -> 247 us
  blocking collectives: 134 us -> 0 us
  matrix products: 39.8 us -> 9.64 us
  between operations: 15.6 us -> 0.96 us
    reduce_scatter x4 -> x0, waiting for transfers between devices: 263 us -> none  [the longest x1 134 us: local(): lax.psum_scatter(jnp.dot(row_block, flat_gate_up, preferred_element_type=...]
    pallas_call x0 -> x10, Pallas kernels: none -> 247 us  [the longest x2 91.4 us: matmul_sum(): pl.pallas_call(matmul_sum_kernel, out_shape=(jax.ShapeDtypeStruct((2, row...]
    all_gather x3 -> x0, waiting for transfers between devices: 132 us -> none  [the longest x1 56.2 us: local(): lax.all_gather(hidden, 'wide', axis=0, tiled=True)]
    psum x2 -> x0, blocking collectives: 68 us -> none  [norm_block(): squares = lax.psum(jnp.sum(widened * widened, axis=1), 'wide')]
    all_gather x3 -> x0, blocking collectives: 52.6 us -> none  [the longest x2 33.6 us: norm_block(): lax.all_gather(values, 'narrow', axis=1, tiled=True)]
    dot_general x8 -> x2, matrix products: 39.8 us -> 9.64 us  [the longest x1 6.01 us: local(): lax.dot_general(w_down, hidden_all, (((0,), (1,)), ((), ())), preferred_e...]
    unnamed x1 -> x0, blocking collectives: 13.2 us -> none
    reduce_sum x4, other arithmetic: 12 us -> 3.85 us  [the longest x2 1.97 us: to_send(): squares = jnp.sum(widened * widened, axis=0, keepdims=True)]
  transfers between devices with their start and end apart: 7 -> 0, of which waited for: 7 -> 0; matrix products, arithmetic and copies ran while one was open for 2% -> 0% of each run, Pallas kernels for 0% -> 0%
where the time goes in v1:
time: 291 us; the launch traced here: 290 us
  Pallas kernels  247 us (85%)
  local copies, waits for them, and re-layouts  20.8 us (7%)
  other arithmetic  12.4 us (4%)
  matrix products  9.64 us (3%)
    pallas_call x2, Pallas kernels, matmul_sum(): pl.pallas_call(matmul_sum_kernel, out_shape=(jax.ShapeDtypeStruct((2, row...  91.4 us
    pallas_call x3, Pallas kernels, gather_wide(): pl.pallas_call(gather_wide_kernel, out_shape=jax.ShapeDtypeStruct((SIDE,...  58.2 us
    pallas_call x2, Pallas kernels, sum_narrow(): pl.pallas_call(sum_narrow_kernel, out_shape=jax.ShapeDtypeStruct((rows, c...  42.1 us
    pallas_call x1, Pallas kernels, gather_both(): pl.pallas_call(gather_both_kernel, out_shape=(jax.ShapeDtypeStruct((8,) +...  33 us
    pallas_call x1, Pallas kernels, gather_narrow(): pl.pallas_call(gather_narrow_kernel, out_shape=jax.ShapeDtypeStruct((8,)...  13.3 us
    pallas_call x1, Pallas kernels, attend(): pl.pallas_call(attend_kernel, out_shape=(jax.ShapeDtypeStruct(queries.sha...  8.56 us
    unnamed x18, local copies, waits for them, and re-layouts  6.09 us
    dot_general x1, matrix products, local(): lax.dot_general(w_down, hidden_all, (((0,), (1,)), ((), ())), preferred_e...  6.01 us

profile of v1, /device:TPU:1, one launch (start us, length us, event | category | flops | bytes accessed | tf_op | source)
XLA Modules:
  0.0 290.4 jit_solution(16662412915840735661)
XLA Ops:
  0.6 0.0 copy-start
  0.6 0.8 convert_element_type.67
  1.5 1.0 fusion.6
  2.5 1.3 concatenate.18.x_ref
  3.8 1.8 reshape.280.cache_ref
  5.6 33.0 %gather_both.1 = (bf16[8,64,1024]{2,1,0:T(8,128)(2,1)}, bf16[4,4,2,256,256]{4,3,2,1,0:T(8,128)(2,1)}) custom-call(bf16[64,1024]{1,0:T(8,128)(2,1)} %concatenate.18.x_ref, bf16[2,256,256]{2,1,0:T(8,128)(2,1)} %reshape.280.cache_ref), custom_call_target="tpu_custom_call" | custom-call | tf_op jit(solution)/shard_map/gather_both/pallas_call | solution.py:264
  38.5 1.2 slice.45
  39.8 1.3 copy.27
  41.1 0.9 convert_reduce_fusion.1
  42.0 0.1 reshape.284
  42.1 0.6 broadcast_in_dim.67.sq_ref
  42.8 0.0 copy-start.3
  42.8 24.7 %matmul_sum_2.1 = (f32[2,32,1152]{2,1,0:T(8,128)}, f32[8,128]{1,0:T(8,128)}) custom-call(bf16[4,4,2,32,448]{4,3,2,1,0:T(8,128)(2,1)} %bitcast.78, bf16[448,1152]{1,0:T(8,128)(2,1)} %bitcast.85, f32[4,4,8,128]{3,2,1,0:T(8,128)} %broadcast_in_dim.67.sq_ref), custom_call_target="tpu_custom_call" | custom-call | tf_op jit(solution)/shard_map/matmul_sum_2/pallas_call | solution.py:506
  67.5 0.7 broadcast_compare_fusion.1
  68.2 1.0 reshape.285
  69.2 0.2 multiply_select_fusion
  69.4 0.0 copy-done.3
  69.4 0.0 copy-done.5
  69.5 0.1 fusion.11
  69.6 0.2 multiply_cosine_fusion
  69.8 0.2 subtract_convert_fusion
  70.0 0.1 pad_maximum_fusion
  70.2 0.6 maximum_bitcast_fusion.x_ref
  70.8 13.7 %gather_wide_3.1 = bf16[4,4,2,32,256]{4,3,2,1,0:T(8,128)(2,1)} custom-call(bf16[2,32,256]{2,1,0:T(8,128)(2,1)} %maximum_bitcast_fusion.x_ref), custom_call_target="tpu_custom_call" | custom-call | tf_op jit(solution)/shard_map/gather_wide_3/pallas_call | solution.py:179
  84.5 0.1 slice_maximum_fusion
  84.6 0.7 copy.28
  85.3 8.6 %attend.1 = (bf16[2,224,128]{2,1,0:T(8,128)(2,1)}, f32[2,224,128]{2,1,0:T(8,128)}) custom-call(s32[2]{0:T(128)} %lengths_ref.1, s32[1]{0:T(128)} %bitcast.1.spot_ref, bf16[2,224,128]{2,1,0:T(8,128)(2,1)} %bitcast.90, bf16[16,2,256,256]{3,2,1,0:T(8,128)(2,1)} %bitcast.77, bf16[16,2,32,256]{3,2,1,0:T(8,128)(2,1)} %bitcast.82), custom_call_target="tpu_custom_call" | custom-call | tf_op jit(solution)/shard_map/attend/pallas_call | solution.py:592
  93.8 0.0 copy-start.4
  93.8 1.0 copy.40
  94.9 0.8 reshape.291.x_ref
  95.7 15.2 %gather_wide_4.1 = bf16[4,4,2,32,896]{4,3,2,1,0:T(8,128)(2,1)} custom-call(bf16[2,32,896]{2,1,0:T(8,128)(2,1)} %reshape.291.x_ref), custom_call_target="tpu_custom_call" | custom-call | tf_op jit(solution)/shard_map/gather_wide_4/pallas_call | solution.py:179
  110.9 0.0 copy-done.4
  110.9 0.0 copy-start.1
  111.0 0.0 copy-start.6
  111.0 3.6 %convolution_convert_fusion.1 = bf16[1024,448]{0,1:T(8,128)(2,1)} fusion(bf16[1024,896]{1,0:T(8,128)(2,1)} %bitcast.83, bf16[896,448]{0,1:T(8,128)(2,1)S(1)} %copy-done.4), kind=kOutput, calls=%fused_computation.1 | convolution fusion | flops 822542336 | bytes 3555328 | tf_op jit(solution)/shard_map/dot_general | solution.py:686
  114.6 25.7 %sum_narrow_5.1 = f32[56,1024]{1,0:T(8,128)} custom-call(bf16[4,2,56,1024]{3,2,1,0:T(8,128)(2,1)} %bitcast.86), custom_call_target="tpu_custom_call" | custom-call | tf_op jit(solution)/shard_map/sum_narrow_5/pallas_call | solution.py:330
  140.3 0.0 copy-done.1
  140.3 1.0 fusion.3
  141.3 0.0 copy-done.6
  141.3 0.1 fusion.2
  141.4 1.3 concatenate.22.x_ref
  142.7 13.3 %gather_narrow_6.1 = bf16[8,64,1024]{2,1,0:T(8,128)(2,1)} custom-call(bf16[64,1024]{1,0:T(8,128)(2,1)} %concatenate.22.x_ref), custom_call_target="tpu_custom_call" | custom-call | tf_op jit(solution)/shard_map/gather_narrow_6/pallas_call | solution.py:237
  156.1 0.0 slice-start
  156.1 1.2 slice-done
  157.2 1.3 copy.32
  158.6 0.9 convert_reduce_fusion
  159.5 0.1 reshape.297
  159.6 0.6 broadcast_in_dim.73.sq_ref
  160.2 5.4 %copy.38 = bf16[56,8,2,2560]{3,1,2,0:T(8,128)(2,1)} copy(bf16[56,8,2,2560]{3,2,1,0:T(2,128)(2,1)} %bitcast.76) | data formatting | bytes 9175040
  165.6 66.7 %matmul_sum_7.1 = (f32[2,32,5120]{2,1,0:T(8,128)}, f32[8,128]{1,0:T(8,128)}) custom-call(bf16[4,4,2,32,448]{4,3,2,1,0:T(8,128)(2,1)} %bitcast.79, bf16[448,5120]{1,0:T(8,128)(2,1)} %bitcast.74, f32[4,4,8,128]{3,2,1,0:T(8,128)} %broadcast_in_dim.73.sq_ref), custom_call_target="tpu_custom_call" | custom-call | tf_op jit(solution)/shard_map/matmul_sum_7/pallas_call | solution.py:506
  232.3 0.7 broadcast_compare_fusion
  233.0 1.5 fusion
  234.5 0.9 fusion.1
  235.4 29.3 %gather_wide_8.1 = bf16[4,4,2,32,2560]{4,3,2,1,0:T(8,128)(2,1)} custom-call(bf16[2,32,2560]{2,1,0:T(8,128)(2,1)} %bitcast.84), custom_call_target="tpu_custom_call" | custom-call | tf_op jit(solution)/shard_map/gather_wide_8/pallas_call | solution.py:179
  264.6 0.0 copy-done
  264.7 6.0 %convolution_convert_fusion = bf16[1024,448]{0,1:T(8,128)(2,1)} fusion(bf16[1024,2560]{1,0:T(8,128)(2,1)} %bitcast.75, bf16[2560,448]{0,1:T(8,128)(2,1)S(1)} %copy-done), kind=kOutput, calls=%fused_computation | convolution fusion | flops 2349268992 | bytes 8454144 | tf_op jit(solution)/shard_map/dot_general | solution.py:697
  270.7 16.5 %sum_narrow_9.1 = f32[56,1024]{1,0:T(8,128)} custom-call(bf16[4,2,56,1024]{3,2,1,0:T(8,128)(2,1)} %bitcast.87), custom_call_target="tpu_custom_call" | custom-call | tf_op jit(solution)/shard_map/sum_narrow_9/pallas_call | solution.py:330
  287.1 1.6 fusion.8
  288.7 0.7 maximum_bitcast_fusion.1
  289.4 0.0 copy-done.2
  289.4 0.1 slice_reduce_fusion
  289.6 0.1 reshape_squeeze.3
  289.7 0.1 copy.33
  289.8 0.7 copy.34
  (17 shorter events, 0.1 us)
Async XLA Ops:
  0.6 264.0 %copy-start = (bf16[2560,448]{0,1:T(8,128)(2,1)S(1)}, bf16[2560,448]{0,1:T(8,128)(2,1)}, u32[]{:S(2)}) copy-start(bf16[2560,448]{0,1:T(8,128)(2,1)} %param.19) | copy-start | bytes 6881284
  42.8 26.7 %copy-start.3 = (s32[2]{0:T(128)S(1)}, s32[2]{0:T(128)}, u32[]{:S(2)}) copy-start(s32[2]{0:T(128)} %lengths_ref.1) | copy-start | bytes 28
  42.8 26.7 %copy-start.5 = (s32[2]{0:T(128)S(1)}, s32[2]{0:T(128)}, u32[]{:S(2)}) copy-start(s32[2]{0:T(128)} %param.15) | copy-start | bytes 28
  93.8 17.1 %copy-start.4 = (bf16[896,448]{0,1:T(8,128)(2,1)S(1)}, bf16[896,448]{0,1:T(8,128)(2,1)}, u32[]{:S(2)}) copy-start(bf16[896,448]{0,1:T(8,128)(2,1)} %param.16) | copy-start | bytes 2408452
  110.9 29.3 %copy-start.1 = (bf16[1024,56]{0,1:T(8,128)(2,1)S(1)}, bf16[1024,56]{0,1:T(8,128)(2,1)}, u32[]{:S(2)}) copy-start(bf16[1024,56]{0,1:T(8,128)(2,1)} %param.10) | copy-start | bytes 344068
  111.0 30.3 %copy-start.6 = (bf16[56]{0:T(256)(128)(2,1)S(1)}, bf16[56]{0:T(256)(128)(2,1)}, u32[]{:S(2)}) copy-start(bf16[56]{0:T(256)(128)(2,1)} %param.17) | copy-start | bytes 340
  156.1 1.2 slice-start
  270.7 18.8 %copy-start.2 = (f32[2,224,128]{2,1,0:T(8,128)S(1)}, f32[2,224,128]{2,1,0:T(8,128)}, u32[]{:S(2)}) copy-start(f32[2,224,128]{2,1,0:T(8,128)} %get-tuple-element.18) | copy-start | bytes 688132

commit v2 on v1

--- a/solution.py
+++ b/solution.py
@@ -20,7 +20,6 @@
 MESH = pl.DeviceIdType.MESH
 BF = jnp.bfloat16
 F32 = jnp.float32
-ANY = pl.BlockSpec(memory_space=pl.ANY)
 VM = pl.BlockSpec(memory_space=pltpu.VMEM)
 SM = pl.BlockSpec(memory_space=pltpu.SMEM)
 VMEM_LIMIT = 60 * 1024 * 1024
@@ -164,6 +163,54 @@
 WIDE_COPIES = 40
 
 
+def gather_direct_steps(x_ref, out_ref, local_sem, copies):
+    y, z = wide_place()
+    names = (("y", "z"), ("z", "y"))
+    spots = ((y, z), (z, y))
+
+    def place(half, first, second):
+        if half == 0:
+            return out_ref.at[first, second, 0]
+        return out_ref.at[second, first, 1]
+
+    own = pltpu.make_async_copy(x_ref, out_ref.at[y, z], local_sem)
+    own.start()
+    hop1 = [[copies.slot() for _ in range(3)] for _ in range(2)]
+    hop2 = [[[copies.slot() for _ in range(3)] for _ in range(4)] for _ in range(2)]
+
+    def send2(half, block, src):
+        target = place(half, turn(spots[half][0], block), spots[half][1])
+        for by in (2, 1, 3):
+            copies.start(hop2[half][block][by - 1], src, target, ring_devices(names[half][1], by))
+
+    for half in range(2):
+        target = place(half, *spots[half])
+        for by in (2, 1, 3):
+            copies.start(hop1[half][by - 1], x_ref.at[half], target, ring_devices(names[half][0], by))
+    for half in range(2):
+        send2(half, 0, x_ref.at[half])
+    yield
+    for by in (1, 3, 2):
+        for half in range(2):
+            came = place(half, turn(spots[half][0], 4 - by), spots[half][1])
+            copies.arrived(hop1[half][by - 1], came)
+            send2(half, 4 - by, came)
+        yield
+    for block in range(4):
+        for half in range(2):
+            for by in (1, 3, 2):
+                came = place(half, turn(spots[half][0], block), turn(spots[half][1], 4 - by))
+                copies.arrived(hop2[half][block][by - 1], came)
+    own.wait()
+
+
+DIRECT_COPIES = 30
+
+
+def wide_lines():
+    return [ring_devices(axis, by) for axis in ("y", "z") for by in (1, 2, 3)]
+
+
 def wide_neighbours():
     return [ring_devices(axis, by) for axis in ("y", "z") for by in (1, 3)]
 
@@ -180,13 +227,15 @@
         gather_wide_kernel,
         out_shape=jax.ShapeDtypeStruct((SIDE, SIDE) + x.shape, x.dtype),
         in_specs=[VM],
-        out_specs=ANY,
+        out_specs=VM,
         scratch_shapes=[
             pltpu.SemaphoreType.DMA,
             pltpu.SemaphoreType.DMA((WIDE_COPIES,)),
             pltpu.SemaphoreType.DMA((WIDE_COPIES,)),
         ],
-        compiler_params=pltpu.CompilerParams(collective_id=collective_id, has_side_effects=True),
+        compiler_params=pltpu.CompilerParams(
+            collective_id=collective_id, has_side_effects=True, vmem_limit_bytes=VMEM_LIMIT
+        ),
         name=f"gather_wide_{collective_id}",
     )(x)
 
@@ -244,7 +293,9 @@
             pltpu.SemaphoreType.DMA((NARROW_COPIES,)),
             pltpu.SemaphoreType.DMA((NARROW_COPIES,)),
         ],
-        compiler_params=pltpu.CompilerParams(collective_id=collective_id, has_side_effects=True),
+        compiler_params=pltpu.CompilerParams(
+            collective_id=collective_id, has_side_effects=True, vmem_limit_bytes=VMEM_LIMIT
+        ),
         name=f"gather_narrow_{collective_id}",
     )(x)
 
@@ -268,7 +319,7 @@
             jax.ShapeDtypeStruct((SIDE, SIDE) + cache.shape, cache.dtype),
         ),
         in_specs=[VM, VM],
-        out_specs=(VM, ANY),
+        out_specs=(VM, VM),
         scratch_shapes=[
             pltpu.SemaphoreType.DMA((2,)),
             pltpu.SemaphoreType.DMA((NARROW_COPIES,)),
@@ -276,7 +327,9 @@
             pltpu.SemaphoreType.DMA((WIDE_COPIES,)),
             pltpu.SemaphoreType.DMA((WIDE_COPIES,)),
         ],
-        compiler_params=pltpu.CompilerParams(collective_id=collective_id, has_side_effects=True),
+        compiler_params=pltpu.CompilerParams(
+            collective_id=collective_id, has_side_effects=True, vmem_limit_bytes=VMEM_LIMIT
+        ),
         name="gather_both",
     )(x, cache)
 
@@ -534,72 +587,90 @@
     return out.reshape(2 * rows, cols), sq_out[0, : 2 * rows]
 
 
-def attend_kernel(lengths_ref, spot_ref, q_ref, cache_ref, span_ref, out_ref, sums_ref):
+CHUNK = 2
+
+
+def attend_kernel(
+    lengths_ref, q_ref, cache_ref, own_ref, out_ref, sums_ref, span_ref, local_sem, send_sem, recv_sem
+):
     scale = HDIM ** (-0.5)
     rows = q_ref.shape[1]
-    per = span_ref.shape[2]
-    block = cache_ref.shape[2] * 2
-
+    per = own_ref.shape[1]
+    block = cache_ref.shape[2] * CHUNK
+    spot = lax.axis_index("wide")
+    copies = Copies(send_sem, recv_sem)
+    greet(wide_lines())
+    gather = gather_direct_steps(own_ref, span_ref, local_sem, copies)
+    next(gather)
+    queries = [q_ref[request] for request in range(R)]
+
+    def absorb(running, q, keys, values, allowed):
+        peak, weight_sum, gathered = running
+        scores = lax.dot_general(q, keys, (((1,), (1,)), ((), ())), preferred_element_type=F32) * scale
+        scores = jnp.where(allowed(scores.shape), scores, floor_score)
+        new_peak = jnp.maximum(peak, jnp.max(scores, axis=1, keepdims=True))
+        weights = jnp.exp(scores - new_peak)
+        factor = jnp.exp(peak - new_peak)
+        weight_sum = weight_sum * factor + jnp.sum(weights, axis=1, keepdims=True)
+        gathered = gathered * factor + jnp.dot(weights.astype(BF), values, preferred_element_type=F32)
+        return new_peak, weight_sum, gathered
+
+    def own_keys(shape):
+        key = lax.broadcasted_iota(jnp.int32, shape, 1)
+        row = lax.broadcasted_iota(jnp.int32, shape, 0)
+        return key <= spot * per + lax.rem(row, per)
+
+    running = [
+        (
+            jnp.full((rows, 1), floor_score, F32),
+            jnp.zeros((rows, 1), F32),
+            jnp.zeros((rows, HDIM), F32),
+        )
+        for _ in range(R)
+    ]
+    for index in range(cache_ref.shape[0] // CHUNK):
+        for request in range(R):
+            pair = cache_ref[pl.ds(index * CHUNK, CHUNK), request].reshape(block, 2 * HDIM)
+            running[request] = absorb(
+                running[request],
+                queries[request],
+                pair[:, :HDIM],
+                pair[:, HDIM:],
+                lambda shape: index * block + lax.broadcasted_iota(jnp.int32, shape, 1) < lengths_ref[request],
+            )
+        if index >= 2:
+            next(gather, None)
+    interleave(gather)
     for request in range(R):
-        q = q_ref[request]
-
-        def absorb(running, keys, values, allowed):
-            peak, weight_sum, gathered = running
-            scores = lax.dot_general(q, keys, (((1,), (1,)), ((), ())), preferred_element_type=F32) * scale
-            scores = jnp.where(allowed(scores.shape), scores, floor_score)
-            new_peak = jnp.maximum(peak, jnp.max(scores, axis=1, keepdims=True))
-            weights = jnp.exp(scores - new_peak)
-            factor = jnp.exp(peak - new_peak)
-            weight_sum = weight_sum * factor + jnp.sum(weights, axis=1, keepdims=True)
-            gathered = gathered * factor + jnp.dot(weights.astype(BF), values, preferred_element_type=F32)
-            return new_peak, weight_sum, gathered
-
-        span = span_ref[:, request].reshape(SIDE * SIDE * per, 2 * HDIM)
-
-        def own_keys(shape):
-            key = lax.broadcasted_iota(jnp.int32, shape, 1)
-            row = lax.broadcasted_iota(jnp.int32, shape, 0)
-            return key <= spot_ref[0] * per + lax.rem(row, per)
-
-        running = absorb(
-            (
-                jnp.full((rows, 1), floor_score, F32),
-                jnp.zeros((rows, 1), F32),
-                jnp.zeros((rows, HDIM), F32),
-            ),
-            span[:, :HDIM],
-            span[:, HDIM:],
-            own_keys,
+        span = span_ref[:, :, request].reshape(SIDE * SIDE * per, 2 * HDIM)
+        peak, weight_sum, gathered = absorb(
+            running[request], queries[request], span[:, :HDIM], span[:, HDIM:], own_keys
         )
-        length = lengths_ref[request]
-
-        def cached(index, running):
-            pair = cache_ref[pl.ds(index * 2, 2), request].reshape(block, 2 * HDIM)
-
-            def in_use(shape):
-                return index * block + lax.broadcasted_iota(jnp.int32, shape, 1) < length
-
-            keep = index * block + lax.broadcasted_iota(jnp.int32, (block, HDIM), 0) < length
-            values = jnp.where(keep, pair[:, HDIM:], jnp.zeros((), BF))
-            return absorb(running, pair[:, :HDIM], values, in_use)
-
-        peak, weight_sum, gathered = lax.fori_loop(0, lax.div(length + block - 1, block), cached, running)
         out_ref[request] = (gathered / weight_sum).astype(BF)
         sums_ref[request] = jnp.broadcast_to(peak + jnp.log(weight_sum), (rows, HDIM))
-
-
-def attend(lengths, spot, queries, cache, span):
+    copies.sent()
+
+
+def attend(lengths, queries, cache, own, collective_id):
     return pl.pallas_call(
         attend_kernel,
         out_shape=(
             jax.ShapeDtypeStruct(queries.shape, BF),
             jax.ShapeDtypeStruct(queries.shape, F32),
         ),
-        in_specs=[SM, SM, VM, VM, VM],
+        in_specs=[SM, VM, VM, VM],
         out_specs=(VM, VM),
-        compiler_params=pltpu.CompilerParams(vmem_limit_bytes=VMEM_LIMIT),
+        scratch_shapes=[
+            pltpu.VMEM((SIDE, SIDE) + own.shape, BF),
+            pltpu.SemaphoreType.DMA,
+            pltpu.SemaphoreType.DMA((DIRECT_COPIES,)),
+            pltpu.SemaphoreType.DMA((DIRECT_COPIES,)),
+        ],
+        compiler_params=pltpu.CompilerParams(
+            collective_id=collective_id, has_side_effects=True, vmem_limit_bytes=VMEM_LIMIT
+        ),
         name="attend",
-    )(lengths, spot, queries, cache, span)
+    )(lengths, queries, cache, own)
 
 
 def token_angles(lengths, offsets, first_token, row_count, dim_size):
@@ -654,10 +725,9 @@
 def local(
     hidden_in, attn_gain, w_qkv, cache_kv, lengths, offsets, w_out, mlp_gain, w_gate_up, w_down
 ):
-    wide_index = lax.axis_index("wide")
     all_tokens, features = hidden_in.shape
     per_device = all_tokens // lax.axis_size("wide")
-    first_token = wide_index * per_device
+    first_token = lax.axis_index("wide") * per_device
     flipped = hidden_in.T
     positions = cache_kv.shape[1]
     cache = cache_kv.reshape(R, positions, 2 * HDIM)
@@ -671,14 +741,13 @@
     new_cache = jnp.stack([new_keys, new_values], axis=1)[:, None]
     per_request = per_device // R
     span = jnp.concatenate([new_keys, new_values], axis=1).reshape(per_request, R, 2 * HDIM)
-    span_all = gather_wide(span.transpose(1, 0, 2), 3)
     queries = rotated[:, :GROUP].reshape(per_request, R, GROUP, HDIM).transpose(1, 2, 0, 3)
     attended, sums = attend(
         lengths,
-        wide_index.reshape(1),
         queries.reshape(R, GROUP * per_request, HDIM),
         cache_all.reshape(SIDE * SIDE, R, positions, 2 * HDIM),
-        span_all.reshape(SIDE * SIDE, R, per_request, 2 * HDIM),
+        span.transpose(1, 0, 2),
+        3,
     )
     attended = attended.reshape(R, GROUP, per_request, HDIM).transpose(2, 0, 1, 3).reshape(2, -1, GROUP * HDIM)
     softmax_sums = sums[:, :, 0].reshape(R, GROUP, per_request).transpose(2, 0, 1).reshape(per_device, GROUP)

time: 291 us -> 283 us (0.973)
  Pallas kernels: 247 us -> 239 us
    pallas_call x3 -> x2, Pallas kernels: 58.2 us -> 47.3 us  [gather_wide(): pl.pallas_call(gather_wide_kernel, out_shape=jax.ShapeDtypeStruct((SIDE,...]
    pallas_call x1, Pallas kernels: 8.56 us -> 14.6 us  [attend(): pl.pallas_call(attend_kernel, out_shape=(jax.ShapeDtypeStruct(queries.sha...]
where the time goes in v2:
time: 283 us
  Pallas kernels  239 us (84%)
  local copies, waits for them, and re-layouts  20.8 us (7%)
  other arithmetic  12.4 us (4%)
  matrix products  9.63 us (3%)
    pallas_call x2, Pallas kernels, matmul_sum(): pl.pallas_call(matmul_sum_kernel, out_shape=(jax.ShapeDtypeStruct((2, row...  90.2 us
    pallas_call x2, Pallas kernels, gather_wide(): pl.pallas_call(gather_wide_kernel, out_shape=jax.ShapeDtypeStruct((SIDE,...  47.3 us
    pallas_call x2, Pallas kernels, sum_narrow(): pl.pallas_call(sum_narrow_kernel, out_shape=jax.ShapeDtypeStruct((rows, c...  39.6 us
    pallas_call x1, Pallas kernels, gather_both(): pl.pallas_call(gather_both_kernel, out_shape=(jax.ShapeDtypeStruct((8,) +...  33.8 us
    pallas_call x1, Pallas kernels, attend(): pl.pallas_call(attend_kernel, out_shape=(jax.ShapeDtypeStruct(queries.sha...  14.6 us
    pallas_call x1, Pallas kernels, gather_narrow(): pl.pallas_call(gather_narrow_kernel, out_shape=jax.ShapeDtypeStruct((8,)...  13.1 us
    unnamed x18, local copies, waits for them, and re-layouts  6.09 us
    dot_general x1, matrix products, local(): lax.dot_general(w_down, hidden_all, (((0,), (1,)), ((), ())), preferred_e...  6.01 us

profile of v2, /device:TPU:1, one launch (start us, length us, event | category | flops | bytes accessed | tf_op | source)
XLA Modules:
  0.0 282.5 jit_solution(14578093749551912089)
XLA Ops:
  0.6 0.0 copy-start
  0.6 0.8 convert_element_type.67
  1.5 1.0 fusion.6
  2.5 1.3 concatenate.18.x_ref
  3.8 1.8 reshape.273.cache_ref
  5.6 33.8 %gather_both.1 = (bf16[8,64,1024]{2,1,0:T(8,128)(2,1)}, bf16[4,4,2,256,256]{4,3,2,1,0:T(8,128)(2,1)}) custom-call(bf16[64,1024]{1,0:T(8,128)(2,1)} %concatenate.18.x_ref, bf16[2,256,256]{2,1,0:T(8,128)(2,1)} %reshape.273.cache_ref), custom_call_target="tpu_custom_call" | custom-call | tf_op jit(solution)/shard_map/gather_both/pallas_call | solution.py:315
  39.4 1.2 slice.45
  40.7 1.3 copy.27
  42.0 0.9 convert_reduce_fusion.1
  42.9 0.1 reshape.277
  43.0 0.6 broadcast_in_dim.67.sq_ref
  43.6 0.0 copy-start.3
  43.6 0.0 copy-start.5
  43.6 24.2 %matmul_sum_2.1 = (f32[2,32,1152]{2,1,0:T(8,128)}, f32[8,128]{1,0:T(8,128)}) custom-call(bf16[4,4,2,32,448]{4,3,2,1,0:T(8,128)(2,1)} %bitcast.76, bf16[448,1152]{1,0:T(8,128)(2,1)} %bitcast.82, f32[4,4,8,128]{3,2,1,0:T(8,128)} %broadcast_in_dim.67.sq_ref), custom_call_target="tpu_custom_call" | custom-call | tf_op jit(solution)/shard_map/matmul_sum_2/pallas_call | solution.py:559
  67.9 0.7 broadcast_compare_fusion.1
  68.5 1.0 reshape.278
  69.6 0.2 multiply_select_fusion
  69.8 0.0 copy-done.3
  69.8 0.0 copy-done.5
  69.8 0.1 fusion.11
  69.9 0.2 multiply_cosine_fusion
  70.1 0.2 subtract_convert_fusion
  70.3 0.1 pad_maximum_fusion
  70.5 0.6 maximum_bitcast_fusion.own_ref
  71.1 0.1 slice_maximum_fusion
  71.3 0.7 copy.28
  71.9 14.6 %attend.1 = (bf16[2,224,128]{2,1,0:T(8,128)(2,1)}, f32[2,224,128]{2,1,0:T(8,128)}) custom-call(s32[2]{0:T(128)} %lengths_ref.1, bf16[2,224,128]{2,1,0:T(8,128)(2,1)} %bitcast.87, bf16[16,2,256,256]{3,2,1,0:T(8,128)(2,1)} %bitcast.75, bf16[2,32,256]{2,1,0:T(8,128)(2,1)} %maximum_bitcast_fusion.own_ref), custom_call_target="tpu_custom_call" | custom-call | tf_op jit(solution)/shard_map/attend/pallas_call | solution.py:655
  86.6 0.0 copy-start.4
  86.6 1.0 copy.40
  87.6 0.8 reshape.283.x_ref
  88.4 15.7 %gather_wide_4.1 = bf16[4,4,2,32,896]{4,3,2,1,0:T(8,128)(2,1)} custom-call(bf16[2,32,896]{2,1,0:T(8,128)(2,1)} %reshape.283.x_ref), custom_call_target="tpu_custom_call" | custom-call | tf_op jit(solution)/shard_map/gather_wide_4/pallas_call | solution.py:226
  104.1 0.0 copy-done.4
  104.1 0.0 copy-start.1
  104.1 0.0 copy-start.6
  104.1 3.6 %convolution_convert_fusion.1 = bf16[1024,448]{0,1:T(8,128)(2,1)} fusion(bf16[1024,896]{1,0:T(8,128)(2,1)} %bitcast.80, bf16[896,448]{0,1:T(8,128)(2,1)S(1)} %copy-done.4), kind=kOutput, calls=%fused_computation.1 | convolution fusion | flops 822542336 | bytes 3555328 | tf_op jit(solution)/shard_map/dot_general | solution.py:755
  107.7 23.3 %sum_narrow_5.1 = f32[56,1024]{1,0:T(8,128)} custom-call(bf16[4,2,56,1024]{3,2,1,0:T(8,128)(2,1)} %bitcast.83), custom_call_target="tpu_custom_call" | custom-call | tf_op jit(solution)/shard_map/sum_narrow_5/pallas_call | solution.py:383
  131.0 0.0 copy-done.1
  131.0 1.0 fusion.3
  132.0 0.0 copy-done.6
  132.0 0.1 fusion.2
  132.1 1.3 concatenate.22.x_ref
  133.4 13.1 %gather_narrow_6.1 = bf16[8,64,1024]{2,1,0:T(8,128)(2,1)} custom-call(bf16[64,1024]{1,0:T(8,128)(2,1)} %concatenate.22.x_ref), custom_call_target="tpu_custom_call" | custom-call | tf_op jit(solution)/shard_map/gather_narrow_6/pallas_call | solution.py:286
  146.6 0.0 slice-start
  146.6 1.2 slice-done
  147.7 1.3 copy.32
  149.1 0.9 convert_reduce_fusion
  150.0 0.1 reshape.289
  150.1 0.6 broadcast_in_dim.73.sq_ref
  150.7 5.4 %copy.38 = bf16[56,8,2,2560]{3,1,2,0:T(8,128)(2,1)} copy(bf16[56,8,2,2560]{3,2,1,0:T(2,128)(2,1)} %bitcast.74) | data formatting | bytes 9175040
  156.1 66.0 %matmul_sum_7.1 = (f32[2,32,5120]{2,1,0:T(8,128)}, f32[8,128]{1,0:T(8,128)}) custom-call(bf16[4,4,2,32,448]{4,3,2,1,0:T(8,128)(2,1)} %bitcast.77, bf16[448,5120]{1,0:T(8,128)(2,1)} %bitcast.72, f32[4,4,8,128]{3,2,1,0:T(8,128)} %broadcast_in_dim.73.sq_ref), custom_call_target="tpu_custom_call" | custom-call | tf_op jit(solution)/shard_map/matmul_sum_7/pallas_call | solution.py:559
  222.1 0.7 broadcast_compare_fusion
  222.8 1.5 fusion
  224.3 0.9 fusion.1
  225.2 31.7 %gather_wide_8.1 = bf16[4,4,2,32,2560]{4,3,2,1,0:T(8,128)(2,1)} custom-call(bf16[2,32,2560]{2,1,0:T(8,128)(2,1)} %bitcast.81), custom_call_target="tpu_custom_call" | custom-call | tf_op jit(solution)/shard_map/gather_wide_8/pallas_call | solution.py:226
  256.9 0.0 copy-done
  256.9 6.0 %convolution_convert_fusion = bf16[1024,448]{0,1:T(8,128)(2,1)} fusion(bf16[1024,2560]{1,0:T(8,128)(2,1)} %bitcast.73, bf16[2560,448]{0,1:T(8,128)(2,1)S(1)} %copy-done), kind=kOutput, calls=%fused_computation | convolution fusion | flops 2349268992 | bytes 8454144 | tf_op jit(solution)/shard_map/dot_general | solution.py:766
  262.9 16.3 %sum_narrow_9.1 = f32[56,1024]{1,0:T(8,128)} custom-call(bf16[4,2,56,1024]{3,2,1,0:T(8,128)(2,1)} %bitcast.84), custom_call_target="tpu_custom_call" | custom-call | tf_op jit(solution)/shard_map/sum_narrow_9/pallas_call | solution.py:383
  279.2 1.6 fusion.8
  280.8 0.7 maximum_bitcast_fusion.1
  281.5 0.0 copy-done.2
  281.5 0.1 slice_reduce_fusion
  281.7 0.1 reshape_squeeze.3
  281.8 0.1 copy.33
  281.9 0.7 copy.34
  (16 shorter events, 0.1 us)
Async XLA Ops:
  0.6 256.2 %copy-start = (bf16[2560,448]{0,1:T(8,128)(2,1)S(1)}, bf16[2560,448]{0,1:T(8,128)(2,1)}, u32[]{:S(2)}) copy-start(bf16[2560,448]{0,1:T(8,128)(2,1)} %param.19) | copy-start | bytes 6881284
  43.6 26.2 %copy-start.3 = (s32[2]{0:T(128)S(1)}, s32[2]{0:T(128)}, u32[]{:S(2)}) copy-start(s32[2]{0:T(128)} %lengths_ref.1) | copy-start | bytes 28
  43.6 26.2 %copy-start.5 = (s32[2]{0:T(128)S(1)}, s32[2]{0:T(128)}, u32[]{:S(2)}) copy-start(s32[2]{0:T(128)} %param.15) | copy-start | bytes 28
  86.6 17.5 %copy-start.4 = (bf16[896,448]{0,1:T(8,128)(2,1)S(1)}, bf16[896,448]{0,1:T(8,128)(2,1)}, u32[]{:S(2)}) copy-start(bf16[896,448]{0,1:T(8,128)(2,1)} %param.16) | copy-start | bytes 2408452
  104.1 26.9 %copy-start.1 = (bf16[1024,56]{0,1:T(8,128)(2,1)S(1)}, bf16[1024,56]{0,1:T(8,128)(2,1)}, u32[]{:S(2)}) copy-start(bf16[1024,56]{0,1:T(8,128)(2,1)} %param.10) | copy-start | bytes 344068
  104.1 27.9 %copy-start.6 = (bf16[56]{0:T(256)(128)(2,1)S(1)}, bf16[56]{0:T(256)(128)(2,1)}, u32[]{:S(2)}) copy-start(bf16[56]{0:T(256)(128)(2,1)} %param.17) | copy-start | bytes 340
  146.6 1.2 slice-start
  262.9 18.7 %copy-start.2 = (f32[2,224,128]{2,1,0:T(8,128)S(1)}, f32[2,224,128]{2,1,0:T(8,128)}, u32[]{:S(2)}) copy-start(f32[2,224,128]{2,1,0:T(8,128)} %get-tuple-element.18) | copy-start | bytes 688132

commit v3 on v2

--- a/solution.py
+++ b/solution.py
@@ -585,6 +585,281 @@
         name=f"matmul_sum_{collective_id}",
     )(x.reshape(SIDE, SIDE, 2, rows, depth), w, blocks)
     return out.reshape(2 * rows, cols), sq_out[0, : 2 * rows]
+
+
+def gate_up_kernel(
+    x_ref, w_ref, sq_ref, out_ref, part, mid, hid, got1, got2, sq1, sqm, sq2, inv,
+    send1, recv1, send2, recv2, send3, recv3, send4, recv4, own_sem, sq_send, sq_recv,
+):
+    pieces, width = part.shape[0], part.shape[-1]
+    units = out_ref.shape[-1]
+    wide = width // 2
+    rows = x_ref.shape[3]
+    y, z = wide_place()
+    names = (("y", "z"), ("z", "y"))
+    spots = ((y, z), (z, y))
+    greet(wide_lines())
+    squares = Copies(sq_send, sq_recv)
+    for by in (1, 2, 3):
+        squares.start(by - 1, sq_ref.at[turn(y, by)], sq1.at[by - 1], ring_devices("y", by))
+
+    lower, upper = pl.ds(0, 2), pl.ds(2, 2)
+    low, high = pl.ds(0, rows // 2), pl.ds(rows // 2, rows // 2)
+
+    def product(half, chunk, piece):
+        block = x_ref[chunk, :, 0] if half == 0 else x_ref[:, chunk, 1]
+        block = block.reshape(SIDE * rows, block.shape[-1])
+        at = pl.multiple_of(piece * wide, 128)
+        gate = jnp.dot(block, w_ref[:, pl.ds(at, wide)], preferred_element_type=F32)
+        up = jnp.dot(block, w_ref[:, pl.ds(pl.multiple_of(units + at, 128), wide)], preferred_element_type=F32)
+        return jnp.concatenate([gate, up], axis=1).reshape(SIDE, rows, width)
+
+    def remote(src, dst, send, recv, axis, way):
+        return pltpu.make_async_remote_copy(
+            src_ref=src,
+            dst_ref=dst,
+            send_sem=send,
+            recv_sem=recv,
+            device_id=ring_devices(axis, 1 if way == 0 else 3),
+            device_id_type=MESH,
+        )
+
+    def copy1(piece, half, kind, way, src):
+        spot = (piece, half, kind, way)
+        return remote(src, got1.at[spot], send1.at[spot], recv1.at[spot], names[half][0], way)
+
+    def copy2(piece, half, kind, way, src):
+        spot = (piece, half, kind, way)
+        return remote(src, got2.at[spot], send2.at[spot], recv2.at[spot], names[half][1], way)
+
+    def landed(ref, sem):
+        pltpu.make_async_copy(ref, ref, sem).wait()
+
+    def await1(piece, half, kind, way):
+        landed(got1.at[piece, half, kind, way], recv1.at[piece, half, kind, way])
+        return got1[piece, half, kind, way].astype(F32)
+
+    def await2(piece, half, kind, way):
+        landed(got2.at[piece, half, kind, way], recv2.at[piece, half, kind, way])
+        return got2[piece, half, kind, way].astype(F32)
+
+    def place(piece, half, first, second, part_rows):
+        columns = pl.ds(pl.multiple_of(piece * wide, 128), wide)
+        if half == 0:
+            return out_ref.at[first, second, 0, part_rows, columns]
+        return out_ref.at[second, first, 1, part_rows, columns]
+
+    whole = pl.ds(0, rows)
+
+    def copy3(piece, half, kind, way, src, dst):
+        return remote(src, dst, send3.at[piece, half, kind, way], recv3.at[piece, half, kind, way], names[half][0], way)
+
+    def copy4(piece, half, block, kind, way, src, dst):
+        spot = (piece, half, block, kind, way)
+        return remote(src, dst, send4.at[spot], recv4.at[spot], names[half][1], way)
+
+    def send4_whole(piece, half, block, src):
+        dst = place(piece, half, turn(spots[half][0], block), spots[half][1], whole)
+        for way in range(2):
+            copy4(piece, half, block, 0, way, src, dst).start()
+
+    def relay4(piece, half, block):
+        first = turn(spots[half][0], block)
+        for way, by, part_rows in ((0, 3, low), (1, 1, high)):
+            second = turn(spots[half][1], by)
+            landed(place(piece, half, first, second, whole), recv4.at[piece, half, block, 0, way])
+            came = place(piece, half, first, second, part_rows)
+            copy4(piece, half, block, 1, way, came, came).start()
+
+    def stage1(piece):
+        for half in range(2):
+            far = turn(spots[half][0], 2)
+            part[piece, half, far] = product(half, far, piece).astype(BF)
+            copy1(piece, half, 0, 0, part.at[piece, half, far, lower]).start()
+            copy1(piece, half, 0, 1, part.at[piece, half, far, upper]).start()
+        for half in range(2):
+            right, left = turn(spots[half][0], 1), turn(spots[half][0], 3)
+            part[piece, half, right] = product(half, right, piece).astype(BF)
+            copy1(piece, half, 1, 0, part.at[piece, half, right, upper]).start()
+            part[piece, half, left] = product(half, left, piece).astype(BF)
+            copy1(piece, half, 1, 1, part.at[piece, half, left, lower]).start()
+
+    def stage2(piece):
+        for half in range(2):
+            right, left = turn(spots[half][0], 1), turn(spots[half][0], 3)
+            got = await1(piece, half, 0, 0)
+            part[piece, half, right, lower] = (part[piece, half, right, lower].astype(F32) + got).astype(BF)
+            copy1(piece, half, 2, 0, part.at[piece, half, right, lower]).start()
+            got = await1(piece, half, 0, 1)
+            part[piece, half, left, upper] = (part[piece, half, left, upper].astype(F32) + got).astype(BF)
+            copy1(piece, half, 2, 1, part.at[piece, half, left, upper]).start()
+
+    def stage3(piece):
+        for half in range(2):
+            own = product(half, spots[half][0], piece)
+            mid[piece, half, lower] = (
+                own[:2] + await1(piece, half, 1, 1) + await1(piece, half, 2, 0)
+            ).astype(BF)
+            mid[piece, half, upper] = (
+                own[2:] + await1(piece, half, 1, 0) + await1(piece, half, 2, 1)
+            ).astype(BF)
+            far, right, left = (turn(spots[half][1], by) for by in (2, 1, 3))
+            copy2(piece, half, 0, 0, mid.at[piece, half, far, low]).start()
+            copy2(piece, half, 0, 1, mid.at[piece, half, far, high]).start()
+            copy2(piece, half, 1, 0, mid.at[piece, half, right, high]).start()
+            copy2(piece, half, 1, 1, mid.at[piece, half, left, low]).start()
+
+    def stage4(piece):
+        for half in range(2):
+            right, left = turn(spots[half][1], 1), turn(spots[half][1], 3)
+            got = await2(piece, half, 0, 0)
+            mid[piece, half, right, low] = (mid[piece, half, right, low].astype(F32) + got).astype(BF)
+            copy2(piece, half, 2, 0, mid.at[piece, half, right, low]).start()
+            got = await2(piece, half, 0, 1)
+            mid[piece, half, left, high] = (mid[piece, half, left, high].astype(F32) + got).astype(BF)
+            copy2(piece, half, 2, 1, mid.at[piece, half, left, high]).start()
+
+    def activate(sums, factor):
+        sums = jnp.where(factor > 0, sums * factor, 0.0)
+        gate, up = sums[:, :wide], sums[:, wide:]
+        return (gate / (1.0 + jnp.exp(-gate)) * up).astype(BF)
+
+    def stage5(piece):
+        for half in range(2):
+            own = spots[half][1]
+            hid[piece, half, low] = activate(
+                mid[piece, half, own, low].astype(F32) + await2(piece, half, 1, 1) + await2(piece, half, 2, 0),
+                inv[half, low][:, :1],
+            )
+            hid[piece, half, high] = activate(
+                mid[piece, half, own, high].astype(F32) + await2(piece, half, 1, 0) + await2(piece, half, 2, 1),
+                inv[half, high][:, :1],
+            )
+            mine = hid.at[piece, half]
+            dst = place(piece, half, *spots[half], whole)
+            pltpu.make_async_copy(mine, dst, own_sem.at[piece, half]).start()
+            for way in range(2):
+                copy3(piece, half, 0, way, mine, dst).start()
+            send4_whole(piece, half, 0, mine)
+
+    def stage6(piece):
+        for half in range(2):
+            for way, by, part_rows in ((0, 3, low), (1, 1, high)):
+                first = turn(spots[half][0], by)
+                landed(place(piece, half, first, spots[half][1], whole), recv3.at[piece, half, 0, way])
+                came = place(piece, half, first, spots[half][1], part_rows)
+                copy3(piece, half, 1, way, came, came).start()
+                send4_whole(piece, half, by, place(piece, half, first, spots[half][1], whole))
+        for half in range(2):
+            relay4(piece, half, 0)
+
+    def stage7(piece):
+        for half in range(2):
+            far = turn(spots[half][0], 2)
+            landed(place(piece, half, far, spots[half][1], low), recv3.at[piece, half, 1, 0])
+            landed(place(piece, half, far, spots[half][1], high), recv3.at[piece, half, 1, 1])
+            send4_whole(piece, half, 2, place(piece, half, far, spots[half][1], whole))
+        for half in range(2):
+            relay4(piece, half, 3)
+            relay4(piece, half, 1)
+
+    def stage8(piece):
+        for half in range(2):
+            relay4(piece, half, 2)
+
+    def stage9(piece):
+        for half in range(2):
+            for block in range(4):
+                first, second = turn(spots[half][0], block), turn(spots[half][1], 2)
+                landed(place(piece, half, first, second, low), recv4.at[piece, half, block, 1, 0])
+                landed(place(piece, half, first, second, high), recv4.at[piece, half, block, 1, 1])
+            mine = place(piece, half, *spots[half], whole)
+            landed(mine, own_sem.at[piece, half])
+            for way in range(2):
+                for kind in range(3):
+                    copy1(piece, half, kind, way, part.at[piece, half, 0, lower]).wait_send()
+                    copy2(piece, half, kind, way, mid.at[piece, half, 0, low]).wait_send()
+                for kind, part_rows in ((0, whole), (1, low)):
+                    ref = place(piece, half, *spots[half], part_rows)
+                    copy3(piece, half, kind, way, ref, ref).wait_send()
+                    for block in range(4):
+                        copy4(piece, half, block, kind, way, ref, ref).wait_send()
+
+    stages = (stage1, stage2, stage3, stage4, stage5, stage6, stage7, stage8, stage9)
+
+    def step(t, carry):
+        for lag, stage in enumerate(stages):
+            piece = t - lag
+
+            @pl.when((piece >= 0) & (piece < pieces))
+            def _():
+                stage(jnp.clip(piece, 0, pieces - 1))
+
+        return carry
+
+    lax.fori_loop(0, 3, step, 0)
+
+    for by in (1, 2, 3):
+        squares.arrived(by - 1, sq1.at[by - 1])
+    sqm[...] = sq_ref[y] + sq1[0] + sq1[1] + sq1[2]
+    for by in (1, 2, 3):
+        squares.start(2 + by, sqm.at[turn(z, by)], sq2.at[by - 1], ring_devices("z", by))
+    lax.fori_loop(3, 4, step, 0)
+    for by in (1, 2, 3):
+        squares.arrived(2 + by, sq2.at[by - 1])
+    total = (sqm[z] + sq2[0] + sq2[1] + sq2[2])[:1]
+    factor = lax.rsqrt(total / D + epsilon)
+    token = lax.broadcasted_iota(jnp.int32, (2 * rows, 128), 0)
+    lane = lax.broadcasted_iota(jnp.int32, (2 * rows, 128), 1)
+    column = jnp.sum(jnp.where(token == lane, factor, 0.0), axis=1, keepdims=True)
+    inv[...] = jnp.broadcast_to(column, (2 * rows, 128)).reshape(2, rows, 128)
+    lax.fori_loop(4, pieces + len(stages) - 1, step, 0)
+    squares.sent()
+
+
+def token_blocks(sq, rows):
+    blocks = jnp.pad(sq.reshape(SIDE, SIDE, 1, 2 * rows), ((0, 0), (0, 0), (0, 0), (0, 128 - 2 * rows)))
+    return jnp.broadcast_to(blocks, (SIDE, SIDE, 8, 128))
+
+
+def gate_up(x, w, sq, pieces, collective_id):
+    tokens, depth = x.shape
+    units = w.shape[1] // 2
+    width = 2 * units // pieces
+    rows = tokens // (2 * SIDE * SIDE)
+    dma = pltpu.SemaphoreType.DMA
+    return pl.pallas_call(
+        gate_up_kernel,
+        out_shape=jax.ShapeDtypeStruct((SIDE, SIDE, 2, rows, units), BF),
+        in_specs=[VM, VM, VM],
+        out_specs=VM,
+        scratch_shapes=[
+            pltpu.VMEM((pieces, 2, SIDE, SIDE, rows, width), BF),
+            pltpu.VMEM((pieces, 2, SIDE, rows, width), BF),
+            pltpu.VMEM((pieces, 2, rows, width // 2), BF),
+            pltpu.VMEM((pieces, 2, 3, 2, 2, rows, width), BF),
+            pltpu.VMEM((pieces, 2, 3, 2, rows // 2, width), BF),
+            pltpu.VMEM((3, SIDE, 8, 128), F32),
+            pltpu.VMEM((SIDE, 8, 128), F32),
+            pltpu.VMEM((3, 8, 128), F32),
+            pltpu.VMEM((2, rows, 128), F32),
+            dma((pieces, 2, 3, 2)),
+            dma((pieces, 2, 3, 2)),
+            dma((pieces, 2, 3, 2)),
+            dma((pieces, 2, 3, 2)),
+            dma((pieces, 2, 2, 2)),
+            dma((pieces, 2, 2, 2)),
+            dma((pieces, 2, 4, 2, 2)),
+            dma((pieces, 2, 4, 2, 2)),
+            dma((pieces, 2)),
+            dma((6,)),
+            dma((6,)),
+        ],
+        compiler_params=pltpu.CompilerParams(
+            collective_id=collective_id, has_side_effects=True, vmem_limit_bytes=VMEM_LIMIT
+        ),
+        name="gate_up",
+    )(x.reshape(SIDE, SIDE, 2, rows, depth), w, token_blocks(sq, rows))
 
 
 CHUNK = 2
@@ -759,10 +1034,7 @@
     residual = (flipped.astype(F32) + summed).astype(BF)
     scaled, squares = unpack(gather_narrow(to_send(residual, mlp_gain), 6), features)
     units = w_gate_up.shape[2]
-    both, squares = matmul_sum(scaled, w_gate_up.reshape(w_gate_up.shape[0], -1), squares, 4, 7)
-    both = rescale(both, squares)
-    hidden = (jax.nn.silu(both[:, :units]) * both[:, units:]).astype(BF)
-    hidden_all = gather_wide(hidden.reshape(2, -1, units), 8).reshape(all_tokens, units)
+    hidden_all = gate_up(scaled, w_gate_up.reshape(w_gate_up.shape[0], -1), squares, 4, 7).reshape(all_tokens, units)
     down_terms = lax.dot_general(
         w_down, hidden_all, (((0,), (1,)), ((), ())), preferred_element_type=F32
     ).astype(BF)

time: 283 us -> 276 us (0.975)
  Pallas kernels: 239 us -> 233 us
    pallas_call x0 -> x1, Pallas kernels: none -> 94.6 us  [gate_up(): pl.pallas_call(gate_up_kernel, out_shape=jax.ShapeDtypeStruct((SIDE, SIDE...]
    pallas_call x2 -> x1, Pallas kernels: 90.2 us -> 24.2 us  [matmul_sum(): pl.pallas_call(matmul_sum_kernel, out_shape=(jax.ShapeDtypeStruct((2, row...]
    pallas_call x2 -> x1, Pallas kernels: 47.3 us -> 15.6 us  [gather_wide(): pl.pallas_call(gather_wide_kernel, out_shape=jax.ShapeDtypeStruct((SIDE,...]
    unnamed x18 -> x10, local copies, waits for them, and re-layouts: 6.09 us -> 6.14 us
where the time goes in v3:
time: 276 us; the launch traced here: 275 us
  Pallas kernels  233 us (84%)
  local copies, waits for them, and re-layouts  20.7 us (8%)
  other arithmetic  10.7 us (4%)
  matrix products  9.62 us (3%)
    pallas_call x1, Pallas kernels, gate_up(): pl.pallas_call(gate_up_kernel, out_shape=jax.ShapeDtypeStruct((SIDE, SIDE...  94.6 us
    pallas_call x2, Pallas kernels, sum_narrow(): pl.pallas_call(sum_narrow_kernel, out_shape=jax.ShapeDtypeStruct((rows, c...  36.9 us
    pallas_call x1, Pallas kernels, gather_both(): pl.pallas_call(gather_both_kernel, out_shape=(jax.ShapeDtypeStruct((8,) +...  33.8 us
    pallas_call x1, Pallas kernels, matmul_sum(): pl.pallas_call(matmul_sum_kernel, out_shape=(jax.ShapeDtypeStruct((2, row...  24.2 us
    pallas_call x1, Pallas kernels, gather_wide(): pl.pallas_call(gather_wide_kernel, out_shape=jax.ShapeDtypeStruct((SIDE,...  15.6 us
    pallas_call x1, Pallas kernels, attend(): pl.pallas_call(attend_kernel, out_shape=(jax.ShapeDtypeStruct(queries.sha...  14.6 us
    pallas_call x1, Pallas kernels, gather_narrow(): pl.pallas_call(gather_narrow_kernel, out_shape=jax.ShapeDtypeStruct((8,)...  13.2 us
    unnamed x10, local copies, waits for them, and re-layouts  6.14 us

profile of v3, /device:TPU:1, one launch (start us, length us, event | category | flops | bytes accessed | tf_op | source)
XLA Modules:
  0.0 274.9 jit_solution(8486789618716875633)
XLA Ops:
  0.6 0.0 copy-start
  0.7 0.8 convert_element_type.64
  1.5 0.7 add.70
  2.1 0.7 convert_element_type.73
  2.8 0.1 fusion.9
  2.9 0.2 multiply_cosine_fusion
  3.1 1.0 fusion.4
  4.1 1.3 concatenate.18.x_ref
  5.4 1.8 reshape.250.cache_ref
  7.2 5.4 %copy.38 = bf16[56,8,2,2560]{3,1,2,0:T(8,128)(2,1)} copy(bf16[56,8,2,2560]{3,2,1,0:T(2,128)(2,1)} %bitcast.66) | data formatting | bytes 9175040
  12.7 33.8 %gather_both.1 = (bf16[8,64,1024]{2,1,0:T(8,128)(2,1)}, bf16[4,4,2,256,256]{4,3,2,1,0:T(8,128)(2,1)}) custom-call(bf16[64,1024]{1,0:T(8,128)(2,1)} %concatenate.18.x_ref, bf16[2,256,256]{2,1,0:T(8,128)(2,1)} %reshape.250.cache_ref), custom_call_target="tpu_custom_call" | custom-call | tf_op jit(solution)/shard_map/gather_both/pallas_call | solution.py:315
  46.5 0.9 convert_reduce_fusion.1
  47.5 1.2 slice.36
  48.7 0.1 reshape.254
  48.8 0.6 broadcast_in_dim.54.sq_ref
  49.4 1.3 copy.27
  50.8 24.2 %matmul_sum_2.1 = (f32[2,32,1152]{2,1,0:T(8,128)}, f32[8,128]{1,0:T(8,128)}) custom-call(bf16[4,4,2,32,448]{4,3,2,1,0:T(8,128)(2,1)} %bitcast.68, bf16[448,1152]{1,0:T(8,128)(2,1)} %bitcast.73, f32[4,4,8,128]{3,2,1,0:T(8,128)} %broadcast_in_dim.54.sq_ref), custom_call_target="tpu_custom_call" | custom-call | tf_op jit(solution)/shard_map/matmul_sum_2/pallas_call | solution.py:559
  75.0 0.7 broadcast_compare_fusion
  75.6 1.0 reshape.255
  76.7 0.2 multiply_select_fusion
  76.9 0.2 subtract_convert_fusion
  77.1 0.1 pad_maximum_fusion
  77.2 0.1 slice_maximum_fusion
  77.3 0.7 copy.28
  78.0 0.7 maximum_bitcast_fusion.1
  78.7 0.6 maximum_bitcast_fusion.own_ref
  79.3 14.6 %attend.1 = (bf16[2,224,128]{2,1,0:T(8,128)(2,1)}, f32[2,224,128]{2,1,0:T(8,128)}) custom-call(s32[2]{0:T(128)} %lengths_ref.1, bf16[2,224,128]{2,1,0:T(8,128)(2,1)} %bitcast.78, bf16[16,2,256,256]{3,2,1,0:T(8,128)(2,1)} %bitcast.67, bf16[2,32,256]{2,1,0:T(8,128)(2,1)} %maximum_bitcast_fusion.own_ref), custom_call_target="tpu_custom_call" | custom-call | tf_op jit(solution)/shard_map/attend/pallas_call | solution.py:930
  94.0 0.0 copy-start.2
  94.0 1.2 slice_reduce_fusion
  95.1 0.1 reshape_squeeze.3
  95.2 1.0 copy.40
  96.2 0.8 reshape.260.x_ref
  97.0 0.1 copy.33
  97.1 0.7 copy.34
  97.8 15.6 %gather_wide_4.1 = bf16[4,4,2,32,896]{4,3,2,1,0:T(8,128)(2,1)} custom-call(bf16[2,32,896]{2,1,0:T(8,128)(2,1)} %reshape.260.x_ref), custom_call_target="tpu_custom_call" | custom-call | tf_op jit(solution)/shard_map/gather_wide_4/pallas_call | solution.py:226
  113.4 0.0 copy-done.2
  113.4 0.0 copy-start.1
  113.4 3.6 %convolution_convert_fusion.1 = bf16[1024,448]{0,1:T(8,128)(2,1)} fusion(bf16[1024,896]{1,0:T(8,128)(2,1)} %bitcast.72, bf16[896,448]{0,1:T(8,128)(2,1)S(1)} %copy-done.2), kind=kOutput, calls=%fused_computation.1 | convolution fusion | flops 822542336 | bytes 3555328 | tf_op jit(solution)/shard_map/dot_general | solution.py:1030
  117.0 23.3 %sum_narrow_5.1 = f32[56,1024]{1,0:T(8,128)} custom-call(bf16[4,2,56,1024]{3,2,1,0:T(8,128)(2,1)} %bitcast.74), custom_call_target="tpu_custom_call" | custom-call | tf_op jit(solution)/shard_map/sum_narrow_5/pallas_call | solution.py:383
  140.3 0.0 copy-done.1
  140.3 1.0 fusion.1
  141.3 0.1 fusion
  141.4 1.3 concatenate.22.x_ref
  142.7 13.2 %gather_narrow_6.1 = bf16[8,64,1024]{2,1,0:T(8,128)(2,1)} custom-call(bf16[64,1024]{1,0:T(8,128)(2,1)} %concatenate.22.x_ref), custom_call_target="tpu_custom_call" | custom-call | tf_op jit(solution)/shard_map/gather_narrow_6/pallas_call | solution.py:286
  155.9 0.0 slice-start
  155.9 1.0 convert_reduce_fusion
  156.9 0.1 reshape.266
  157.0 0.6 broadcast_in_dim.60.sq_ref
  157.6 0.0 slice-done
  157.6 1.3 copy.32
  159.0 94.6 %gate_up.1 = bf16[4,4,2,32,2560]{4,3,2,1,0:T(8,128)(2,1)} custom-call(bf16[4,4,2,32,448]{4,3,2,1,0:T(8,128)(2,1)} %bitcast.69, bf16[448,5120]{1,0:T(8,128)(2,1)} %bitcast.64, f32[4,4,8,128]{3,2,1,0:T(8,128)} %broadcast_in_dim.60.sq_ref), custom_call_target="tpu_custom_call" | custom-call | tf_op jit(solution)/shard_map/gate_up/pallas_call | solution.py:831
  253.6 0.0 copy-done
  253.6 6.0 %convolution_convert_fusion = bf16[1024,448]{0,1:T(8,128)(2,1)} fusion(bf16[1024,2560]{1,0:T(8,128)(2,1)} %bitcast.65, bf16[2560,448]{0,1:T(8,128)(2,1)S(1)} %copy-done), kind=kOutput, calls=%fused_computation | convolution fusion | flops 2349268992 | bytes 8454144 | tf_op jit(solution)/shard_map/dot_general | solution.py:1038
  259.6 13.7 %sum_narrow_9.1 = f32[56,1024]{1,0:T(8,128)} custom-call(bf16[4,2,56,1024]{3,2,1,0:T(8,128)(2,1)} %bitcast.75), custom_call_target="tpu_custom_call" | custom-call | tf_op jit(solution)/shard_map/sum_narrow_9/pallas_call | solution.py:383
  273.3 1.6 fusion.6
  (13 shorter events, 0.1 us)
Async XLA Ops:
  0.6 252.9 %copy-start = (bf16[2560,448]{0,1:T(8,128)(2,1)S(1)}, bf16[2560,448]{0,1:T(8,128)(2,1)}, u32[]{:S(2)}) copy-start(bf16[2560,448]{0,1:T(8,128)(2,1)} %param.19) | copy-start | bytes 6881284
  94.0 19.4 %copy-start.2 = (bf16[896,448]{0,1:T(8,128)(2,1)S(1)}, bf16[896,448]{0,1:T(8,128)(2,1)}, u32[]{:S(2)}) copy-start(bf16[896,448]{0,1:T(8,128)(2,1)} %param.16) | copy-start | bytes 2408452
  113.4 26.9 %copy-start.1 = (bf16[1024,56]{0,1:T(8,128)(2,1)S(1)}, bf16[1024,56]{0,1:T(8,128)(2,1)}, u32[]{:S(2)}) copy-start(bf16[1024,56]{0,1:T(8,128)(2,1)} %param.10) | copy-start | bytes 344068
  155.9 1.8 slice-start

commit v4 on v3

--- a/solution.py
+++ b/solution.py
@@ -213,31 +213,6 @@
 
 def wide_neighbours():
     return [ring_devices(axis, by) for axis in ("y", "z") for by in (1, 3)]
-
-
-def gather_wide_kernel(x_ref, out_ref, local_sem, send_sem, recv_sem):
-    copies = Copies(send_sem, recv_sem)
-    greet(wide_neighbours())
-    interleave(gather_wide_steps(x_ref, out_ref, local_sem, copies))
-    copies.sent()
-
-
-def gather_wide(x, collective_id):
-    return pl.pallas_call(
-        gather_wide_kernel,
-        out_shape=jax.ShapeDtypeStruct((SIDE, SIDE) + x.shape, x.dtype),
-        in_specs=[VM],
-        out_specs=VM,
-        scratch_shapes=[
-            pltpu.SemaphoreType.DMA,
-            pltpu.SemaphoreType.DMA((WIDE_COPIES,)),
-            pltpu.SemaphoreType.DMA((WIDE_COPIES,)),
-        ],
-        compiler_params=pltpu.CompilerParams(
-            collective_id=collective_id, has_side_effects=True, vmem_limit_bytes=VMEM_LIMIT
-        ),
-        name=f"gather_wide_{collective_id}",
-    )(x)
 
 
 def gather_narrow_steps(x_ref, out_ref, local_sem, copies):
@@ -275,31 +250,6 @@
     return [ring_devices("x", 1), ring_devices("x", 3), partner_device()]
 
 
-def gather_narrow_kernel(x_ref, out_ref, local_sem, send_sem, recv_sem):
-    copies = Copies(send_sem, recv_sem)
-    greet(narrow_neighbours())
-    interleave(gather_narrow_steps(x_ref, out_ref, local_sem, copies))
-    copies.sent()
-
-
-def gather_narrow(x, collective_id):
-    return pl.pallas_call(
-        gather_narrow_kernel,
-        out_shape=jax.ShapeDtypeStruct((8,) + x.shape, x.dtype),
-        in_specs=[VM],
-        out_specs=VM,
-        scratch_shapes=[
-            pltpu.SemaphoreType.DMA,
-            pltpu.SemaphoreType.DMA((NARROW_COPIES,)),
-            pltpu.SemaphoreType.DMA((NARROW_COPIES,)),
-        ],
-        compiler_params=pltpu.CompilerParams(
-            collective_id=collective_id, has_side_effects=True, vmem_limit_bytes=VMEM_LIMIT
-        ),
-        name=f"gather_narrow_{collective_id}",
-    )(x)
-
-
 def gather_both_kernel(x_ref, cache_ref, xo_ref, cacheo_ref, local_sem, send_n, recv_n, send_w, recv_w):
     near, far = Copies(send_n, recv_n), Copies(send_w, recv_w)
     greet(narrow_neighbours() + wide_neighbours())
@@ -334,14 +284,15 @@
     )(x, cache)
 
 
-def sum_narrow_kernel(p_ref, out_ref, mate, total, relay, direct, joined, send_sem, recv_sem):
-    copies = Copies(send_sem, recv_sem)
+SUM_COPIES = 10
+
+
+def sum_narrow_body(p_ref, acc, mate, total, relay, direct, joined, copies):
     n = lax.axis_index("narrow")
     x, core = lax.div(n, 2), lax.rem(n, 2)
     width = p_ref.shape[3] // 2
     lower, upper = pl.ds(0, width), pl.ds(width, width)
     right, left = ring_devices("x", 1), ring_devices("x", 3)
-    greet(narrow_neighbours())
     order = (2, 1, 3, 0)
     mates = {by: copies.slot() for by in order}
     slots = [copies.slot() for _ in range(6)]
@@ -365,40 +316,97 @@
     copies.arrived(slots[1], relay.at[1])
     total[3, :, upper] = (total[3, :, upper].astype(F32) + relay[1].astype(F32)).astype(BF)
     copies.start(slots[5], total.at[3, :, upper], joined.at[1], left)
-    out_ref[...] = pair(0)
+    acc[...] = pair(0)
     copies.arrived(slots[2], direct.at[0])
-    out_ref[:, upper] += direct[0].astype(F32)
+    acc[:, upper] += direct[0].astype(F32)
     copies.arrived(slots[3], direct.at[1])
-    out_ref[:, lower] += direct[1].astype(F32)
+    acc[:, lower] += direct[1].astype(F32)
     copies.arrived(slots[4], joined.at[0])
-    out_ref[:, lower] += joined[0].astype(F32)
+    acc[:, lower] += joined[0].astype(F32)
     copies.arrived(slots[5], joined.at[1])
-    out_ref[:, upper] += joined[1].astype(F32)
-    copies.sent()
-
-
-def sum_narrow(p, collective_id):
-    rows, cols = p.shape[2:]
+    acc[:, upper] += joined[1].astype(F32)
+
+
+def sum_scratch(rows, cols):
     piece = pltpu.VMEM((2, rows, cols // 2), BF)
+    dma = pltpu.SemaphoreType.DMA
+    return [
+        pltpu.VMEM((4, 2, rows, cols), BF),
+        pltpu.VMEM((rows, cols), F32),
+        pltpu.VMEM((4, rows, cols), BF),
+        pltpu.VMEM((4, rows, cols), BF),
+        piece,
+        piece,
+        piece,
+        dma((SUM_COPIES,)),
+        dma((SUM_COPIES,)),
+    ]
+
+
+def split_terms(terms):
+    return terms.astype(BF).reshape(4, 2, terms.shape[0] // 8, terms.shape[1])
+
+
+def out_proj_kernel(
+    own_ref, w_ref, x_ref, gain_ref, res_ref, out_ref, all_ref, block, terms, acc, mate, total, relay, direct, joined,
+    sum_send, sum_recv, local_sem, wide_send, wide_recv, near_send, near_recv,
+):
+    rows = x_ref.shape[0]
+    wide, sums, near = Copies(wide_send, wide_recv), Copies(sum_send, sum_recv), Copies(near_send, near_recv)
+    greet(wide_neighbours() + narrow_neighbours())
+    interleave(gather_wide_steps(own_ref, all_ref, local_sem.at[0], wide))
+    depth = w_ref.shape[1]
+    tokens = x_ref.shape[1] // SIDE
+    for group in range(SIDE):
+        values = all_ref[group].reshape(tokens, depth)
+        got = lax.dot_general(w_ref[...], values, (((1,), (1,)), ((), ())), preferred_element_type=F32)
+        terms[:, :, :, pl.ds(group * tokens, tokens)] = split_terms(got)
+    sum_narrow_body(terms, acc, mate, total, relay, direct, joined, sums)
+    residual = (x_ref[...].astype(F32) + acc[...]).astype(BF)
+    res_ref[...] = residual
+    widened = residual.astype(F32)
+    squares = jnp.sum(widened * widened, axis=0, keepdims=True)
+    high = squares.astype(BF).astype(F32)
+    rest = squares - high
+    middle = rest.astype(BF).astype(F32)
+    low = rest - middle
+    line = lax.broadcasted_iota(jnp.int32, (8, widened.shape[1]), 0)
+    tail = jnp.where(line == 0, high, jnp.where(line == 1, middle, jnp.where(line == 2, low, 0.0)))
+    block[...] = jnp.concatenate([widened * gain_ref[:, :1], tail], axis=0).astype(BF)
+    interleave(gather_narrow_steps(block, out_ref, local_sem.at[1], near))
+    wide.sent()
+    sums.sent()
+    near.sent()
+
+
+def out_proj(own, w, x, gain, collective_id):
+    rows, tokens = x.shape
+    dma = pltpu.SemaphoreType.DMA
     return pl.pallas_call(
-        sum_narrow_kernel,
-        out_shape=jax.ShapeDtypeStruct((rows, cols), F32),
-        in_specs=[VM],
-        out_specs=VM,
+        out_proj_kernel,
+        out_shape=(
+            jax.ShapeDtypeStruct((rows, tokens), BF),
+            jax.ShapeDtypeStruct((8, rows + 8, tokens), BF),
+        ),
+        in_specs=[VM] * 4,
+        out_specs=(VM, VM),
         scratch_shapes=[
-            pltpu.VMEM((4, rows, cols), BF),
-            pltpu.VMEM((4, rows, cols), BF),
-            piece,
-            piece,
-            piece,
-            pltpu.SemaphoreType.DMA((10,)),
-            pltpu.SemaphoreType.DMA((10,)),
+            pltpu.VMEM((SIDE, SIDE) + own.shape, BF),
+            pltpu.VMEM((rows + 8, tokens), BF),
+        ]
+        + sum_scratch(rows, tokens)
+        + [
+            dma((2,)),
+            dma((WIDE_COPIES,)),
+            dma((WIDE_COPIES,)),
+            dma((NARROW_COPIES,)),
+            dma((NARROW_COPIES,)),
         ],
         compiler_params=pltpu.CompilerParams(
             collective_id=collective_id, has_side_effects=True, vmem_limit_bytes=VMEM_LIMIT
         ),
-        name=f"sum_narrow_{collective_id}",
-    )(p)
+        name="out_proj",
+    )(own, w, x, jnp.broadcast_to(gain.astype(F32)[:, None], (rows, 128)))
 
 
 def matmul_sum_kernel(
@@ -588,8 +596,9 @@
 
 
 def gate_up_kernel(
-    x_ref, w_ref, sq_ref, out_ref, part, mid, hid, got1, got2, sq1, sqm, sq2, inv,
+    x_ref, w_ref, sq_ref, down_ref, res_ref, final_ref, out_ref, part, mid, hid, got1, got2, sq1, sqm, sq2, inv,
     send1, recv1, send2, recv2, send3, recv3, send4, recv4, own_sem, sq_send, sq_recv,
+    grown, terms, acc, mate, total, relay, direct, joined, sum_send, sum_recv,
 ):
     pieces, width = part.shape[0], part.shape[-1]
     units = out_ref.shape[-1]
@@ -598,7 +607,7 @@
     y, z = wide_place()
     names = (("y", "z"), ("z", "y"))
     spots = ((y, z), (z, y))
-    greet(wide_lines())
+    greet(wide_lines() + narrow_neighbours())
     squares = Copies(sq_send, sq_recv)
     for by in (1, 2, 3):
         squares.start(by - 1, sq_ref.at[turn(y, by)], sq1.at[by - 1], ring_devices("y", by))
@@ -784,6 +793,15 @@
                     copy3(piece, half, kind, way, ref, ref).wait_send()
                     for block in range(4):
                         copy4(piece, half, block, kind, way, ref, ref).wait_send()
+        columns = pl.ds(pl.multiple_of(piece * wide, 128), wide)
+        tokens = 2 * SIDE * rows
+        for group in range(SIDE):
+            values = out_ref[group, :, :, :, columns].reshape(tokens, wide)
+            got = lax.dot_general(
+                down_ref[:, columns], values, (((1,), (1,)), ((), ())), preferred_element_type=F32
+            )
+            spot = pl.ds(group * tokens, tokens)
+            grown[:, spot] += got
 
     stages = (stage1, stage2, stage3, stage4, stage5, stage6, stage7, stage8, stage9)
 
@@ -797,6 +815,7 @@
 
         return carry
 
+    grown[...] = jnp.zeros_like(grown)
     lax.fori_loop(0, 3, step, 0)
 
     for by in (1, 2, 3):
@@ -807,14 +826,19 @@
     lax.fori_loop(3, 4, step, 0)
     for by in (1, 2, 3):
         squares.arrived(2 + by, sq2.at[by - 1])
-    total = (sqm[z] + sq2[0] + sq2[1] + sq2[2])[:1]
-    factor = lax.rsqrt(total / D + epsilon)
+    everything = (sqm[z] + sq2[0] + sq2[1] + sq2[2])[:1]
+    factor = lax.rsqrt(everything / D + epsilon)
     token = lax.broadcasted_iota(jnp.int32, (2 * rows, 128), 0)
     lane = lax.broadcasted_iota(jnp.int32, (2 * rows, 128), 1)
     column = jnp.sum(jnp.where(token == lane, factor, 0.0), axis=1, keepdims=True)
     inv[...] = jnp.broadcast_to(column, (2 * rows, 128)).reshape(2, rows, 128)
     lax.fori_loop(4, pieces + len(stages) - 1, step, 0)
     squares.sent()
+    sums = Copies(sum_send, sum_recv)
+    terms[...] = split_terms(grown[...])
+    sum_narrow_body(terms, acc, mate, total, relay, direct, joined, sums)
+    final_ref[...] = (res_ref[...].astype(F32) + acc[...]).astype(BF)
+    sums.sent()
 
 
 def token_blocks(sq, rows):
@@ -822,7 +846,7 @@
     return jnp.broadcast_to(blocks, (SIDE, SIDE, 8, 128))
 
 
-def gate_up(x, w, sq, pieces, collective_id):
+def gate_up(x, w, sq, down, residual, pieces, collective_id):
     tokens, depth = x.shape
     units = w.shape[1] // 2
     width = 2 * units // pieces
@@ -830,10 +854,11 @@
     dma = pltpu.SemaphoreType.DMA
     return pl.pallas_call(
         gate_up_kernel,
-        out_shape=jax.ShapeDtypeStruct((SIDE, SIDE, 2, rows, units), BF),
-        in_specs=[VM, VM, VM],
+        out_shape=jax.ShapeDtypeStruct(residual.shape, BF),
+        in_specs=[VM] * 5,
         out_specs=VM,
         scratch_shapes=[
+            pltpu.VMEM((SIDE, SIDE, 2, rows, units), BF),
             pltpu.VMEM((pieces, 2, SIDE, SIDE, rows, width), BF),
             pltpu.VMEM((pieces, 2, SIDE, rows, width), BF),
             pltpu.VMEM((pieces, 2, rows, width // 2), BF),
@@ -854,12 +879,14 @@
             dma((pieces, 2)),
             dma((6,)),
             dma((6,)),
-        ],
+            pltpu.VMEM((down.shape[0], tokens), F32),
+        ]
+        + sum_scratch(*residual.shape),
         compiler_params=pltpu.CompilerParams(
             collective_id=collective_id, has_side_effects=True, vmem_limit_bytes=VMEM_LIMIT
         ),
         name="gate_up",
-    )(x.reshape(SIDE, SIDE, 2, rows, depth), w, token_blocks(sq, rows))
+    )(x.reshape(SIDE, SIDE, 2, rows, depth), w, token_blocks(sq, rows), down, residual)
 
 
 CHUNK = 2
@@ -1026,20 +1053,10 @@
     )
     attended = attended.reshape(R, GROUP, per_request, HDIM).transpose(2, 0, 1, 3).reshape(2, -1, GROUP * HDIM)
     softmax_sums = sums[:, :, 0].reshape(R, GROUP, per_request).transpose(2, 0, 1).reshape(per_device, GROUP)
-    attended_all = gather_wide(attended, 4).reshape(all_tokens, -1)
-    out_terms = lax.dot_general(
-        w_out, attended_all, (((0,), (1,)), ((), ())), preferred_element_type=F32
-    ).astype(BF)
-    summed = sum_narrow(out_terms.reshape(4, 2, features, all_tokens), 5)
-    residual = (flipped.astype(F32) + summed).astype(BF)
-    scaled, squares = unpack(gather_narrow(to_send(residual, mlp_gain), 6), features)
-    units = w_gate_up.shape[2]
-    hidden_all = gate_up(scaled, w_gate_up.reshape(w_gate_up.shape[0], -1), squares, 4, 7).reshape(all_tokens, units)
-    down_terms = lax.dot_general(
-        w_down, hidden_all, (((0,), (1,)), ((), ())), preferred_element_type=F32
-    ).astype(BF)
-    summed = sum_narrow(down_terms.reshape(4, 2, features, all_tokens), 9)
-    hidden_out = (residual.astype(F32) + summed).astype(BF).T
+    residual, gathered = out_proj(attended, w_out.T, flipped, mlp_gain, 5)
+    scaled, squares = unpack(gathered, features)
+    flat_gate_up = w_gate_up.reshape(w_gate_up.shape[0], -1)
+    hidden_out = gate_up(scaled, flat_gate_up, squares, w_down.T, residual, 4, 7).T
     return (hidden_out, softmax_sums, new_cache)
 
 

time: 276 us -> 255 us (0.924)
  matrix products: 9.62 us -> 0 us
  Pallas kernels: 233 us -> 226 us
  other arithmetic: 10.7 us -> 6.47 us
    dot_general x2 -> x0, matrix products: 9.62 us -> none  [the longest x1 6 us: local(): lax.dot_general(w_down, hidden_all, (((0,), (1,)), ((), ())), preferred_e...]
    pallas_call x5 -> x2, Pallas kernels: 160 us -> 153 us  [the longest x1 106 us: gate_up(): pl.pallas_call(gate_up_kernel, out_shape=jax.ShapeDtypeStruct(residual.sh...]
    unnamed x10 -> x13, local copies, waits for them, and re-layouts: 6.14 us -> 7.61 us
where the time goes in v4:
time: 255 us
  Pallas kernels  226 us (89%)
  local copies, waits for them, and re-layouts  21.8 us (9%)
  other arithmetic  6.47 us (3%)
    pallas_call x1, Pallas kernels, gate_up(): pl.pallas_call(gate_up_kernel, out_shape=jax.ShapeDtypeStruct(residual.sh...  106 us
    pallas_call x1, Pallas kernels, out_proj(): pl.pallas_call(out_proj_kernel, out_shape=(jax.ShapeDtypeStruct((rows, to...  47.3 us
    pallas_call x1, Pallas kernels, gather_both(): pl.pallas_call(gather_both_kernel, out_shape=(jax.ShapeDtypeStruct((8,) +...  33.8 us
    pallas_call x1, Pallas kernels, matmul_sum(): pl.pallas_call(matmul_sum_kernel, out_shape=(jax.ShapeDtypeStruct((2, row...  24.2 us
    pallas_call x1, Pallas kernels, attend(): pl.pallas_call(attend_kernel, out_shape=(jax.ShapeDtypeStruct(queries.sha...  14.6 us
    unnamed x13, local copies, waits for them, and re-layouts  7.61 us

profile of v4, /device:TPU:1, one launch (start us, length us, event | category | flops | bytes accessed | tf_op | source)
XLA Modules:
  0.0 254.7 jit_solution(3189532257632959653)
XLA Ops:
  0.6 0.7 convert_element_type.36
  1.3 1.0 fusion.1
  2.3 0.0 copy-start.1
  2.3 0.0 copy-start.3
  2.3 1.3 concatenate.14.x_ref
  3.6 1.8 reshape.210.cache_ref
  5.5 33.8 %gather_both.1 = (bf16[8,64,1024]{2,1,0:T(8,128)(2,1)}, bf16[4,4,2,256,256]{4,3,2,1,0:T(8,128)(2,1)}) custom-call(bf16[64,1024]{1,0:T(8,128)(2,1)} %concatenate.14.x_ref, bf16[2,256,256]{2,1,0:T(8,128)(2,1)} %reshape.210.cache_ref), custom_call_target="tpu_custom_call" | custom-call | tf_op jit(solution)/shard_map/gather_both/pallas_call | solution.py:265
  39.3 1.2 slice.36
  40.6 1.3 copy.27
  41.9 0.9 convert_reduce_fusion.1
  42.8 0.1 reshape.214
  42.9 0.6 broadcast_in_dim.62.sq_ref
  43.6 24.2 %matmul_sum_2.1 = (f32[2,32,1152]{2,1,0:T(8,128)}, f32[8,128]{1,0:T(8,128)}) custom-call(bf16[4,4,2,32,448]{4,3,2,1,0:T(8,128)(2,1)} %bitcast.47, bf16[448,1152]{1,0:T(8,128)(2,1)} %bitcast.52, f32[4,4,8,128]{3,2,1,0:T(8,128)} %broadcast_in_dim.62.sq_ref), custom_call_target="tpu_custom_call" | custom-call | tf_op jit(solution)/shard_map/matmul_sum_2/pallas_call | solution.py:567
  67.7 0.0 copy-start.2
  67.8 0.7 broadcast_compare_fusion
  68.4 1.0 reshape.215
  69.5 0.2 multiply_select_fusion
  69.7 0.0 copy-done.1
  69.7 0.0 copy-done.3
  69.7 0.1 fusion.3
  69.8 0.2 multiply_cosine_fusion
  70.0 0.2 subtract_convert_fusion
  70.2 0.1 pad_maximum_fusion
  70.4 0.7 maximum_bitcast_fusion.1
  71.1 0.6 maximum_bitcast_fusion.own_ref
  71.7 0.1 slice_maximum_fusion
  71.8 0.7 copy.28
  72.5 14.6 %attend.1 = (bf16[2,224,128]{2,1,0:T(8,128)(2,1)}, f32[2,224,128]{2,1,0:T(8,128)}) custom-call(s32[2]{0:T(128)} %lengths_ref.1, bf16[2,224,128]{2,1,0:T(8,128)(2,1)} %bitcast.58, bf16[16,2,256,256]{3,2,1,0:T(8,128)(2,1)} %bitcast.46, bf16[2,32,256]{2,1,0:T(8,128)(2,1)} %maximum_bitcast_fusion.own_ref), custom_call_target="tpu_custom_call" | custom-call | tf_op jit(solution)/shard_map/attend/pallas_call | solution.py:957
  87.2 1.0 copy.40
  88.1 0.8 reshape.220.own_ref
  88.9 0.0 copy-done.2
  88.9 0.7 broadcast_in_dim.67.gain_ref
  89.6 47.3 %out_proj.1 = (bf16[56,1024]{1,0:T(8,128)(2,1)}, bf16[8,64,1024]{2,1,0:T(8,128)(2,1)}) custom-call(bf16[2,32,896]{2,1,0:T(8,128)(2,1)} %reshape.220.own_ref, bf16[448,896]{1,0:T(8,128)(2,1)} %bitcast.53, bf16[56,1024]{1,0:T(8,128)(2,1)} %bitcast.57, f32[56,128]{1,0:T(8,128)} %broadcast_in_dim.67.gain_ref), custom_call_target="tpu_custom_call" | custom-call | tf_op jit(solution)/shard_map/out_proj/pallas_call | solution.py:385
  136.9 1.2 slice.44
  138.1 1.3 copy.32
  139.4 0.9 convert_reduce_fusion
  140.4 0.1 reshape.224
  140.5 0.6 broadcast_in_dim.69.sq_ref
  141.1 5.3 %copy.38 = bf16[56,8,2,2560]{3,1,2,0:T(8,128)(2,1)} copy(bf16[56,8,2,2560]{3,2,1,0:T(2,128)(2,1)} %bitcast.45) | data formatting | bytes 9175040
  146.5 0.0 copy-start
  146.5 105.6 %gate_up.1 = bf16[56,1024]{1,0:T(8,128)(2,1)} custom-call(bf16[4,4,2,32,448]{4,3,2,1,0:T(8,128)(2,1)} %bitcast.48, bf16[448,5120]{1,0:T(8,128)(2,1)} %bitcast.44, f32[4,4,8,128]{3,2,1,0:T(8,128)} %broadcast_in_dim.69.sq_ref, bf16[448,2560]{1,0:T(8,128)(2,1)} %bitcast.51, bf16[56,1024]{1,0:T(8,128)(2,1)} %get-tuple-element.17.res_ref), custom_call_target="tpu_custom_call" | custom-call | tf_op jit(solution)/shard_map/gate_up/pallas_call | solution.py:855
  252.1 0.0 copy-done
  252.1 0.1 slice_reduce_fusion
  252.2 0.1 reshape_squeeze.3
  252.3 0.1 copy.33
  252.4 0.7 copy.34
  253.1 1.6 copy.42
  (13 shorter events, 0.1 us)
Async XLA Ops:
  2.3 67.4 %copy-start.1 = (s32[2]{0:T(128)S(1)}, s32[2]{0:T(128)}, u32[]{:S(2)}) copy-start(s32[2]{0:T(128)} %lengths_ref.1) | copy-start | bytes 28
  2.3 67.4 %copy-start.3 = (s32[2]{0:T(128)S(1)}, s32[2]{0:T(128)}, u32[]{:S(2)}) copy-start(s32[2]{0:T(128)} %param.15) | copy-start | bytes 28
  67.7 21.2 %copy-start.2 = (bf16[56]{0:T(256)(128)(2,1)S(1)}, bf16[56]{0:T(256)(128)(2,1)}, u32[]{:S(2)}) copy-start(bf16[56]{0:T(256)(128)(2,1)} %param.17) | copy-start | bytes 340
  146.5 105.6 %copy-start = (f32[2,224,128]{2,1,0:T(8,128)S(1)}, f32[2,224,128]{2,1,0:T(8,128)}, u32[]{:S(2)}) copy-start(f32[2,224,128]{2,1,0:T(8,128)} %get-tuple-element.18) | copy-start | bytes 688132

commit v5 on v4

--- a/solution.py
+++ b/solution.py
@@ -20,6 +20,7 @@
 MESH = pl.DeviceIdType.MESH
 BF = jnp.bfloat16
 F32 = jnp.float32
+ANY = pl.BlockSpec(memory_space=pl.ANY)
 VM = pl.BlockSpec(memory_space=pltpu.VMEM)
 SM = pl.BlockSpec(memory_space=pltpu.SMEM)
 VMEM_LIMIT = 60 * 1024 * 1024
@@ -250,38 +251,105 @@
     return [ring_devices("x", 1), ring_devices("x", 3), partner_device()]
 
 
-def gather_both_kernel(x_ref, cache_ref, xo_ref, cacheo_ref, local_sem, send_n, recv_n, send_w, recv_w):
+def unpack_steps(got_ref, x_ref, sq_ref):
+    rows = x_ref.shape[1] // 8
+    tokens = x_ref.shape[0]
+    width = tokens // SIDE
+    sums = jnp.zeros((8, tokens), F32)
+    for device in range(8):
+        sums = sums + got_ref[device].astype(F32)[rows:]
+    squares = jnp.broadcast_to(jnp.sum(sums, axis=0, keepdims=True), (8, tokens))
+    for pair in range(tokens // 128):
+        block = squares[:, pair * 128 : pair * 128 + 128]
+        y, z = divmod(2 * pair, SIDE)
+        sq_ref[y, z] = block
+        sq_ref[y, z + 1] = pltpu.roll(block, 64, 1)
+    yield
+    for group in range(SIDE):
+        spot = pl.ds(group * width, width)
+        turned = jnp.concatenate([got_ref[device, :, spot].astype(F32)[:rows] for device in range(8)], axis=0)
+        x_ref[spot, :] = turned.T.astype(BF)
+        yield
+
+
+def flatten_steps(w_ref, out_ref, paired, flat, sem):
+    came = pltpu.make_async_copy(w_ref, paired, sem.at[0])
+    came.start()
+    yield
+    yield
+    came.wait()
+    for start in range(0, w_ref.shape[0], 64):
+
+        def some(index, carry):
+            spot = pl.ds(pl.multiple_of(start + index * 16, 16), 16)
+            flat[0, spot] = paired[spot, 0, :]
+            flat[1, spot] = paired[spot, 1, :]
+            return carry
+
+        lax.fori_loop(0, 4, some, 0)
+        yield
+    went = pltpu.make_async_copy(flat, out_ref, sem.at[1])
+    went.start()
+    yield
+    went.wait()
+
+
+def gather_both_kernel(
+    x_ref, cache_ref, w_ref, xo_ref, sqo_ref, cacheo_ref, wo_ref,
+    got, own, paired, flat, local_sem, flat_sem, send_n, recv_n, send_w, recv_w,
+):
     near, far = Copies(send_n, recv_n), Copies(send_w, recv_w)
+    for half in range(2):
+        own[half, :, :HDIM] = cache_ref[half, :, 0, :]
+        own[half, :, HDIM:] = cache_ref[half, :, 1, :]
     greet(narrow_neighbours() + wide_neighbours())
+
+    def features():
+        yield from gather_narrow_steps(x_ref, got, local_sem.at[0], near)
+        yield from unpack_steps(got, xo_ref, sqo_ref)
+
     interleave(
-        gather_narrow_steps(x_ref, xo_ref, local_sem.at[0], near),
-        gather_wide_steps(cache_ref, cacheo_ref, local_sem.at[1], far),
+        features(),
+        gather_wide_steps(own, cacheo_ref, local_sem.at[1], far),
+        flatten_steps(w_ref, wo_ref, paired, flat, flat_sem),
     )
     near.sent()
     far.sent()
 
 
-def gather_both(x, cache, collective_id):
+def gather_both(x, cache, w, collective_id):
+    rows, tokens = x.shape
+    rows -= 8
+    dma = pltpu.SemaphoreType.DMA
+    flat = (w.shape[1], w.shape[0], w.shape[2])
+    block = cache.shape[:2] + (2 * HDIM,)
     return pl.pallas_call(
         gather_both_kernel,
         out_shape=(
-            jax.ShapeDtypeStruct((8,) + x.shape, x.dtype),
-            jax.ShapeDtypeStruct((SIDE, SIDE) + cache.shape, cache.dtype),
+            jax.ShapeDtypeStruct((tokens, 8 * rows), BF),
+            jax.ShapeDtypeStruct((SIDE, SIDE, 8, 128), F32),
+            jax.ShapeDtypeStruct((SIDE, SIDE) + block, BF),
+            jax.ShapeDtypeStruct(flat, BF),
         ),
-        in_specs=[VM, VM],
-        out_specs=(VM, VM),
+        in_specs=[VM, VM, ANY],
+        out_specs=(VM, VM, VM, ANY),
         scratch_shapes=[
-            pltpu.SemaphoreType.DMA((2,)),
-            pltpu.SemaphoreType.DMA((NARROW_COPIES,)),
-            pltpu.SemaphoreType.DMA((NARROW_COPIES,)),
-            pltpu.SemaphoreType.DMA((WIDE_COPIES,)),
-            pltpu.SemaphoreType.DMA((WIDE_COPIES,)),
+            pltpu.VMEM((8, rows + 8, tokens), BF),
+            pltpu.VMEM(block, BF),
+            pltpu.VMEM(w.shape, BF),
+            pltpu.VMEM(flat, BF),
+            dma((2,)),
+            dma((2,)),
+            dma((NARROW_COPIES,)),
+            dma((NARROW_COPIES,)),
+            dma((WIDE_COPIES,)),
+            dma((WIDE_COPIES,)),
         ],
         compiler_params=pltpu.CompilerParams(
             collective_id=collective_id, has_side_effects=True, vmem_limit_bytes=VMEM_LIMIT
         ),
         name="gather_both",
-    )(x, cache)
+    )(x, cache, w)
 
 
 SUM_COPIES = 10
@@ -348,7 +416,7 @@
 
 
 def out_proj_kernel(
-    own_ref, w_ref, x_ref, gain_ref, res_ref, out_ref, all_ref, block, terms, acc, mate, total, relay, direct, joined,
+    own_ref, w_ref, x_ref, gain_ref, res_ref, xo_ref, sqo_ref, got, all_ref, block, terms, acc, mate, total, relay, direct, joined,
     sum_send, sum_recv, local_sem, wide_send, wide_recv, near_send, near_recv,
 ):
     rows = x_ref.shape[0]
@@ -359,8 +427,8 @@
     tokens = x_ref.shape[1] // SIDE
     for group in range(SIDE):
         values = all_ref[group].reshape(tokens, depth)
-        got = lax.dot_general(w_ref[...], values, (((1,), (1,)), ((), ())), preferred_element_type=F32)
-        terms[:, :, :, pl.ds(group * tokens, tokens)] = split_terms(got)
+        term = lax.dot_general(w_ref[...], values, (((1,), (1,)), ((), ())), preferred_element_type=F32)
+        terms[:, :, :, pl.ds(group * tokens, tokens)] = split_terms(term)
     sum_narrow_body(terms, acc, mate, total, relay, direct, joined, sums)
     residual = (x_ref[...].astype(F32) + acc[...]).astype(BF)
     res_ref[...] = residual
@@ -373,7 +441,8 @@
     line = lax.broadcasted_iota(jnp.int32, (8, widened.shape[1]), 0)
     tail = jnp.where(line == 0, high, jnp.where(line == 1, middle, jnp.where(line == 2, low, 0.0)))
     block[...] = jnp.concatenate([widened * gain_ref[:, :1], tail], axis=0).astype(BF)
-    interleave(gather_narrow_steps(block, out_ref, local_sem.at[1], near))
+    interleave(gather_narrow_steps(block, got, local_sem.at[1], near))
+    interleave(unpack_steps(got, xo_ref, sqo_ref))
     wide.sent()
     sums.sent()
     near.sent()
@@ -386,11 +455,13 @@
         out_proj_kernel,
         out_shape=(
             jax.ShapeDtypeStruct((rows, tokens), BF),
-            jax.ShapeDtypeStruct((8, rows + 8, tokens), BF),
+            jax.ShapeDtypeStruct((tokens, 8 * rows), BF),
+            jax.ShapeDtypeStruct((SIDE, SIDE, 8, 128), F32),
         ),
         in_specs=[VM] * 4,
-        out_specs=(VM, VM),
+        out_specs=(VM, VM, VM),
         scratch_shapes=[
+            pltpu.VMEM((8, rows + 8, tokens), BF),
             pltpu.VMEM((SIDE, SIDE) + own.shape, BF),
             pltpu.VMEM((rows + 8, tokens), BF),
         ]
@@ -562,8 +633,6 @@
     cols = w.shape[1]
     width = cols // pieces
     rows = tokens // (2 * SIDE * SIDE)
-    blocks = jnp.pad(sq.reshape(SIDE, SIDE, 1, 2 * rows), ((0, 0), (0, 0), (0, 0), (0, 128 - 2 * rows)))
-    blocks = jnp.broadcast_to(blocks, (SIDE, SIDE, 8, 128))
     out, sq_out = pl.pallas_call(
         matmul_sum_kernel,
         out_shape=(
@@ -591,7 +660,7 @@
             collective_id=collective_id, has_side_effects=True, vmem_limit_bytes=VMEM_LIMIT
         ),
         name=f"matmul_sum_{collective_id}",
-    )(x.reshape(SIDE, SIDE, 2, rows, depth), w, blocks)
+    )(x.reshape(SIDE, SIDE, 2, rows, depth), w, sq)
     return out.reshape(2 * rows, cols), sq_out[0, : 2 * rows]
 
 
@@ -601,7 +670,6 @@
     grown, terms, acc, mate, total, relay, direct, joined, sum_send, sum_recv,
 ):
     pieces, width = part.shape[0], part.shape[-1]
-    units = out_ref.shape[-1]
     wide = width // 2
     rows = x_ref.shape[3]
     y, z = wide_place()
@@ -619,8 +687,8 @@
         block = x_ref[chunk, :, 0] if half == 0 else x_ref[:, chunk, 1]
         block = block.reshape(SIDE * rows, block.shape[-1])
         at = pl.multiple_of(piece * wide, 128)
-        gate = jnp.dot(block, w_ref[:, pl.ds(at, wide)], preferred_element_type=F32)
-        up = jnp.dot(block, w_ref[:, pl.ds(pl.multiple_of(units + at, 128), wide)], preferred_element_type=F32)
+        gate = jnp.dot(block, w_ref[0, :, pl.ds(at, wide)], preferred_element_type=F32)
+        up = jnp.dot(block, w_ref[1, :, pl.ds(at, wide)], preferred_element_type=F32)
         return jnp.concatenate([gate, up], axis=1).reshape(SIDE, rows, width)
 
     def remote(src, dst, send, recv, axis, way):
@@ -841,14 +909,9 @@
     sums.sent()
 
 
-def token_blocks(sq, rows):
-    blocks = jnp.pad(sq.reshape(SIDE, SIDE, 1, 2 * rows), ((0, 0), (0, 0), (0, 0), (0, 128 - 2 * rows)))
-    return jnp.broadcast_to(blocks, (SIDE, SIDE, 8, 128))
-
-
 def gate_up(x, w, sq, down, residual, pieces, collective_id):
     tokens, depth = x.shape
-    units = w.shape[1] // 2
+    units = w.shape[2]
     width = 2 * units // pieces
     rows = tokens // (2 * SIDE * SIDE)
     dma = pltpu.SemaphoreType.DMA
@@ -886,10 +949,10 @@
             collective_id=collective_id, has_side_effects=True, vmem_limit_bytes=VMEM_LIMIT
         ),
         name="gate_up",
-    )(x.reshape(SIDE, SIDE, 2, rows, depth), w, token_blocks(sq, rows), down, residual)
-
-
-CHUNK = 2
+    )(x.reshape(SIDE, SIDE, 2, rows, depth), w, sq, down, residual)
+
+
+CHUNK = 8
 
 
 def attend_kernel(
@@ -1013,12 +1076,6 @@
     return jnp.concatenate([scaled, high, middle, low, pad], axis=0).astype(BF)
 
 
-def unpack(gathered, rows):
-    scaled = gathered[:, :rows].reshape(8 * rows, -1).T
-    squares = jnp.sum(gathered[:, rows : rows + 3].astype(F32), axis=(0, 1))
-    return scaled, squares
-
-
 def rescale(sums, squares):
     inv_scale = lax.rsqrt(squares / D + epsilon)[:, None]
     return jnp.where(inv_scale > 0, sums * inv_scale, 0.0)
@@ -1032,10 +1089,9 @@
     first_token = lax.axis_index("wide") * per_device
     flipped = hidden_in.T
     positions = cache_kv.shape[1]
-    cache = cache_kv.reshape(R, positions, 2 * HDIM)
-    gathered, cache_all = gather_both(to_send(flipped, attn_gain), cache, 1)
-    scaled, squares = unpack(gathered, features)
-    projected, squares = matmul_sum(scaled, w_qkv.reshape(w_qkv.shape[0], -1), squares, 3, 2)
+    cache = cache_kv.reshape(R, positions, 2, HDIM)
+    scaled, squares, cache_all, flat_gate_up = gather_both(to_send(flipped, attn_gain), cache, w_gate_up, 1)
+    projected, squares = matmul_sum(scaled, w_qkv.reshape(w_qkv.shape[0], -1), squares, 1, 2)
     projected = rescale(projected, squares).reshape(per_device, GROUP + 2, HDIM)
     angles = token_angles(lengths, offsets, first_token, per_device, HDIM)
     rotated = rotate(projected[:, : GROUP + 1], angles).astype(BF)
@@ -1053,10 +1109,8 @@
     )
     attended = attended.reshape(R, GROUP, per_request, HDIM).transpose(2, 0, 1, 3).reshape(2, -1, GROUP * HDIM)
     softmax_sums = sums[:, :, 0].reshape(R, GROUP, per_request).transpose(2, 0, 1).reshape(per_device, GROUP)
-    residual, gathered = out_proj(attended, w_out.T, flipped, mlp_gain, 5)
-    scaled, squares = unpack(gathered, features)
-    flat_gate_up = w_gate_up.reshape(w_gate_up.shape[0], -1)
-    hidden_out = gate_up(scaled, flat_gate_up, squares, w_down.T, residual, 4, 7).T
+    residual, scaled, squares = out_proj(attended, w_out.T, flipped, mlp_gain, 5)
+    hidden_out = gate_up(scaled, flat_gate_up, squares, w_down.T, residual, 2, 7).T
     return (hidden_out, softmax_sums, new_cache)
 
 

time: 255 us -> 238 us (0.933)
  local copies, waits for them, and re-layouts: 21.8 us -> 8.03 us
    unnamed x13 -> x12, local copies, waits for them, and re-layouts: 7.61 us -> 2.26 us
    reshape x5 -> x0, local copies, waits for them, and re-layouts: 4.6 us -> none  [the longest x2 2.62 us: unpack(): scaled = gathered[:, :rows].reshape(8 * rows, -1).T]
    pallas_call x1, Pallas kernels: 33.8 us -> 37.2 us  [gather_both(): pl.pallas_call(gather_both_kernel, out_shape=(jax.ShapeDtypeStruct((token...]
where the time goes in v5:
time: 238 us
  Pallas kernels  224 us (94%)
  local copies, waits for them, and re-layouts  8.03 us (3%)
  other arithmetic  4.58 us (2%)
    pallas_call x1, Pallas kernels, gate_up(): pl.pallas_call(gate_up_kernel, out_shape=jax.ShapeDtypeStruct(residual.sh...  104 us
    pallas_call x1, Pallas kernels, out_proj(): pl.pallas_call(out_proj_kernel, out_shape=(jax.ShapeDtypeStruct((rows, to...  46.7 us
    pallas_call x1, Pallas kernels, gather_both(): pl.pallas_call(gather_both_kernel, out_shape=(jax.ShapeDtypeStruct((token...  37.2 us
    pallas_call x1, Pallas kernels, matmul_sum(): pl.pallas_call(matmul_sum_kernel, out_shape=(jax.ShapeDtypeStruct((2, row...  23.4 us
    pallas_call x1, Pallas kernels, attend(): pl.pallas_call(attend_kernel, out_shape=(jax.ShapeDtypeStruct(queries.sha...  13 us

profile of v5, /device:TPU:1, one launch (start us, length us, event | category | flops | bytes accessed | tf_op | source)
XLA Modules:
  0.0 237.7 jit_solution(6775524183197710616)
XLA Ops:
  0.6 0.7 convert_element_type.27
  1.3 1.0 fusion.1
  2.3 0.0 copy-start.1
  2.3 0.0 copy-start.3
  2.3 1.3 concatenate.14.x_ref
  3.6 37.2 %gather_both.1 = (bf16[1024,448]{1,0:T(8,128)(2,1)}, f32[4,4,8,128]{3,2,1,0:T(8,128)}, bf16[4,4,2,256,256]{4,3,2,1,0:T(8,128)(2,1)}, bf16[2,448,2560]{2,1,0:T(8,128)(2,1)}) custom-call(bf16[64,1024]{1,0:T(8,128)(2,1)} %concatenate.14.x_ref, bf16[2,256,2,128]{3,2,1,0:T(2,128)(2,1)} %bitcast.44, bf16[448,2,2560]{2,1,0:T(2,128)(2,1)} %w_ref.1), custom_call_target="tpu_custom_call" | custom-call | tf_op jit(solution)/shard_map/gather_both/pallas_call | solution.py:326
  40.8 23.4 %matmul_sum_2.1 = (f32[2,32,1152]{2,1,0:T(8,128)}, f32[8,128]{1,0:T(8,128)}) custom-call(bf16[4,4,2,32,448]{4,3,2,1,0:T(8,128)(2,1)} %bitcast.35, bf16[448,1152]{1,0:T(8,128)(2,1)} %bitcast.37, f32[4,4,8,128]{3,2,1,0:T(8,128)} %get-tuple-element.15.sq_ref), custom_call_target="tpu_custom_call" | custom-call | tf_op jit(solution)/shard_map/matmul_sum_2/pallas_call | solution.py:636
  64.2 0.0 copy-start.2
  64.2 0.7 broadcast_compare_fusion
  64.9 1.0 reshape.198
  65.9 0.2 multiply_select_fusion
  66.1 0.0 copy-done.1
  66.2 0.0 copy-done.3
  66.2 0.1 fusion.3
  66.3 0.2 multiply_cosine_fusion
  66.5 0.2 subtract_convert_fusion
  66.7 0.1 pad_maximum_fusion
  66.8 0.7 maximum_bitcast_fusion.1
  67.6 0.6 maximum_bitcast_fusion.own_ref
  68.2 0.1 slice_maximum_fusion
  68.3 0.7 copy.23
  69.0 13.0 %attend.1 = (bf16[2,224,128]{2,1,0:T(8,128)(2,1)}, f32[2,224,128]{2,1,0:T(8,128)}) custom-call(s32[2]{0:T(128)} %lengths_ref.1, bf16[2,224,128]{2,1,0:T(8,128)(2,1)} %bitcast.43, bf16[16,2,256,256]{3,2,1,0:T(8,128)(2,1)} %bitcast.33, bf16[2,32,256]{2,1,0:T(8,128)(2,1)} %maximum_bitcast_fusion.own_ref), custom_call_target="tpu_custom_call" | custom-call | tf_op jit(solution)/shard_map/attend/pallas_call | solution.py:1020
  82.0 1.0 copy.33
  82.9 0.8 reshape.203.own_ref
  83.7 0.0 copy-done.2
  83.7 0.7 broadcast_in_dim.51.gain_ref
  84.4 0.0 copy-start
  84.4 46.7 %out_proj.1 = (bf16[56,1024]{1,0:T(8,128)(2,1)}, bf16[1024,448]{1,0:T(8,128)(2,1)}, f32[4,4,8,128]{3,2,1,0:T(8,128)}) custom-call(bf16[2,32,896]{2,1,0:T(8,128)(2,1)} %reshape.203.own_ref, bf16[448,896]{1,0:T(8,128)(2,1)} %bitcast.38, bf16[56,1024]{1,0:T(8,128)(2,1)} %bitcast.42, f32[56,128]{1,0:T(8,128)} %broadcast_in_dim.51.gain_ref), custom_call_target="tpu_custom_call" | custom-call | tf_op jit(solution)/shard_map/out_proj/pallas_call | solution.py:454
  131.2 104.0 %gate_up.1 = bf16[56,1024]{1,0:T(8,128)(2,1)} custom-call(bf16[4,4,2,32,448]{4,3,2,1,0:T(8,128)(2,1)} %bitcast.36, bf16[2,448,2560]{2,1,0:T(8,128)(2,1)} %get-tuple-element.21.w_ref, f32[4,4,8,128]{3,2,1,0:T(8,128)} %get-tuple-element.22.sq_ref, bf16[448,2560]{1,0:T(8,128)(2,1)} %bitcast.34, bf16[56,1024]{1,0:T(8,128)(2,1)} %get-tuple-element.23.res_ref), custom_call_target="tpu_custom_call" | custom-call | tf_op jit(solution)/shard_map/gate_up/pallas_call | solution.py:918
  235.1 0.0 copy-done
  235.1 0.1 slice_reduce_fusion
  235.3 0.1 reshape_squeeze.3
  235.4 0.1 copy.27
  235.5 0.7 copy.28
  236.1 1.6 copy.35
  (11 shorter events, 0.1 us)
Async XLA Ops:
  2.3 63.8 %copy-start.1 = (s32[2]{0:T(128)S(1)}, s32[2]{0:T(128)}, u32[]{:S(2)}) copy-start(s32[2]{0:T(128)} %lengths_ref.1) | copy-start | bytes 28
  2.3 63.8 %copy-start.3 = (s32[2]{0:T(128)S(1)}, s32[2]{0:T(128)}, u32[]{:S(2)}) copy-start(s32[2]{0:T(128)} %param.15) | copy-start | bytes 28
  64.2 19.5 %copy-start.2 = (bf16[56]{0:T(256)(128)(2,1)S(1)}, bf16[56]{0:T(256)(128)(2,1)}, u32[]{:S(2)}) copy-start(bf16[56]{0:T(256)(128)(2,1)} %param.17) | copy-start | bytes 340
  84.4 150.7 %copy-start = (f32[2,224,128]{2,1,0:T(8,128)S(1)}, f32[2,224,128]{2,1,0:T(8,128)}, u32[]{:S(2)}) copy-start(f32[2,224,128]{2,1,0:T(8,128)} %get-tuple-element.24) | copy-start | bytes 688132

commit v6 on v5

--- a/solution.py
+++ b/solution.py
@@ -661,7 +661,7 @@
         ),
         name=f"matmul_sum_{collective_id}",
     )(x.reshape(SIDE, SIDE, 2, rows, depth), w, sq)
-    return out.reshape(2 * rows, cols), sq_out[0, : 2 * rows]
+    return out, sq_out
 
 
 def gate_up_kernel(
@@ -956,17 +956,42 @@
 
 
 def attend_kernel(
-    lengths_ref, q_ref, cache_ref, own_ref, out_ref, sums_ref, span_ref, local_sem, send_sem, recv_sem
+    lengths_ref, sums_in_ref, sq_ref, cos_ref, sin_ref, cache_ref, out_ref, sums_ref, fresh_ref,
+    lines, q_ref, own_ref, rows_out, rows_sum, span_ref, local_sem, send_sem, recv_sem,
 ):
     scale = HDIM ** (-0.5)
     rows = q_ref.shape[1]
     per = own_ref.shape[1]
+    tokens = R * per
+    factor = lax.rsqrt(sq_ref[:1] / D + epsilon)
+    token = lax.broadcasted_iota(jnp.int32, (tokens, 128), 0)
+    lane = lax.broadcasted_iota(jnp.int32, (tokens, 128), 1)
+    column = jnp.sum(jnp.where(token == lane, factor, 0.0), axis=1, keepdims=True)
+
+    def slot_of(index, turned):
+        got = sums_in_ref[:, :, index * HDIM : index * HDIM + HDIM].reshape(tokens, HDIM)
+        got = jnp.where(column > 0, got * column, 0.0)
+        if turned:
+            got = got * cos_ref[...] + pltpu.roll(got, HDIM // 2, 1) * sin_ref[...]
+        lines[index] = got
+        return got.astype(BF)
+
+    fresh_ref[:, :HDIM] = slot_of(GROUP, True)
+    fresh_ref[:, HDIM:] = slot_of(GROUP + 1, False)
+    for request in range(R):
+        mine = pl.ds(request, per, stride=R)
+        own_ref[request, :, :HDIM] = lines[GROUP, mine, :].astype(BF)
+        own_ref[request, :, HDIM:] = lines[GROUP + 1, mine, :].astype(BF)
     block = cache_ref.shape[2] * CHUNK
     spot = lax.axis_index("wide")
     copies = Copies(send_sem, recv_sem)
     greet(wide_lines())
     gather = gather_direct_steps(own_ref, span_ref, local_sem, copies)
     next(gather)
+    for index in range(GROUP):
+        slot_of(index, True)
+        for request in range(R):
+            q_ref[request, index * per : index * per + per] = lines[index, pl.ds(request, per, stride=R), :].astype(BF)
     queries = [q_ref[request] for request in range(R)]
 
     def absorb(running, q, keys, values, allowed):
@@ -1011,31 +1036,50 @@
         peak, weight_sum, gathered = absorb(
             running[request], queries[request], span[:, :HDIM], span[:, HDIM:], own_keys
         )
-        out_ref[request] = (gathered / weight_sum).astype(BF)
-        sums_ref[request] = jnp.broadcast_to(peak + jnp.log(weight_sum), (rows, HDIM))
+        gathered = gathered / weight_sum
+        logs = peak + jnp.log(weight_sum)
+        mine = pl.ds(request, per, stride=R)
+        line = jnp.zeros((per, 128), F32)
+        spot_of = lax.broadcasted_iota(jnp.int32, (per, 128), 1)
+        for index in range(GROUP):
+            rows_out[index, mine, :] = gathered[index * per : index * per + per]
+            line = line + jnp.where(spot_of == index, logs[index * per : index * per + per], 0.0)
+        rows_sum[mine, :] = line
+    for index in range(GROUP):
+        out_ref[:, :, index * HDIM : index * HDIM + HDIM] = rows_out[index].astype(BF).reshape(2, per, HDIM)
+    sums_ref[...] = rows_sum[...]
     copies.sent()
 
 
-def attend(lengths, queries, cache, own, collective_id):
+def attend(lengths, sums, sq, cosine, sine, cache, collective_id):
+    per = sums.shape[1]
+    tokens = R * per
+    dma = pltpu.SemaphoreType.DMA
     return pl.pallas_call(
         attend_kernel,
         out_shape=(
-            jax.ShapeDtypeStruct(queries.shape, BF),
-            jax.ShapeDtypeStruct(queries.shape, F32),
+            jax.ShapeDtypeStruct((2, per, GROUP * HDIM), BF),
+            jax.ShapeDtypeStruct((tokens, 128), F32),
+            jax.ShapeDtypeStruct((tokens, 2 * HDIM), BF),
         ),
-        in_specs=[SM, VM, VM, VM],
-        out_specs=(VM, VM),
+        in_specs=[SM] + [VM] * 5,
+        out_specs=(VM, VM, VM),
         scratch_shapes=[
-            pltpu.VMEM((SIDE, SIDE) + own.shape, BF),
-            pltpu.SemaphoreType.DMA,
-            pltpu.SemaphoreType.DMA((DIRECT_COPIES,)),
-            pltpu.SemaphoreType.DMA((DIRECT_COPIES,)),
+            pltpu.VMEM((GROUP + 2, tokens, HDIM), F32),
+            pltpu.VMEM((R, GROUP * per, HDIM), BF),
+            pltpu.VMEM((R, per, 2 * HDIM), BF),
+            pltpu.VMEM((GROUP, tokens, HDIM), F32),
+            pltpu.VMEM((tokens, 128), F32),
+            pltpu.VMEM((SIDE, SIDE, R, per, 2 * HDIM), BF),
+            dma,
+            dma((DIRECT_COPIES,)),
+            dma((DIRECT_COPIES,)),
         ],
         compiler_params=pltpu.CompilerParams(
             collective_id=collective_id, has_side_effects=True, vmem_limit_bytes=VMEM_LIMIT
         ),
         name="attend",
-    )(lengths, queries, cache, own)
+    )(lengths, sums, sq, cosine, sine, cache)
 
 
 def token_angles(lengths, offsets, first_token, row_count, dim_size):
@@ -1047,21 +1091,6 @@
     position = (chosen + token_ids // R).astype(jnp.float32)
     inverse = rope_base ** (-(jnp.arange(dim_size // 2, dtype=jnp.float32) * 2.0) / dim_size)
     return position[:, None] * inverse[None, :]
-
-
-def rotate(values, angles):
-    half_dim = values.shape[-1] // 2
-    first_half = values[..., :half_dim]
-    second_half = values[..., half_dim:]
-    cosine = jnp.cos(angles)[:, None, :]
-    sine_part = jnp.sin(angles)[:, None, :]
-    return jnp.concatenate(
-        [
-            first_half * cosine - second_half * sine_part,
-            second_half * cosine + first_half * sine_part,
-        ],
-        axis=-1,
-    )
 
 
 def to_send(flipped, gain):
@@ -1074,11 +1103,6 @@
     scaled = widened * gain.astype(F32)[:, None]
     pad = jnp.zeros((5, flipped.shape[1]), F32)
     return jnp.concatenate([scaled, high, middle, low, pad], axis=0).astype(BF)
-
-
-def rescale(sums, squares):
-    inv_scale = lax.rsqrt(squares / D + epsilon)[:, None]
-    return jnp.where(inv_scale > 0, sums * inv_scale, 0.0)
 
 
 def local(
@@ -1092,23 +1116,19 @@
     cache = cache_kv.reshape(R, positions, 2, HDIM)
     scaled, squares, cache_all, flat_gate_up = gather_both(to_send(flipped, attn_gain), cache, w_gate_up, 1)
     projected, squares = matmul_sum(scaled, w_qkv.reshape(w_qkv.shape[0], -1), squares, 1, 2)
-    projected = rescale(projected, squares).reshape(per_device, GROUP + 2, HDIM)
     angles = token_angles(lengths, offsets, first_token, per_device, HDIM)
-    rotated = rotate(projected[:, : GROUP + 1], angles).astype(BF)
-    new_keys, new_values = rotated[:, GROUP], projected[:, GROUP + 1].astype(BF)
-    new_cache = jnp.stack([new_keys, new_values], axis=1)[:, None]
-    per_request = per_device // R
-    span = jnp.concatenate([new_keys, new_values], axis=1).reshape(per_request, R, 2 * HDIM)
-    queries = rotated[:, :GROUP].reshape(per_request, R, GROUP, HDIM).transpose(1, 2, 0, 3)
-    attended, sums = attend(
+    cosine, sine = jnp.cos(angles), jnp.sin(angles)
+    attended, sums, fresh = attend(
         lengths,
-        queries.reshape(R, GROUP * per_request, HDIM),
+        projected,
+        squares,
+        jnp.concatenate([cosine, cosine], axis=1),
+        jnp.concatenate([-sine, sine], axis=1),
         cache_all.reshape(SIDE * SIDE, R, positions, 2 * HDIM),
-        span.transpose(1, 0, 2),
         3,
     )
-    attended = attended.reshape(R, GROUP, per_request, HDIM).transpose(2, 0, 1, 3).reshape(2, -1, GROUP * HDIM)
-    softmax_sums = sums[:, :, 0].reshape(R, GROUP, per_request).transpose(2, 0, 1).reshape(per_device, GROUP)
+    softmax_sums = sums[:, :GROUP]
+    new_cache = fresh.reshape(per_device, 1, 2, HDIM)
     residual, scaled, squares = out_proj(attended, w_out.T, flipped, mlp_gain, 5)
     hidden_out = gate_up(scaled, flat_gate_up, squares, w_down.T, residual, 2, 7).T
     return (hidden_out, softmax_sums, new_cache)

time: 238 us -> 233 us (0.979)
  local copies, waits for them, and re-layouts: 8.03 us -> 4.84 us
    reshape x4 -> x1, local copies, waits for them, and re-layouts: 3.45 us -> 0.63 us  [local(): new_cache = fresh.reshape(per_device, 1, 2, HDIM)]
where the time goes in v6:
time: 233 us
  Pallas kernels  225 us (97%)
  local copies, waits for them, and re-layouts  4.84 us (2%)
  other arithmetic  2.71 us (1%)
    pallas_call x1, Pallas kernels, gate_up(): pl.pallas_call(gate_up_kernel, out_shape=jax.ShapeDtypeStruct(residual.sh...  104 us
    pallas_call x1, Pallas kernels, out_proj(): pl.pallas_call(out_proj_kernel, out_shape=(jax.ShapeDtypeStruct((rows, to...  46.8 us
    pallas_call x1, Pallas kernels, gather_both(): pl.pallas_call(gather_both_kernel, out_shape=(jax.ShapeDtypeStruct((token...  37.2 us
    pallas_call x1, Pallas kernels, matmul_sum(): pl.pallas_call(matmul_sum_kernel, out_shape=(jax.ShapeDtypeStruct((2, row...  23.4 us
    pallas_call x1, Pallas kernels, attend(): pl.pallas_call(attend_kernel, out_shape=(jax.ShapeDtypeStruct((2, per, GR...  13.3 us

profile of v6, /device:TPU:1, one launch (start us, length us, event | category | flops | bytes accessed | tf_op | source)
XLA Modules:
  0.0 233.0 jit_solution(7220671822710853007)
XLA Ops:
  0.6 0.0 copy-start.2
  0.6 0.0 copy-start.4
  0.7 0.7 convert_element_type.18
  1.3 1.0 fusion.1
  2.3 1.3 concatenate.10.x_ref
  3.6 37.2 %gather_both.1 = (bf16[1024,448]{1,0:T(8,128)(2,1)}, f32[4,4,8,128]{3,2,1,0:T(8,128)}, bf16[4,4,2,256,256]{4,3,2,1,0:T(8,128)(2,1)}, bf16[2,448,2560]{2,1,0:T(8,128)(2,1)}) custom-call(bf16[64,1024]{1,0:T(8,128)(2,1)} %concatenate.10.x_ref, bf16[2,256,2,128]{3,2,1,0:T(2,128)(2,1)} %bitcast.22, bf16[448,2,2560]{2,1,0:T(2,128)(2,1)} %w_ref.1), custom_call_target="tpu_custom_call" | custom-call | tf_op jit(solution)/shard_map/gather_both/pallas_call | solution.py:326
  40.8 0.0 copy-start.3
  40.9 23.4 %matmul_sum_2.1 = (f32[2,32,1152]{2,1,0:T(8,128)}, f32[8,128]{1,0:T(8,128)}) custom-call(bf16[4,4,2,32,448]{4,3,2,1,0:T(8,128)(2,1)} %bitcast.16, bf16[448,1152]{1,0:T(8,128)(2,1)} %bitcast.18, f32[4,4,8,128]{3,2,1,0:T(8,128)} %get-tuple-element.16.sq_ref), custom_call_target="tpu_custom_call" | custom-call | tf_op jit(solution)/shard_map/matmul_sum_2/pallas_call | solution.py:636
  64.3 0.0 copy-done.2
  64.3 0.0 copy-done.4
  64.3 0.1 fusion.4
  64.4 0.2 fusion.2
  64.6 0.7 pad_maximum_fusion
  65.3 13.3 %attend.1 = (bf16[2,32,896]{2,1,0:T(8,128)(2,1)}, f32[64,128]{1,0:T(8,128)}, bf16[64,256]{1,0:T(8,128)(2,1)}) custom-call(s32[2]{0:T(128)} %lengths_ref.1, f32[2,32,1152]{2,1,0:T(8,128)} %get-tuple-element.17.sums_in_ref, f32[8,128]{1,0:T(8,128)} %get-tuple-element.18.sq_ref, f32[64,128]{1,0:T(8,128)} %get-tuple-element.41.cos_ref, ...), custom_call_target="tpu_custom_call" | custom-call | tf_op jit(solution)/shard_map/attend/pallas_call | solution.py:1058
  78.7 0.0 copy-done.3
  78.7 0.7 broadcast_in_dim.19.gain_ref
  79.4 0.0 copy-start.1
  79.4 0.0 copy-start
  79.4 46.8 %out_proj.1 = (bf16[56,1024]{1,0:T(8,128)(2,1)}, bf16[1024,448]{1,0:T(8,128)(2,1)}, f32[4,4,8,128]{3,2,1,0:T(8,128)}) custom-call(bf16[2,32,896]{2,1,0:T(8,128)(2,1)} %get-tuple-element.20.own_ref, bf16[448,896]{1,0:T(8,128)(2,1)} %bitcast.19, bf16[56,1024]{1,0:T(8,128)(2,1)} %bitcast.21, f32[56,128]{1,0:T(8,128)} %broadcast_in_dim.19.gain_ref), custom_call_target="tpu_custom_call" | custom-call | tf_op jit(solution)/shard_map/out_proj/pallas_call | solution.py:454
  126.2 103.9 %gate_up.1 = bf16[56,1024]{1,0:T(8,128)(2,1)} custom-call(bf16[4,4,2,32,448]{4,3,2,1,0:T(8,128)(2,1)} %bitcast.17, bf16[2,448,2560]{2,1,0:T(8,128)(2,1)} %get-tuple-element.22.w_ref, f32[4,4,8,128]{3,2,1,0:T(8,128)} %get-tuple-element.23.sq_ref, bf16[448,2560]{1,0:T(8,128)(2,1)} %bitcast.15, bf16[56,1024]{1,0:T(8,128)(2,1)} %get-tuple-element.24.res_ref), custom_call_target="tpu_custom_call" | custom-call | tf_op jit(solution)/shard_map/gate_up/pallas_call | solution.py:918
  230.1 0.0 copy-done.1
  230.1 0.6 reshape.103
  230.7 0.0 copy-done
  230.8 0.7 copy.15
  231.4 1.6 copy.18
  (6 shorter events, 0.1 us)
Async XLA Ops:
  0.6 63.6 %copy-start.2 = (s32[2]{0:T(128)S(1)}, s32[2]{0:T(128)}, u32[]{:S(2)}) copy-start(s32[2]{0:T(128)} %lengths_ref.1) | copy-start | bytes 28
  0.6 63.6 %copy-start.4 = (s32[2]{0:T(128)S(1)}, s32[2]{0:T(128)}, u32[]{:S(2)}) copy-start(s32[2]{0:T(128)} %param.15) | copy-start | bytes 28
  40.8 37.8 %copy-start.3 = (bf16[56]{0:T(256)(128)(2,1)S(1)}, bf16[56]{0:T(256)(128)(2,1)}, u32[]{:S(2)}) copy-start(bf16[56]{0:T(256)(128)(2,1)} %param.17) | copy-start | bytes 340
  79.4 150.7 %copy-start.1 = (bf16[64,256]{1,0:T(8,128)(2,1)S(1)}, bf16[64,256]{1,0:T(8,128)(2,1)}, u32[]{:S(2)}) copy-start(bf16[64,256]{1,0:T(8,128)(2,1)} %get-tuple-element.26) | copy-start | bytes 98308
  79.4 151.4 %copy-start = (f32[64,128]{1,0:T(8,128)S(1)}, f32[64,128]{1,0:T(8,128)}, u32[]{:S(2)}) copy-start(f32[64,128]{1,0:T(8,128)} %get-tuple-element.25) | copy-start | bytes 98308

commit v7 on v6

--- a/solution.py
+++ b/solution.py
@@ -251,6 +251,22 @@
     return [ring_devices("x", 1), ring_devices("x", 3), partner_device()]
 
 
+def to_send(flipped, gain):
+    widened = flipped.astype(F32)
+    squares = jnp.sum(widened * widened, axis=0, keepdims=True)
+    high = squares.astype(BF).astype(F32)
+    rest = squares - high
+    middle = rest.astype(BF).astype(F32)
+    low = rest - middle
+    line = lax.broadcasted_iota(jnp.int32, (8, widened.shape[1]), 0)
+    tail = jnp.where(line == 0, high, jnp.where(line == 1, middle, jnp.where(line == 2, low, 0.0)))
+    return jnp.concatenate([widened * gain, tail], axis=0).astype(BF)
+
+
+def spread(gain):
+    return jnp.broadcast_to(gain.astype(F32)[:, None], (gain.shape[0], 128))
+
+
 def unpack_steps(got_ref, x_ref, sq_ref):
     rows = x_ref.shape[1] // 8
     tokens = x_ref.shape[0]
@@ -295,17 +311,18 @@
 
 
 def gather_both_kernel(
-    x_ref, cache_ref, w_ref, xo_ref, sqo_ref, cacheo_ref, wo_ref,
-    got, own, paired, flat, local_sem, flat_sem, send_n, recv_n, send_w, recv_w,
+    x_ref, gain_ref, cache_ref, w_ref, xo_ref, sqo_ref, cacheo_ref, wo_ref,
+    block, got, own, paired, flat, local_sem, flat_sem, send_n, recv_n, send_w, recv_w,
 ):
     near, far = Copies(send_n, recv_n), Copies(send_w, recv_w)
+    block[...] = to_send(x_ref[...], gain_ref[:, :1])
     for half in range(2):
         own[half, :, :HDIM] = cache_ref[half, :, 0, :]
         own[half, :, HDIM:] = cache_ref[half, :, 1, :]
     greet(narrow_neighbours() + wide_neighbours())
 
     def features():
-        yield from gather_narrow_steps(x_ref, got, local_sem.at[0], near)
+        yield from gather_narrow_steps(block, got, local_sem.at[0], near)
         yield from unpack_steps(got, xo_ref, sqo_ref)
 
     interleave(
@@ -317,25 +334,25 @@
     far.sent()
 
 
-def gather_both(x, cache, w, collective_id):
+def gather_both(x, gain, cache, w, collective_id):
     rows, tokens = x.shape
-    rows -= 8
     dma = pltpu.SemaphoreType.DMA
     flat = (w.shape[1], w.shape[0], w.shape[2])
-    block = cache.shape[:2] + (2 * HDIM,)
+    pair = cache.shape[:2] + (2 * HDIM,)
     return pl.pallas_call(
         gather_both_kernel,
         out_shape=(
             jax.ShapeDtypeStruct((tokens, 8 * rows), BF),
             jax.ShapeDtypeStruct((SIDE, SIDE, 8, 128), F32),
-            jax.ShapeDtypeStruct((SIDE, SIDE) + block, BF),
+            jax.ShapeDtypeStruct((SIDE, SIDE) + pair, BF),
             jax.ShapeDtypeStruct(flat, BF),
         ),
-        in_specs=[VM, VM, ANY],
+        in_specs=[VM, VM, VM, ANY],
         out_specs=(VM, VM, VM, ANY),
         scratch_shapes=[
+            pltpu.VMEM((rows + 8, tokens), BF),
             pltpu.VMEM((8, rows + 8, tokens), BF),
-            pltpu.VMEM(block, BF),
+            pltpu.VMEM(pair, BF),
             pltpu.VMEM(w.shape, BF),
             pltpu.VMEM(flat, BF),
             dma((2,)),
@@ -349,7 +366,7 @@
             collective_id=collective_id, has_side_effects=True, vmem_limit_bytes=VMEM_LIMIT
         ),
         name="gather_both",
-    )(x, cache, w)
+    )(x, spread(gain), cache, w)
 
 
 SUM_COPIES = 10
@@ -421,7 +438,6 @@
 ):
     rows = x_ref.shape[0]
     wide, sums, near = Copies(wide_send, wide_recv), Copies(sum_send, sum_recv), Copies(near_send, near_recv)
-    greet(wide_neighbours() + narrow_neighbours())
     interleave(gather_wide_steps(own_ref, all_ref, local_sem.at[0], wide))
     depth = w_ref.shape[1]
     tokens = x_ref.shape[1] // SIDE
@@ -432,52 +448,12 @@
     sum_narrow_body(terms, acc, mate, total, relay, direct, joined, sums)
     residual = (x_ref[...].astype(F32) + acc[...]).astype(BF)
     res_ref[...] = residual
-    widened = residual.astype(F32)
-    squares = jnp.sum(widened * widened, axis=0, keepdims=True)
-    high = squares.astype(BF).astype(F32)
-    rest = squares - high
-    middle = rest.astype(BF).astype(F32)
-    low = rest - middle
-    line = lax.broadcasted_iota(jnp.int32, (8, widened.shape[1]), 0)
-    tail = jnp.where(line == 0, high, jnp.where(line == 1, middle, jnp.where(line == 2, low, 0.0)))
-    block[...] = jnp.concatenate([widened * gain_ref[:, :1], tail], axis=0).astype(BF)
+    block[...] = to_send(residual, gain_ref[:, :1])
     interleave(gather_narrow_steps(block, got, local_sem.at[1], near))
     interleave(unpack_steps(got, xo_ref, sqo_ref))
     wide.sent()
     sums.sent()
     near.sent()
-
-
-def out_proj(own, w, x, gain, collective_id):
-    rows, tokens = x.shape
-    dma = pltpu.SemaphoreType.DMA
-    return pl.pallas_call(
-        out_proj_kernel,
-        out_shape=(
-            jax.ShapeDtypeStruct((rows, tokens), BF),
-            jax.ShapeDtypeStruct((tokens, 8 * rows), BF),
-            jax.ShapeDtypeStruct((SIDE, SIDE, 8, 128), F32),
-        ),
-        in_specs=[VM] * 4,
-        out_specs=(VM, VM, VM),
-        scratch_shapes=[
-            pltpu.VMEM((8, rows + 8, tokens), BF),
-            pltpu.VMEM((SIDE, SIDE) + own.shape, BF),
-            pltpu.VMEM((rows + 8, tokens), BF),
-        ]
-        + sum_scratch(rows, tokens)
-        + [
-            dma((2,)),
-            dma((WIDE_COPIES,)),
-            dma((WIDE_COPIES,)),
-            dma((NARROW_COPIES,)),
-            dma((NARROW_COPIES,)),
-        ],
-        compiler_params=pltpu.CompilerParams(
-            collective_id=collective_id, has_side_effects=True, vmem_limit_bytes=VMEM_LIMIT
-        ),
-        name="out_proj",
-    )(own, w, x, jnp.broadcast_to(gain.astype(F32)[:, None], (rows, 128)))
 
 
 def matmul_sum_kernel(
@@ -489,7 +465,6 @@
     y, z = wide_place()
     names = (("y", "z"), ("z", "y"))
     spots = ((y, z), (z, y))
-    greet([ring_devices(axis, by) for axis in ("y", "z") for by in (1, 2, 3)])
     squares = Copies(sq_send, sq_recv)
     for by in (1, 2, 3):
         squares.start(by - 1, sq_ref.at[turn(y, by)], sq1.at[by - 1], ring_devices("y", by))
@@ -626,42 +601,6 @@
         return carry
 
     lax.fori_loop(0, pieces, drain, 0)
-
-
-def matmul_sum(x, w, sq, pieces, collective_id):
-    tokens, depth = x.shape
-    cols = w.shape[1]
-    width = cols // pieces
-    rows = tokens // (2 * SIDE * SIDE)
-    out, sq_out = pl.pallas_call(
-        matmul_sum_kernel,
-        out_shape=(
-            jax.ShapeDtypeStruct((2, rows, cols), F32),
-            jax.ShapeDtypeStruct((8, 128), F32),
-        ),
-        in_specs=[VM, VM, VM],
-        out_specs=(VM, VM),
-        scratch_shapes=[
-            pltpu.VMEM((pieces, 2, SIDE, SIDE, rows, width), BF),
-            pltpu.VMEM((pieces, 2, SIDE, rows, width), BF),
-            pltpu.VMEM((pieces, 2, 3, 2, 2, rows, width), BF),
-            pltpu.VMEM((pieces, 2, 3, 2, rows // 2, width), BF),
-            pltpu.VMEM((3, SIDE, 8, 128), F32),
-            pltpu.VMEM((SIDE, 8, 128), F32),
-            pltpu.VMEM((3, 8, 128), F32),
-            pltpu.SemaphoreType.DMA((pieces, 2, 3, 2)),
-            pltpu.SemaphoreType.DMA((pieces, 2, 3, 2)),
-            pltpu.SemaphoreType.DMA((pieces, 2, 3, 2)),
-            pltpu.SemaphoreType.DMA((pieces, 2, 3, 2)),
-            pltpu.SemaphoreType.DMA((6,)),
-            pltpu.SemaphoreType.DMA((6,)),
-        ],
-        compiler_params=pltpu.CompilerParams(
-            collective_id=collective_id, has_side_effects=True, vmem_limit_bytes=VMEM_LIMIT
-        ),
-        name=f"matmul_sum_{collective_id}",
-    )(x.reshape(SIDE, SIDE, 2, rows, depth), w, sq)
-    return out, sq_out
 
 
 def gate_up_kernel(
@@ -985,7 +924,6 @@
     block = cache_ref.shape[2] * CHUNK
     spot = lax.axis_index("wide")
     copies = Copies(send_sem, recv_sem)
-    greet(wide_lines())
     gather = gather_direct_steps(own_ref, span_ref, local_sem, copies)
     next(gather)
     for index in range(GROUP):
@@ -1051,35 +989,99 @@
     copies.sent()
 
 
-def attend(lengths, sums, sq, cosine, sine, cache, collective_id):
-    per = sums.shape[1]
+def matmul_scratch(pieces, rows, width):
+    dma = pltpu.SemaphoreType.DMA
+    return [
+        pltpu.VMEM((pieces, 2, SIDE, SIDE, rows, width), BF),
+        pltpu.VMEM((pieces, 2, SIDE, rows, width), BF),
+        pltpu.VMEM((pieces, 2, 3, 2, 2, rows, width), BF),
+        pltpu.VMEM((pieces, 2, 3, 2, rows // 2, width), BF),
+        pltpu.VMEM((3, SIDE, 8, 128), F32),
+        pltpu.VMEM((SIDE, 8, 128), F32),
+        pltpu.VMEM((3, 8, 128), F32),
+        dma((pieces, 2, 3, 2)),
+        dma((pieces, 2, 3, 2)),
+        dma((pieces, 2, 3, 2)),
+        dma((pieces, 2, 3, 2)),
+        dma((6,)),
+        dma((6,)),
+    ]
+
+
+def attend_scratch(per):
     tokens = R * per
     dma = pltpu.SemaphoreType.DMA
+    return [
+        pltpu.VMEM((GROUP + 2, tokens, HDIM), F32),
+        pltpu.VMEM((R, GROUP * per, HDIM), BF),
+        pltpu.VMEM((R, per, 2 * HDIM), BF),
+        pltpu.VMEM((GROUP, tokens, HDIM), F32),
+        pltpu.VMEM((tokens, 128), F32),
+        pltpu.VMEM((SIDE, SIDE, R, per, 2 * HDIM), BF),
+        dma,
+        dma((DIRECT_COPIES,)),
+        dma((DIRECT_COPIES,)),
+    ]
+
+
+def proj_scratch(per, rows, tokens):
+    dma = pltpu.SemaphoreType.DMA
+    return [
+        pltpu.VMEM((8, rows + 8, tokens), BF),
+        pltpu.VMEM((SIDE, SIDE, 2, per, GROUP * HDIM), BF),
+        pltpu.VMEM((rows + 8, tokens), BF),
+        *sum_scratch(rows, tokens),
+        dma((2,)),
+        dma((WIDE_COPIES,)),
+        dma((WIDE_COPIES,)),
+        dma((NARROW_COPIES,)),
+        dma((NARROW_COPIES,)),
+    ]
+
+
+def attention_kernel(
+    count_matmul, count_attend, lengths_ref, x_ref, wq_ref, sq_ref, cos_ref, sin_ref, cache_ref, wo_ref, flip_ref, gain_ref,
+    sums_ref, fresh_ref, res_ref, xo_ref, sqo_ref, proj, total_sq, attended, *scratch,
+):
+    greet(wide_lines() + narrow_neighbours())
+    for_attend = count_matmul + count_attend
+    matmul_sum_kernel(x_ref, wq_ref, sq_ref, proj, total_sq, *scratch[:count_matmul])
+    attend_kernel(
+        lengths_ref, proj, total_sq, cos_ref, sin_ref, cache_ref, attended, sums_ref, fresh_ref,
+        *scratch[count_matmul:for_attend],
+    )
+    out_proj_kernel(attended, wo_ref, flip_ref, gain_ref, res_ref, xo_ref, sqo_ref, *scratch[for_attend:])
+
+
+def attention(lengths, x, wq, sq, cosine, sine, cache, wo, flipped, gain, collective_id):
+    rows, tokens = flipped.shape
+    cols = wq.shape[1]
+    per = tokens // (2 * SIDE * SIDE)
+    for_matmul, for_attend = matmul_scratch(1, per, cols), attend_scratch(per)
     return pl.pallas_call(
-        attend_kernel,
+        functools.partial(attention_kernel, len(for_matmul), len(for_attend)),
         out_shape=(
-            jax.ShapeDtypeStruct((2, per, GROUP * HDIM), BF),
-            jax.ShapeDtypeStruct((tokens, 128), F32),
-            jax.ShapeDtypeStruct((tokens, 2 * HDIM), BF),
+            jax.ShapeDtypeStruct((2 * per, 128), F32),
+            jax.ShapeDtypeStruct((2 * per, 2 * HDIM), BF),
+            jax.ShapeDtypeStruct((rows, tokens), BF),
+            jax.ShapeDtypeStruct((tokens, 8 * rows), BF),
+            jax.ShapeDtypeStruct((SIDE, SIDE, 8, 128), F32),
         ),
-        in_specs=[SM] + [VM] * 5,
-        out_specs=(VM, VM, VM),
+        in_specs=[SM] + [VM] * 9,
+        out_specs=(VM,) * 5,
         scratch_shapes=[
-            pltpu.VMEM((GROUP + 2, tokens, HDIM), F32),
-            pltpu.VMEM((R, GROUP * per, HDIM), BF),
-            pltpu.VMEM((R, per, 2 * HDIM), BF),
-            pltpu.VMEM((GROUP, tokens, HDIM), F32),
-            pltpu.VMEM((tokens, 128), F32),
-            pltpu.VMEM((SIDE, SIDE, R, per, 2 * HDIM), BF),
-            dma,
-            dma((DIRECT_COPIES,)),
-            dma((DIRECT_COPIES,)),
+            pltpu.VMEM((2, per, cols), F32),
+            pltpu.VMEM((8, 128), F32),
+            pltpu.VMEM((2, per, GROUP * HDIM), BF),
+            *for_matmul,
+            *for_attend,
+            *proj_scratch(per, rows, tokens),
         ],
         compiler_params=pltpu.CompilerParams(
             collective_id=collective_id, has_side_effects=True, vmem_limit_bytes=VMEM_LIMIT
         ),
-        name="attend",
-    )(lengths, sums, sq, cosine, sine, cache)
+        name="attention",
+    )(lengths, x.reshape(SIDE, SIDE, 2, per, x.shape[1]), wq, sq, cosine, sine, cache, wo, flipped, spread(gain))
 
 
 def token_angles(lengths, offsets, first_token, row_count, dim_size):
@@ -1093,18 +1095,6 @@
     return position[:, None] * inverse[None, :]
 
 
-def to_send(flipped, gain):
-    widened = flipped.astype(F32)
-    squares = jnp.sum(widened * widened, axis=0, keepdims=True)
-    high = lax.reduce_precision(squares, 8, 7)
-    rest = squares - high
-    middle = lax.reduce_precision(rest, 8, 7)
-    low = rest - middle
-    scaled = widened * gain.astype(F32)[:, None]
-    pad = jnp.zeros((5, flipped.shape[1]), F32)
-    return jnp.concatenate([scaled, high, middle, low, pad], axis=0).astype(BF)
-
-
 def local(
     hidden_in, attn_gain, w_qkv, cache_kv, lengths, offsets, w_out, mlp_gain, w_gate_up, w_down
 ):
@@ -1114,22 +1104,24 @@
     flipped = hidden_in.T
     positions = cache_kv.shape[1]
     cache = cache_kv.reshape(R, positions, 2, HDIM)
-    scaled, squares, cache_all, flat_gate_up = gather_both(to_send(flipped, attn_gain), cache, w_gate_up, 1)
-    projected, squares = matmul_sum(scaled, w_qkv.reshape(w_qkv.shape[0], -1), squares, 1, 2)
+    scaled, squares, cache_all, flat_gate_up = gather_both(flipped, attn_gain, cache, w_gate_up, 1)
     angles = token_angles(lengths, offsets, first_token, per_device, HDIM)
     cosine, sine = jnp.cos(angles), jnp.sin(angles)
-    attended, sums, fresh = attend(
+    sums, fresh, residual, scaled, squares = attention(
         lengths,
-        projected,
+        scaled,
+        w_qkv.reshape(w_qkv.shape[0], -1),
         squares,
         jnp.concatenate([cosine, cosine], axis=1),
         jnp.concatenate([-sine, sine], axis=1),
         cache_all.reshape(SIDE * SIDE, R, positions, 2 * HDIM),
-        3,
+        w_out.T,
+        flipped,
+        mlp_gain,
+        2,
     )
     softmax_sums = sums[:, :GROUP]
     new_cache = fresh.reshape(per_device, 1, 2, HDIM)
-    residual, scaled, squares = out_proj(attended, w_out.T, flipped, mlp_gain, 5)
     hidden_out = gate_up(scaled, flat_gate_up, squares, w_down.T, residual, 2, 7).T
     return (hidden_out, softmax_sums, new_cache)
 

time: 233 us -> 226 us (0.970)
  Pallas kernels: 225 us -> 218 us
    pallas_call x3 -> x1, Pallas kernels: 83.5 us -> 76.4 us  [attention(): pl.pallas_call(functools.partial(attention_kernel, len(for_matmul), len(f...]
where the time goes in v7:
time: 226 us
  Pallas kernels  218 us (96%)
  local copies, waits for them, and re-layouts  5.54 us (2%)
    pallas_call x1, Pallas kernels, gate_up(): pl.pallas_call(gate_up_kernel, out_shape=jax.ShapeDtypeStruct(residual.sh...  104 us
    pallas_call x1, Pallas kernels, attention(): pl.pallas_call(functools.partial(attention_kernel, len(for_matmul), len(f...  76.4 us
    pallas_call x1, Pallas kernels, gather_both(): pl.pallas_call(gather_both_kernel, out_shape=(jax.ShapeDtypeStruct((token...  37.8 us

profile of v7, /device:TPU:1, one launch (start us, length us, event | category | flops | bytes accessed | tf_op | source)
XLA Modules:
  0.0 226.2 jit_solution(3459683353737654019)
XLA Ops:
  0.6 0.7 add.41
  1.3 0.1 fusion.1
  1.4 1.3 broadcast_in_dim.16.gain_ref
  2.8 1.3 broadcast_in_dim.19.gain_ref
  4.1 0.2 fusion
  4.3 0.7 pad_maximum_fusion
  5.0 37.8 %gather_both.1 = (bf16[1024,448]{1,0:T(8,128)(2,1)}, f32[4,4,8,128]{3,2,1,0:T(8,128)}, bf16[4,4,2,256,256]{4,3,2,1,0:T(8,128)(2,1)}, bf16[2,448,2560]{2,1,0:T(8,128)(2,1)}) custom-call(bf16[56,1024]{1,0:T(8,128)(2,1)} %bitcast.18, f32[56,128]{1,0:T(8,128)} %broadcast_in_dim.16.gain_ref, bf16[2,256,2,128]{3,2,1,0:T(2,128)(2,1)} %bitcast.20, ...), custom_call_target="tpu_custom_call" | custom-call | tf_op jit(solution)/shard_map/gather_both/pallas_call | solution.py:342
  42.9 76.4 %attention.1 = (f32[64,128]{1,0:T(8,128)}, bf16[64,256]{1,0:T(8,128)(2,1)}, bf16[56,1024]{1,0:T(8,128)(2,1)}, bf16[1024,448]{1,0:T(8,128)(2,1)}, f32[4,4,8,128]{3,2,1,0:T(8,128)}) custom-call(s32[2]{0:T(128)} %lengths_ref.1, bf16[4,4,2,32,448]{4,3,2,1,0:T(8,128)(2,1)} %bitcast.13, bf16[448,1152]{1,0:T(8,128)(2,1)} %bitcast.15, ...), custom_call_target="tpu_custom_call" | custom-call | tf_op jit(solution)/shard_map/attention/pallas_call | solution.py:1061
  119.3 0.0 copy-start
  119.3 0.0 copy-start.1
  119.3 104.0 %gate_up.1 = bf16[56,1024]{1,0:T(8,128)(2,1)} custom-call(bf16[4,4,2,32,448]{4,3,2,1,0:T(8,128)(2,1)} %bitcast.14, bf16[2,448,2560]{2,1,0:T(8,128)(2,1)} %get-tuple-element.16.w_ref, f32[4,4,8,128]{3,2,1,0:T(8,128)} %get-tuple-element.17.sq_ref, bf16[448,2560]{1,0:T(8,128)(2,1)} %bitcast.12, bf16[56,1024]{1,0:T(8,128)(2,1)} %get-tuple-element.18.res_ref), custom_call_target="tpu_custom_call" | custom-call | tf_op jit(solution)/shard_map/gate_up/pallas_call | solution.py:857
  223.3 0.0 copy-done
  223.3 0.7 copy.15
  224.0 0.0 copy-done.1
  224.0 0.6 reshape.75
  224.6 1.6 copy.18
  (3 shorter events, 0.0 us)
Async XLA Ops:
  119.3 104.0 %copy-start = (f32[64,128]{1,0:T(8,128)S(1)}, f32[64,128]{1,0:T(8,128)}, u32[]{:S(2)}) copy-start(f32[64,128]{1,0:T(8,128)} %get-tuple-element.19) | copy-start | bytes 98308
  119.3 104.7 %copy-start.1 = (bf16[64,256]{1,0:T(8,128)(2,1)S(1)}, bf16[64,256]{1,0:T(8,128)(2,1)}, u32[]{:S(2)}) copy-start(bf16[64,256]{1,0:T(8,128)(2,1)} %get-tuple-element.20) | copy-start | bytes 98308
